TPU v7x, 128 devices: a whole 4x4x4 slice. The times are simulated.
128 devices in a mesh: row: 16 (over x, z), col: 8 (over y, core).
Axes of the slice: x: 4, y: 4, z: 4, core: 2. Of those that a mesh axis runs over, the one named last changes fastest.
Arguments:
- innovations: float32 [64, 65536], P(None, ('row', 'col')), may hold values from -300 to 300
- obs_factors: float32 [64, 65536], P(None, ('row', 'col')), may hold values from -6 to 6
- component: int32 [65536], P(('row', 'col')), may hold values 0 or 1
- obs_error: float32 [65536], P(('row', 'col')), may hold values from 0.5 to 2
- coupling: float32 [2, 2], replicated, may hold values from 0.5 to 2
- tile_slots: int32 [16, 8, 8, 3], P('row', 'col'), may hold values from 0 to 15, as said below
Outputs:
- increment: float32 [64, 65536], P(None, ('row', 'col'))
- residual: float32 [64, 65536], P(None, ('row', 'col'))
Inputs may be any that keep to these rules, and one draw needn't show every extreme that they name: `tile_slots`: each device's slots name distinct (local block row, local block column) pairs; on some device all 8 slots are live; the live flag is 0 or 1; local block rows are below 8 and local block columns below 16.
All inputs are finite; a program needn't handle non-finite values. No bound on the sum of `component` on one device may be relied on, other than what follows from the above.
Results may differ from a plain program's by a relative error of at most 0.0003.
Values sent between devices are 32-bit elements; how exact they have to be, the bound alone decides.
No kernel may reach another device: no remote copies, remote signals or barrier semaphores. Data moves between devices by JAX's collectives and lax.ppermute only.
A program may use at most 64 MiB of HBM per device.

v0:
```python
import jax
import jax.numpy as jnp
from jax import lax
from jax.sharding import Mesh
from jax.sharding import PartitionSpec as P

TILE = 512
ITERS = 3
ROW_COL = ("row_0", "row_1", "col_0", "col_1")
COL = ("col_0", "col_1")
ROW = ("row_0", "row_1")


length_sq = 12.0


def over_axes(shard, axes):
    for axis in axes:
        shard = lax.psum(shard, axis)
    return shard


def turned_gather(arrays, axis, dims):
    turned = [jnp.moveaxis(a, dim, 0) for a, dim in zip(arrays, dims)]
    widths = [t[0].size for t in turned]
    both = jnp.concatenate([t.reshape(-1, w) for t, w in zip(turned, widths)], axis=1)
    filled = lax.all_gather(both, axis, axis=0, tiled=True)
    blocks = jnp.split(filled, [sum(widths[:k]) for k in range(1, len(widths))], axis=1)
    return tuple(
        (
            jnp.moveaxis(b.reshape(-1, *t.shape[1:]), 0, dim)
            for b, t, dim in zip(blocks, turned, dims)
        )
    )


def cut_along(shard, dim, devices):
    before, after = (shard.shape[:dim], shard.shape[dim + 1 :])
    return jnp.moveaxis(shard.reshape(*before, devices, -1, *after), dim, 0)


def sent_and_summed(shard, axis, dim):
    blocks = cut_along(shard, dim, lax.axis_size(axis))
    arrived = lax.all_to_all(blocks, axis, split_axis=0, concat_axis=0, tiled=True)
    return arrived.sum(axis=0)


def joined_along(blocks, dim):
    blocks = jnp.moveaxis(blocks, 0, dim)
    lengths = blocks.shape
    return blocks.reshape(*lengths[:dim], lengths[dim] * lengths[dim + 1], *lengths[dim + 2 :])


def from_everyone(shard, axis):
    copies = jnp.broadcast_to(shard, (lax.axis_size(axis), *shard.shape))
    return lax.all_to_all(copies, axis, split_axis=0, concat_axis=0, tiled=True)


def collect(shard, axis, dim):
    return joined_along(from_everyone(shard, axis), dim)


def piece_ends(length, count):
    unit = 8 if length >= 8 * count else 1
    return [length // unit * k // count * unit for k in range(1, count)]


def stacked_from(shard, axes, turns):
    blocks = shard
    for k in turns:
        blocks = lax.all_gather(blocks, axes[k])
    done = turns[::-1]
    back = [done.index(k) for k in range(len(axes))]
    blocks = blocks.transpose(*back, *range(len(axes), blocks.ndim))
    return blocks.reshape(-1, *shard.shape)


def gather_at_once(shard, axes, dim):
    widest = max(range(max(1, shard.ndim - 1)), key=lambda d: shard.shape[d])
    count, gathered = (len(axes), [])
    for first, share in enumerate(
        jnp.split(shard, piece_ends(shard.shape[widest], count), axis=widest)
    ):
        if share.size:
            turns = [(first - k) % count for k in range(count)]
            gathered.append(stacked_from(share, axes, turns))
    return joined_along(jnp.concatenate(gathered, axis=widest + 1), dim)


def tile_matrix(left_factors, right_factors, left_labels, right_labels, coupling):
    left_norms = jnp.sum(left_factors * left_factors, axis=0)
    right_norms = jnp.sum(right_factors * right_factors, axis=0)
    products = lax.dot_general(
        left_factors,
        right_factors,
        (((0,), (0,)), ((), ())),
        precision=lax.Precision.HIGHEST,
        preferred_element_type=jnp.float32,
    )
    pair_coupling = (1.0 - left_labels)[:, None] * (
        (1.0 - right_labels)[None, :] * coupling[0, 0] + right_labels[None, :] * coupling[0, 1]
    ) + left_labels[:, None] * (
        (1.0 - right_labels)[None, :] * coupling[1, 0] + right_labels[None, :] * coupling[1, 1]
    )
    return pair_coupling * jnp.exp(
        -(left_norms[:, None] + right_norms[None, :] - 2.0 * products) / length_sq
    )


def take_segment(array, block):
    start = block * TILE
    return lax.dynamic_slice_in_dim(array, start, TILE, array.ndim - 1)


def add_segment(vector, block, values):
    start = block * TILE
    last_axis = vector.ndim - 1
    before = lax.dynamic_slice_in_dim(vector, start, TILE, last_axis)
    return lax.dynamic_update_slice_in_dim(vector, before + values, start, last_axis)


def two_products(residual, image):
    return (
        over_axes(jnp.sum(residual * residual, axis=1), ROW_COL),
        over_axes(jnp.sum(residual * image, axis=1), ROW_COL),
    )


def shards(innovations, obs_factors, component, obs_error, coupling, tile_slots):
    labels_float = component.astype(jnp.float32)
    row_factors, row_labels = turned_gather((obs_factors, labels_float), COL, (1, 0))
    column_factors, column_labels = turned_gather((obs_factors, labels_float), ROW, (1, 0))
    slots = tile_slots[0, 0]
    count = slots.shape[0]
    flags = slots[:, 2].astype(jnp.float32)
    rhs_count = innovations.shape[0]

    def make_tile(number):
        row_block = slots[number, 0]
        column_block = slots[number, 1]
        block_matrix = tile_matrix(
            take_segment(row_factors, row_block),
            take_segment(column_factors, column_block),
            take_segment(row_labels, row_block),
            take_segment(column_labels, column_block),
            coupling,
        )
        return block_matrix * flags[number]

    def visit(totals, work):
        result = work(totals)
        return result

    stored = jnp.zeros((count, TILE, TILE), jnp.float32)

    def weigh(number, carry):

        def work(carry):
            row_totals, column_totals, stored = carry
            block_matrix = make_tile(number)
            row_totals = add_segment(row_totals, slots[number, 0], jnp.sum(block_matrix, axis=1))
            column_totals = add_segment(
                column_totals, slots[number, 1], jnp.sum(block_matrix, axis=0)
            )
            stored = lax.dynamic_update_index_in_dim(stored, block_matrix, number, 0)
            return (row_totals, column_totals, stored)

        return visit(carry, work)

    start_carry = (
        jnp.zeros((row_factors.shape[1],), jnp.float32),
        jnp.zeros((column_factors.shape[1],), jnp.float32),
        stored,
    )
    row_totals, column_totals, stored = lax.fori_loop(0, count, weigh, start_carry)
    diagonal = (
        obs_error + sent_and_summed(row_totals, COL, 0) + sent_and_summed(column_totals, ROW, 0)
    )

    def fetch(number):
        block_matrix = lax.dynamic_index_in_dim(stored, number, 0, keepdims=False)
        return block_matrix

    def operate(vector):
        column_values = collect(vector, ROW, 1)
        row_values = gather_at_once(vector, COL, 1)

        def sweep(number, carry):

            def work(carry):
                row_image, column_image = carry
                block_matrix = fetch(number)
                row_block = slots[number, 0]
                column_block = slots[number, 1]
                right_part = lax.dot_general(
                    take_segment(column_values, column_block),
                    block_matrix,
                    (((1,), (1,)), ((), ())),
                    precision=lax.Precision.HIGHEST,
                    preferred_element_type=jnp.float32,
                )
                left_part = jnp.dot(
                    take_segment(row_values, row_block),
                    block_matrix,
                    precision=lax.Precision.HIGHEST,
                    preferred_element_type=jnp.float32,
                )
                return (
                    add_segment(row_image, row_block, right_part),
                    add_segment(column_image, column_block, left_part),
                )

            return visit(carry, work)

        start_image = (
            jnp.zeros((rhs_count, row_values.shape[1]), jnp.float32),
            jnp.zeros((rhs_count, column_values.shape[1]), jnp.float32),
        )
        row_image, column_image = lax.fori_loop(0, count, sweep, start_image)
        return (
            diagonal[None, :] * vector
            + sent_and_summed(row_image, COL, 1)
            + sent_and_summed(column_image, ROW, 1)
        )

    increment = jnp.zeros_like(innovations)
    residual = innovations
    image = operate(residual)
    norm_now, product = two_products(residual, image)
    alpha = norm_now / product
    direction = residual
    along = image
    for repeat in range(ITERS):
        increment = increment + alpha[:, None] * direction
        residual = residual - alpha[:, None] * along
        if repeat + 1 < ITERS:
            image = operate(residual)
            norm_next, product = two_products(residual, image)
            ratio = norm_next / norm_now
            alpha = norm_next / (product - ratio * norm_next / alpha)
            direction = residual + ratio[:, None] * direction
            along = image + ratio[:, None] * along
            norm_now = norm_next
    return (increment, residual)


def solution(mesh):
    finer = Mesh(mesh.devices.reshape(4, 4, 4, 2), ("row_0", "row_1", "col_0", "col_1"))
    in_specs = (
        P(None, ROW_COL),
        P(None, ROW_COL),
        P(ROW_COL),
        P(ROW_COL),
        P(),
        P(ROW, COL, None, None),
    )
    out_specs = (P(None, ROW_COL), P(None, ROW_COL))
    return jax.shard_map(
        shards, mesh=finer, in_specs=in_specs, out_specs=out_specs, check_vma=False
    )
```

profile of v0, /device:TPU:1, one launch (start us, length us, event | category | flops | bytes accessed | tf_op | source)
XLA Modules:
  0.0 719.6 jit_solution(14333697399564382852)
XLA Ops:
  12.7 8.6 %all-to-all-start.2 = ((f32[16,64,512]{2,1,0:T(8,128)}), f32[16,64,512]{2,1,0:T(8,128)S(1)}, u32[]{:S(2)}, u32[]{:S(2)}) async-start(f32[16,64,512]{2,1,0:T(8,128)} %broadcast_in_dim.62), calls=%async_computation.2 | async-start | bytes 4194304 | tf_op jit(solution)/shard_map/all_to_all | solution.py:56
  21.4 11.5 %all-gather = f32[128,512]{1,0:T(8,128)S(1)} all-gather(f32[32,512]{1,0:T(8,128)S(1)} %get-tuple-element.703), channel_id=2, replica_groups=mesh['row_0'=4,'row_1'=4,'col_0'=4,'col_1'=2] {'col_0'}, dimensions={0}, use_global_device_ids=true | all-gather | bytes 327680 | tf_op jit(solution)/shard_map/all_gather | solution.py:71
  32.9 4.8 all-gather.1
  40.5 11.0 %all-gather.3 = f32[8,32,512]{2,1,0:T(8,128)} all-gather(f32[2,32,512]{2,1,0:T(8,128)S(1)} %bitcast.180), channel_id=5, replica_groups=mesh['row_0'=4,'row_1'=4,'col_0'=4,'col_1'=2] {'col_0'}, dimensions={0}, use_global_device_ids=true | all-gather | bytes 655360 | tf_op jit(solution)/shard_map/all_gather | solution.py:71
  52.9 31.5 %all-gather.17.cloned.1.call-done = f32[8192,65]{0,1:T(8,128)} async-done(((f32[512,65]{0,1:T(8,128)}), f32[8192,65]{0,1:T(8,128)}) %all-gather.17.cloned.1.call-update) | async-done | bytes 2129936 | tf_op jit(solution)/shard_map/all_gather | solution.py:27
  84.3 3.1 slice_bitcast_fusion
  88.7 112.0 %while.62 = (s32[]{:T(128)}, f32[4096]{0:T(1024)}, f32[8192]{0:T(1024)}, f32[8,512,512]{2,1,0:T(8,128)}, s32[8,3]{0,1:T(4,128)S(1)}, /*index=5*/f32[4096]{0:T(10...) while((s32[]{:T(128)}, f32[4096]{0:T(1024)}, ...), condition=%wide.region_10.11_spmd, body=%wide.region_5.10_spmd.sunk | while | flops 204606480 | bytes 3716449 | solution.py:175
  109.5 3.1 fusion.66
  123.5 3.1 fusion.66
  151.5 3.1 fusion.66
  193.5 3.1 fusion.66
  200.6 5.9 all-to-all-start
  211.2 4.6 all-to-all-start.1
  216.1 51.8 %while.63 = (s32[]{:T(128)}, f32[64,4096]{1,0:T(8,128)S(1)}, f32[64,8192]{1,0:T(8,128)S(1)}, s32[8,3]{0,1:T(4,128)S(1)}, f32[64,8192]{1,0:T(8,128)}, /*index=5*/...) while((s32[]{:T(128)}, f32[64,4096]{1,0:T(8,128)S(1)}, ...), condition=%wide.region_14.15_spmd, body=%wide.region_13.14_spmd.sunk | while | flops 402718720 | bytes 2884853 | solution.py:219
  270.2 4.5 all-to-all-start.3
  278.4 11.3 %all-to-all-done.3 = f32[8,64,512]{2,1,0:T(8,128)S(1)} async-done(((f32[8,64,512]{2,1,0:T(8,128)}), f32[8,64,512]{2,1,0:T(8,128)S(1)}, u32[]{:S(2)}, u32[]{:S(2)}) %all-to-all-start.3) | async-done | bytes 1048608 | tf_op jit(solution)/shard_map/all_to_all | solution.py:44
  289.7 6.9 all-to-all-start.4
  296.9 26.3 %all-to-all-done.4 = f32[16,64,512]{2,1,0:T(8,128)S(1)} async-done(((f32[16,64,512]{2,1,0:T(8,128)}), f32[16,64,512]{2,1,0:T(8,128)S(1)}, u32[]{:S(2)}, u32[]{:S(2)}) %all-to-all-start.4) | async-done | bytes 2097184 | tf_op jit(solution)/shard_map/all_to_all | solution.py:44
  323.4 7.6 %all-reduce.8 = (f32[64]{0:T(128)S(1)}, f32[64]{0:T(128)S(1)}) all-reduce(f32[64]{0:T(128)S(1)} %get-tuple-element.579, f32[64]{0:T(128)S(1)} %get-tuple-element.578), channel_id=1, replica_groups=mesh['row_0'=4,'row_1'=4,'col_0'=4,'col_1'=2] {'row_0'}, use_global_device_ids=true, to_apply=%region_1.2 | all-reduce | flops 128 | bytes 1024 | tf_op jit(solution)/shard_map/psum | solution.py:19
  331.0 7.4 %all-reduce.5 = (f32[64]{0:T(128)S(1)}, f32[64]{0:T(128)S(1)}) all-reduce(f32[64]{0:T(128)S(1)} %get-tuple-element.660, f32[64]{0:T(128)S(1)} %get-tuple-element.661), channel_id=1, replica_groups=mesh['row_0'=4,'row_1'=4,'col_0'=4,'col_1'=2] {'row_1'}, use_global_device_ids=true, to_apply=%region_2.3 | all-reduce | flops 128 | bytes 1024 | tf_op jit(solution)/shard_map/psum | solution.py:19
  338.4 6.9 all-reduce.2
  345.2 10.5 %all-reduce.11 = (f32[64]{0:T(128)S(1)}, f32[64]{0:T(128)S(1)}) all-reduce(f32[64]{0:T(128)S(1)} %get-tuple-element.648, f32[64]{0:T(128)S(1)} %get-tuple-element.649), channel_id=1, replica_groups=mesh['row_0'=4,'row_1'=4,'col_0'=4,'col_1'=2] {'col_1'}, use_global_device_ids=true, to_apply=%region_4.5 | all-reduce | flops 128 | bytes 1024 | tf_op jit(solution)/shard_map/psum | solution.py:19
  357.5 3.7 all-to-all-start.5
  361.3 10.3 %all-gather.4 = f32[128,512]{1,0:T(8,128)S(1)} all-gather(f32[32,512]{1,0:T(8,128)S(1)} %get-tuple-element.701), channel_id=6, replica_groups=mesh['row_0'=4,'row_1'=4,'col_0'=4,'col_1'=2] {'col_0'}, dimensions={0}, use_global_device_ids=true | all-gather | bytes 327680 | tf_op jit(solution)/shard_map/all_gather | solution.py:71
  371.5 4.2 all-gather.5
  377.7 10.9 %all-gather.7 = f32[8,32,512]{2,1,0:T(8,128)S(1)} all-gather(f32[2,32,512]{2,1,0:T(8,128)S(1)} %bitcast.181), channel_id=9, replica_groups=mesh['row_0'=4,'row_1'=4,'col_0'=4,'col_1'=2] {'col_0'}, dimensions={0}, use_global_device_ids=true | all-gather | bytes 655360 | tf_op jit(solution)/shard_map/all_gather | solution.py:71
  392.2 51.6 %while.64 = (s32[]{:T(128)}, f32[64,4096]{1,0:T(8,128)S(1)}, f32[64,8192]{1,0:T(8,128)S(1)}, s32[8,3]{0,1:T(4,128)S(1)}, f32[64,8192]{1,0:T(8,128)}, /*index=5*/...) while((s32[]{:T(128)}, f32[64,4096]{1,0:T(8,128)S(1)}, ...), condition=%wide.region_28.29_spmd, body=%wide.region_27.28_spmd.sunk | while | flops 402718720 | bytes 2884853 | solution.py:219
  446.1 5.4 all-to-all-start.6
  455.3 11.3 %all-to-all-done.6 = f32[8,64,512]{2,1,0:T(8,128)S(1)} async-done(((f32[8,64,512]{2,1,0:T(8,128)}), f32[8,64,512]{2,1,0:T(8,128)S(1)}, u32[]{:S(2)}, u32[]{:S(2)}) %all-to-all-start.6) | async-done | bytes 1048608 | tf_op jit(solution)/shard_map/all_to_all | solution.py:44
  466.6 7.4 %all-to-all-start.7 = ((f32[16,64,512]{2,1,0:T(8,128)}), f32[16,64,512]{2,1,0:T(8,128)S(1)}, u32[]{:S(2)}, u32[]{:S(2)}) async-start(f32[16,64,512]{2,1,0:T(8,128)} %copy.58), calls=%async_computation.7 | async-start | bytes 4194304 | tf_op jit(solution)/shard_map/all_to_all | solution.py:44
  474.2 26.3 %all-to-all-done.7 = f32[16,64,512]{2,1,0:T(8,128)S(1)} async-done(((f32[16,64,512]{2,1,0:T(8,128)}), f32[16,64,512]{2,1,0:T(8,128)S(1)}, u32[]{:S(2)}, u32[]{:S(2)}) %all-to-all-start.7) | async-done | bytes 2097184 | tf_op jit(solution)/shard_map/all_to_all | solution.py:44
  500.8 7.6 %all-reduce.7 = (f32[64]{0:T(128)S(1)}, f32[64]{0:T(128)S(1)}) all-reduce(f32[64]{0:T(128)S(1)} %get-tuple-element.577, f32[64]{0:T(128)S(1)} %get-tuple-element.576), channel_id=1, replica_groups=mesh['row_0'=4,'row_1'=4,'col_0'=4,'col_1'=2] {'row_0'}, use_global_device_ids=true, to_apply=%region_23.24 | all-reduce | flops 128 | bytes 1024 | tf_op jit(solution)/shard_map/psum | solution.py:19
  508.4 7.4 %all-reduce.4 = (f32[64]{0:T(128)S(1)}, f32[64]{0:T(128)S(1)}) all-reduce(f32[64]{0:T(128)S(1)} %get-tuple-element.658, f32[64]{0:T(128)S(1)} %get-tuple-element.659), channel_id=1, replica_groups=mesh['row_0'=4,'row_1'=4,'col_0'=4,'col_1'=2] {'row_1'}, use_global_device_ids=true, to_apply=%region_24.25 | all-reduce | flops 128 | bytes 1024 | tf_op jit(solution)/shard_map/psum | solution.py:19
  515.8 6.9 all-reduce.1
  522.6 10.5 %all-reduce.10 = (f32[64]{0:T(128)S(1)}, f32[64]{0:T(128)S(1)}) all-reduce(f32[64]{0:T(128)S(1)} %get-tuple-element.646, f32[64]{0:T(128)S(1)} %get-tuple-element.647), channel_id=1, replica_groups=mesh['row_0'=4,'row_1'=4,'col_0'=4,'col_1'=2] {'col_1'}, use_global_device_ids=true, to_apply=%region_26.27 | all-reduce | flops 128 | bytes 1024 | tf_op jit(solution)/shard_map/psum | solution.py:19
  537.0 3.7 all-to-all-start.8
  540.7 10.3 %all-gather.8 = f32[128,512]{1,0:T(8,128)S(1)} all-gather(f32[32,512]{1,0:T(8,128)S(1)} %get-tuple-element.699), channel_id=10, replica_groups=mesh['row_0'=4,'row_1'=4,'col_0'=4,'col_1'=2] {'col_0'}, dimensions={0}, use_global_device_ids=true | all-gather | bytes 327680 | tf_op jit(solution)/shard_map/all_gather | solution.py:71
  551.0 4.2 all-gather.9
  557.2 10.8 %all-gather.11 = f32[8,32,512]{2,1,0:T(8,128)S(1)} all-gather(f32[2,32,512]{2,1,0:T(8,128)S(1)} %bitcast.182), channel_id=13, replica_groups=mesh['row_0'=4,'row_1'=4,'col_0'=4,'col_1'=2] {'col_0'}, dimensions={0}, use_global_device_ids=true | all-gather | bytes 655360 | tf_op jit(solution)/shard_map/all_gather | solution.py:71
  571.7 51.3 %while.65 = (s32[]{:T(128)}, f32[64,4096]{1,0:T(8,128)S(1)}, f32[64,8192]{1,0:T(8,128)S(1)}, s32[8,3]{0,1:T(4,128)S(1)}, f32[64,8192]{1,0:T(8,128)}, /*index=5*/...) while((s32[]{:T(128)}, f32[64,4096]{1,0:T(8,128)S(1)}, ...), condition=%wide.region_42.43_spmd, body=%wide.region_41.42_spmd.sunk | while | flops 402718720 | bytes 2884853 | solution.py:219
  625.2 5.4 all-to-all-start.9
  634.4 11.4 %all-to-all-done.9 = f32[8,64,512]{2,1,0:T(8,128)S(1)} async-done(((f32[8,64,512]{2,1,0:T(8,128)}), f32[8,64,512]{2,1,0:T(8,128)S(1)}, u32[]{:S(2)}, u32[]{:S(2)}) %all-to-all-start.9) | async-done | bytes 1048608 | tf_op jit(solution)/shard_map/all_to_all | solution.py:44
  645.7 7.2 all-to-all-start.10
  653.6 25.7 %all-to-all-done.10 = f32[16,64,512]{2,1,0:T(8,128)S(1)} async-done(((f32[16,64,512]{2,1,0:T(8,128)}), f32[16,64,512]{2,1,0:T(8,128)S(1)}, u32[]{:S(2)}, u32[]{:S(2)}) %all-to-all-start.10) | async-done | bytes 2097184 | tf_op jit(solution)/shard_map/all_to_all | solution.py:44
  679.6 7.6 %all-reduce.6 = (f32[64]{0:T(128)S(1)}, f32[64]{0:T(128)S(1)}) all-reduce(f32[64]{0:T(128)S(1)} %get-tuple-element.575, f32[64]{0:T(128)S(1)} %get-tuple-element.574), channel_id=1, replica_groups=mesh['row_0'=4,'row_1'=4,'col_0'=4,'col_1'=2] {'row_0'}, use_global_device_ids=true, to_apply=%region_37.38 | all-reduce | flops 128 | bytes 1024 | tf_op jit(solution)/shard_map/psum | solution.py:19
  687.2 7.4 %all-reduce.3 = (f32[64]{0:T(128)S(1)}, f32[64]{0:T(128)S(1)}) all-reduce(f32[64]{0:T(128)S(1)} %get-tuple-element.656, f32[64]{0:T(128)S(1)} %get-tuple-element.657), channel_id=1, replica_groups=mesh['row_0'=4,'row_1'=4,'col_0'=4,'col_1'=2] {'row_1'}, use_global_device_ids=true, to_apply=%region_38.39 | all-reduce | flops 128 | bytes 1024 | tf_op jit(solution)/shard_map/psum | solution.py:19
  694.6 6.9 all-reduce
  701.4 10.5 %all-reduce.9 = (f32[64]{0:T(128)S(1)}, f32[64]{0:T(128)S(1)}) all-reduce(f32[64]{0:T(128)S(1)} %get-tuple-element.644, f32[64]{0:T(128)S(1)} %get-tuple-element.645), channel_id=1, replica_groups=mesh['row_0'=4,'row_1'=4,'col_0'=4,'col_1'=2] {'col_1'}, use_global_device_ids=true, to_apply=%region_40.41 | all-reduce | flops 128 | bytes 1024 | tf_op jit(solution)/shard_map/psum | solution.py:19
  (255 shorter events, 266.0 us)
Async XLA Ops:
  7.2 44.4 %all-gather.15.cloned.1.call-start = ((), (), s32[]{:S(2)}) async-start(), calls=%async_computation.11 | async-start | bytes 1327104 | tf_op jit(solution)/shard_map/all_gather | solution.py:27
  9.5 74.8 %all-gather.17.cloned.1.call-start = ((), (), s32[]{:S(2)}) async-start(), calls=%async_computation.12 | async-start | bytes 2506752 | tf_op jit(solution)/shard_map/all_gather | solution.py:27
  12.7 8.6 %copy-start.13 = (s32[1,1,8,3]{2,1,3,0:T(1,128)S(1)}, s32[1,1,8,3]{2,1,3,0:T(1,128)}, u32[]{:S(2)}) copy-start(s32[1,1,8,3]{2,1,3,0:T(1,128)} %param.19) | copy-start | bytes 292
  12.7 8.6 %copy-start = (f32[64,512]{1,0:T(8,128)S(1)}, f32[64,512]{1,0:T(8,128)}, u32[]{:S(2)}) copy-start(f32[64,512]{1,0:T(8,128)} %param.14) | copy-start | bytes 393220
  12.7 187.9 %all-to-all-start.2 = ((f32[16,64,512]{2,1,0:T(8,128)}), f32[16,64,512]{2,1,0:T(8,128)S(1)}, u32[]{:S(2)}, u32[]{:S(2)}) async-start(f32[16,64,512]{2,1,0:T(8,128)} %broadcast_in_dim.62), calls=%async_computation.2 | async-start | bytes 4194304 | tf_op jit(solution)/shard_map/all_to_all | solution.py:56
  52.8 35.8 %slice-start.1 = ((f32[4096,65]{0,1:T(8,128)}), f32[4096,1]{0,1:T(1,128)S(1)}, s32[]{:S(2)}) async-start(f32[4096,65]{0,1:T(8,128)} %all-gather.15.cloned.1.call-done), calls=%async_computation.14 | async-start | bytes 32768 | tf_op jit(solution)/shard_map/split | solution.py:28
  52.8 35.8 %copy-start.6 = (f32[2,2]{1,0:T(2,128)S(1)}, f32[2,2]{1,0:T(2,128)}, u32[]{:S(2)}) copy-start(f32[2,2]{1,0:T(2,128)} %param.18) | copy-start | bytes 52
  84.3 4.3 slice-start
  200.6 10.6 %all-to-all-start = ((f32[8,1,512]{2,1,0:T(1,128)}), f32[8,1,512]{2,1,0:T(1,128)S(1)}, u32[]{:S(2)}, u32[]{:S(2)}) async-start(f32[8,1,512]{2,1,0:T(1,128)} %bitcast.24), calls=%async_computation | async-start | bytes 32768 | tf_op jit(solution)/shard_map/all_to_all | solution.py:44
  211.2 58.9 %all-to-all-start.1 = ((f32[16,1,512]{2,1,0:T(1,128)}), f32[16,1,512]{2,1,0:T(1,128)S(1)}, u32[]{:S(2)}, u32[]{:S(2)}) async-start(f32[16,1,512]{2,1,0:T(1,128)} %bitcast.25), calls=%async_computation.1 | async-start | bytes 65536 | tf_op jit(solution)/shard_map/all_to_all | solution.py:44
  270.2 19.6 %all-to-all-start.3 = ((f32[8,64,512]{2,1,0:T(8,128)}), f32[8,64,512]{2,1,0:T(8,128)S(1)}, u32[]{:S(2)}, u32[]{:S(2)}) async-start(f32[8,64,512]{2,1,0:T(8,128)} %copy.52), calls=%async_computation.3 | async-start | bytes 2097152 | tf_op jit(solution)/shard_map/all_to_all | solution.py:44
  278.4 18.3 %copy-start.12 = (f32[512]{0:T(512)S(1)}, f32[512]{0:T(512)}, u32[]{:S(2)}) copy-start(f32[512]{0:T(512)} %param.17) | copy-start | bytes 6148
  289.7 33.4 %all-to-all-start.4 = ((f32[16,64,512]{2,1,0:T(8,128)}), f32[16,64,512]{2,1,0:T(8,128)S(1)}, u32[]{:S(2)}, u32[]{:S(2)}) async-start(f32[16,64,512]{2,1,0:T(8,128)} %copy.53), calls=%async_computation.4 | async-start | bytes 4194304 | tf_op jit(solution)/shard_map/all_to_all | solution.py:44
  323.4 34.1 %copy-start.3 = (f32[64,512]{1,0:T(8,128)}, f32[64,512]{1,0:T(8,128)S(1)}, u32[]{:S(2)}) copy-start(f32[64,512]{1,0:T(8,128)S(1)} %get-tuple-element.677) | copy-start | bytes 393220
  355.7 1.8 copy-start.14
  355.7 1.8 copy-start.16
  355.7 1.8 copy-start.7
  357.5 32.9 %all-to-all-start.5 = ((f32[16,64,512]{2,1,0:T(8,128)}), f32[16,64,512]{2,1,0:T(8,128)S(1)}, u32[]{:S(2)}, u32[]{:S(2)}) async-start(f32[16,64,512]{2,1,0:T(8,128)} %broadcast_in_dim.63), calls=%async_computation.5 | async-start | bytes 4194304 | tf_op jit(solution)/shard_map/all_to_all | solution.py:56
  446.1 20.6 %all-to-all-start.6 = ((f32[8,64,512]{2,1,0:T(8,128)}), f32[8,64,512]{2,1,0:T(8,128)S(1)}, u32[]{:S(2)}, u32[]{:S(2)}) async-start(f32[8,64,512]{2,1,0:T(8,128)} %copy.57), calls=%async_computation.6 | async-start | bytes 2097152 | tf_op jit(solution)/shard_map/all_to_all | solution.py:44
  466.6 33.9 %all-to-all-start.7 = ((f32[16,64,512]{2,1,0:T(8,128)}), f32[16,64,512]{2,1,0:T(8,128)S(1)}, u32[]{:S(2)}, u32[]{:S(2)}) async-start(f32[16,64,512]{2,1,0:T(8,128)} %copy.58), calls=%async_computation.7 | async-start | bytes 4194304 | tf_op jit(solution)/shard_map/all_to_all | solution.py:44
  474.1 59.5 %copy-start.1 = (f32[64,512]{1,0:T(8,128)}, f32[64,512]{1,0:T(8,128)S(1)}, u32[]{:S(2)}) copy-start(f32[64,512]{1,0:T(8,128)S(1)} %reduce_sum.185) | copy-start | bytes 393220
  474.1 58.9 %copy-start.15 = (f32[64]{0:T(128)S(1)}, f32[64]{0:T(128)}, u32[]{:S(2)}) copy-start(f32[64]{0:T(128)} %copy-done.14) | copy-start | bytes 772
  474.2 58.9 %copy-start.17 = (f32[64]{0:T(128)S(1)}, f32[64]{0:T(128)}, u32[]{:S(2)}) copy-start(f32[64]{0:T(128)} %copy-done.16) | copy-start | bytes 772
  474.2 59.5 %copy-start.4 = (f32[64,512]{1,0:T(8,128)S(1)}, f32[64,512]{1,0:T(8,128)}, u32[]{:S(2)}) copy-start(f32[64,512]{1,0:T(8,128)} %copy-done.3) | copy-start | bytes 393220
  533.1 3.9 copy-start.9
  537.0 32.9 %all-to-all-start.8 = ((f32[16,64,512]{2,1,0:T(8,128)}), f32[16,64,512]{2,1,0:T(8,128)S(1)}, u32[]{:S(2)}, u32[]{:S(2)}) async-start(f32[16,64,512]{2,1,0:T(8,128)} %broadcast_in_dim.64), calls=%async_computation.8 | async-start | bytes 4194304 | tf_op jit(solution)/shard_map/all_to_all | solution.py:56
  625.2 20.5 %all-to-all-start.9 = ((f32[8,64,512]{2,1,0:T(8,128)}), f32[8,64,512]{2,1,0:T(8,128)S(1)}, u32[]{:S(2)}, u32[]{:S(2)}) async-start(f32[8,64,512]{2,1,0:T(8,128)} %copy.62), calls=%async_computation.9 | async-start | bytes 2097152 | tf_op jit(solution)/shard_map/all_to_all | solution.py:44
  645.7 33.6 %all-to-all-start.10 = ((f32[16,64,512]{2,1,0:T(8,128)}), f32[16,64,512]{2,1,0:T(8,128)S(1)}, u32[]{:S(2)}, u32[]{:S(2)}) async-start(f32[16,64,512]{2,1,0:T(8,128)} %copy.63), calls=%async_computation.10 | async-start | bytes 4194304 | tf_op jit(solution)/shard_map/all_to_all | solution.py:44
  652.9 59.1 %copy-start.8 = (f32[64]{0:T(128)S(1)}, f32[64]{0:T(128)}, u32[]{:S(2)}) copy-start(f32[64]{0:T(128)} %copy-done.7) | copy-start | bytes 772
  653.6 25.9 %copy-start.2 = (f32[64,512]{1,0:T(8,128)S(1)}, f32[64,512]{1,0:T(8,128)}, u32[]{:S(2)}) copy-start(f32[64,512]{1,0:T(8,128)} %reduce_sum.189) | copy-start | bytes 393220
  653.6 58.3 %copy-start.10 = (f32[64]{0:T(128)S(1)}, f32[64]{0:T(128)}, u32[]{:S(2)}) copy-start(f32[64]{0:T(128)} %copy-done.9) | copy-start | bytes 772
  653.6 58.3 %copy-start.11 = (f32[64]{0:T(128)S(1)}, f32[64]{0:T(128)}, u32[]{:S(2)}) copy-start(f32[64]{0:T(128)} %get-tuple-element.675) | copy-start | bytes 772
  653.6 58.3 %copy-start.5 = (f32[64,512]{1,0:T(8,128)S(1)}, f32[64,512]{1,0:T(8,128)}, u32[]{:S(2)}) copy-start(f32[64,512]{1,0:T(8,128)} %get-tuple-element.673) | copy-start | bytes 393220
Sparse Core Ops, SparseCore 0:
  9.7 28.2 all-gather.14
  40.2 44.1 all-gather.16
where the time goes:
time: 724 us; the launch traced here: 720 us
  blocking collectives  181 us (25%)
  waiting for transfers between devices  146 us (20%)
  matrix products  132 us (18%)
  local copies, waits for them, and re-layouts  79.3 us (11%)
  starting transfers between devices  63.5 us (9%)
  other arithmetic  61.5 us (8%)
  loops' own time  41.6 us (6%)
  between operations  14.4 us (2%)
    all_to_all x8, waiting for transfers between devices, sent_and_summed(): lax.all_to_all(blocks, axis, split_axis=0, concat_axis=0, tiled=True)  113 us
    psum x12, blocking collectives, over_axes(): shard = lax.psum(shard, axis)  96.8 us
    all_gather x12, blocking collectives, stacked_from(): blocks = lax.all_gather(blocks, axes[k])  83.9 us
    dot_general x24, matrix products, work(): lax.dot_general(take_segment(column_values, column_block), block_matrix,...  58 us
    dot_general x24, matrix products, work(): jnp.dot(take_segment(row_values, row_block), block_matrix, precision=lax....  49.5 us
    all_to_all x8, starting transfers between devices, sent_and_summed(): lax.all_to_all(blocks, axis, split_axis=0, concat_axis=0, tiled=True)  47.4 us
    another operation x3, loops' own time, operate(): row_image, column_image = lax.fori_loop(0, count, sweep, start_image)  31.5 us
    all_gather x2, waiting for transfers between devices, turned_gather(): filled = lax.all_gather(both, axis, axis=0, tiled=True)  31.5 us
  transfers between devices with their start and end apart: 13, of which 10 were waited for; matrix products, arithmetic and copies ran while one was open for 24% of the time, Pallas kernels for 0%

commit v1 on v0

v1 whole, which is shorter than its diff:
```python
import functools
import math

import jax
import jax.numpy as jnp
from jax import lax
from jax.experimental import pallas as pl
from jax.experimental.pallas import tpu as pltpu
from jax.sharding import Mesh
from jax.sharding import PartitionSpec as P

TILE = 512
X, Z, Y, C = "row_0", "row_1", "col_0", "col_1"
ALL = (X, Z, Y, C)
ROW, COL = (X, Z), (Y, C)
BODY = 256
ROWS = BODY + 8
KEPT = 32
LISTED = 136
SLOTS_OUT = 144
KAPPA = math.log2(math.e) / 12.0
F32, BF16 = jnp.float32, jnp.bfloat16


def along_row(stage, step):
    pairs = []
    for x in range(4):
        for z in range(4):
            for y in range(4):
                for c in range(2):
                    if (c == 0) == (stage == 1):
                        to = ((x + step) % 4, z)
                    else:
                        to = (x, (z + step) % 4)
                    pairs.append((((x * 4 + z) * 4 + y) * 2 + c, ((to[0] * 4 + to[1]) * 4 + y) * 2 + c))
    return pairs


def hop(a, stage, step):
    return lax.ppermute(a, ALL, along_row(stage, step))


def gather_row(block):
    far = hop(block, 1, 2)
    ahead = hop(block, 1, -1)
    behind = hop(block, 1, 1)
    line = jnp.stack([block, ahead, far, behind])
    right = hop(line, 2, -1)
    left = hop(line, 2, 1)
    far_left = hop(left[:2], 2, 1)
    far_right = hop(right[2:], 2, -1)
    return line, right, far_left, far_right, left


def shift_y(a, step):
    return lax.ppermute(a, Y, [(i, (i + step) % 4) for i in range(4)])


def reduce_col(keep, other):
    got = lax.ppermute(other, C, [(0, 1), (1, 0)])
    parts = [keep[j] + got[j] for j in range(4)]
    return parts[0], shift_y(parts[2], 2), shift_y(parts[1], 1), shift_y(parts[3], -1)


def halves(v):
    h = v.astype(BF16).astype(F32)
    m = (v - h).astype(BF16).astype(F32)
    return h, m, v - h - m


def rows_of(values, count, width):
    at = lax.broadcasted_iota(jnp.int32, (count, width), 0)
    out = jnp.zeros((count, width), F32)
    for k, value in enumerate(values):
        out = jnp.where(at == k, value, out)
    return out


def make_tile(fin, lin, fout, lout, turned, lc_ref, e_ref, pair_ref):
    h, m, l = halves(fin)
    norms = halves(-KAPPA * jnp.sum(fin * fin, axis=0, keepdims=True))
    aug = rows_of([*norms, 1.0, 1.0, 1.0, *[1.0 - lin, lin] * 3], 16, TILE)
    hm = jnp.concatenate([h, m], axis=0).T.astype(BF16)
    hl = jnp.concatenate([h, l], axis=0).T.astype(BF16)
    au = jnp.concatenate([aug, jnp.zeros((112, TILE), F32)], axis=0).T.astype(BF16)
    left = jnp.concatenate([hm, hm, hl, au], axis=1)
    g, n, k = halves(fout * (2.0 * KAPPA))
    norms = halves(-KAPPA * jnp.sum(fout * fout, axis=0, keepdims=True))
    levels = []
    for i in range(2):
        first = jnp.where(turned, lc_ref[2 * i], lc_ref[i])
        second = jnp.where(turned, lc_ref[2 * i + 1], lc_ref[2 + i])
        levels.append(halves(jnp.where(lout > 0.5, second, first)))
    logs = [levels[i][j] for j in range(3) for i in range(2)]
    aug = rows_of([1.0, 1.0, 1.0, *norms, *logs], 16, TILE)
    right = jnp.concatenate([g, g, n, n, k, g, aug, jnp.zeros((112, TILE), F32)], axis=0).astype(BF16)
    e_ref[...] = jnp.dot(left, right, preferred_element_type=F32)
    total = jnp.zeros((8, TILE), F32)
    for at in range(0, TILE, 64):
        t = jnp.exp2(e_ref[at : at + 64, :])
        hi = t.astype(BF16)
        pair_ref[0, at : at + 64, :] = hi
        pair_ref[1, at : at + 64, :] = (t - hi.astype(F32)).astype(BF16)
        total = total + jnp.sum(t.reshape(8, 8, TILE), axis=0)
    return jnp.sum(total, axis=0, keepdims=True)


def add_product(xs_ref, place, pair_ref, acc_ref, k):
    x = xs_ref[place]
    both = jnp.dot(x, pair_ref[0], preferred_element_type=F32)
    low = jnp.dot(x[:64], pair_ref[1], preferred_element_type=F32)
    out = both[:64] + both[64:] + low
    for g in range(4):
        acc_ref[k, g * 64 : g * 64 + 64, :] += out[:, g * 128 : g * 128 + 128]


def split_into(xs_ref, place, lanes, value):
    hi = value.astype(BF16)
    xs_ref[place, 0:64, lanes] = hi
    xs_ref[place, 64:128, lanes] = (value - hi.astype(F32)).astype(BF16)


def unpack(entry):
    return entry & 7, (entry >> 3) & 15, ((entry >> 7) & 1) == 1, entry >> 8


def first_kernel(
    info_ref, lc_ref, line, right, far_left, far_right, left, outs_ref,
    keep_ref, other_ref, list_ref, store_ref, facts_ref,
    fin_ref, xs_ref, e_ref, pair_ref, acc_ref, sems, fact_sem,
):
    place = 0
    for piece in (line, right, far_left, far_right, left):
        for j in range(piece.shape[0]):
            fin_ref[place, 0:64, :] = piece[j, 0:64, :]
            fin_ref[place, 64:72, :] = piece[j, 128:136, :]
            split_into(xs_ref, place, slice(None), piece[j, 64:128, :])
            place += 1
    facts = pltpu.make_async_copy(fin_ref, facts_ref, fact_sem)
    facts.start()
    acc_ref[...] = jnp.zeros_like(acc_ref)

    def enlist(i, n):
        list_ref[n] = info_ref[0, i]
        return n + info_ref[1, i]

    n = lax.fori_loop(0, LISTED, enlist, jnp.int32(0), unroll=8)
    list_ref[SLOTS_OUT - 1] = n

    def saved(t):
        slot = t & 1
        return pltpu.make_async_copy(pair_ref.at[slot], store_ref.at[jnp.minimum(t, KEPT - 1)], sems.at[slot])

    def visit(t, carry):
        k, place, turned, block = unpack(list_ref[t])
        slot = t & 1

        @pl.when((t >= 2) & (t - 2 < KEPT))
        def _():
            saved(t - 2).wait()

        pair = pair_ref.at[slot]
        sums = make_tile(
            fin_ref[place, 0:64, :], fin_ref[place, 64:65, :], outs_ref[block, 0:64, :], outs_ref[block, 64:65, :],
            turned, lc_ref, e_ref, pair,
        )

        @pl.when(t < KEPT)
        def _():
            saved(t).start()

        add_product(xs_ref, place, pair, acc_ref, k)
        spread = jnp.concatenate([sums[:, g * 128 : g * 128 + 128] for g in range(4)] + [jnp.zeros((4, 128), F32)], axis=0)
        acc_ref[k, BODY:ROWS, :] += spread
        return carry

    lax.fori_loop(0, n, visit, jnp.int32(0))
    for back in (2, 1):

        @pl.when((n >= back) & (n - back < KEPT))
        def _():
            saved(n - back).wait()

    keep_ref[...] = acc_ref[0:4]
    other_ref[...] = acc_ref[4:8]
    facts.wait()


DEPTH = 4


def operate_kernel(
    list_ref, lc_ref, line, right, far_left, far_right, left, store_ref, facts_ref, outs_ref,
    keep_ref, other_ref,
    fin_ref, fout_ref, xs_ref, e_ref, pair_ref, acc_ref, sems, fact_sems,
):
    n = list_ref[SLOTS_OUT - 1]
    kept = jnp.minimum(n, KEPT)

    def loaded(t):
        slot = t & (DEPTH - 1)
        return pltpu.make_async_copy(store_ref.at[jnp.minimum(t, KEPT - 1)], pair_ref.at[slot], sems.at[slot])

    for t in range(DEPTH):

        @pl.when(t < kept)
        def _():
            loaded(t).start()

    place = 0
    sums = jnp.zeros((8, 128), F32)
    for piece in (line, right, far_left, far_right, left):
        for j in range(piece.shape[0]):
            for g in range(4):
                split_into(xs_ref, place, slice(g * 128, g * 128 + 128), piece[j, g * 64 : g * 64 + 64, :])
            sums = sums + piece[j, BODY:ROWS, :]
            place += 1
    acc_ref[...] = jnp.zeros_like(acc_ref)
    for k in range(8):
        acc_ref[k, BODY:ROWS, :] = sums

    def visit(t, carry):
        k, place, _, _ = unpack(list_ref[t])
        loaded(t).wait()
        add_product(xs_ref, place, pair_ref.at[t & (DEPTH - 1)], acc_ref, k)

        @pl.when(t + DEPTH < kept)
        def _():
            loaded(t + DEPTH).start()

        return carry

    lax.fori_loop(0, kept, visit, jnp.int32(0))

    def visit_again(t, carry):
        k, place, turned, block = unpack(list_ref[t])
        first = pltpu.make_async_copy(facts_ref.at[place], fin_ref, fact_sems.at[0])
        second = pltpu.make_async_copy(outs_ref.at[block], fout_ref, fact_sems.at[1])
        first.start()
        second.start()
        first.wait()
        second.wait()
        pair = pair_ref.at[0]
        make_tile(fin_ref[0:64, :], fin_ref[64:65, :], fout_ref[0:64, :], fout_ref[64:65, :], turned, lc_ref, e_ref, pair)
        add_product(xs_ref, place, pair, acc_ref, k)
        return carry

    lax.fori_loop(kept, n, visit_again, jnp.int32(0))
    keep_ref[...] = acc_ref[0:4]
    other_ref[...] = acc_ref[4:8]


def group(g):
    return slice(g * 64, g * 64 + 64)


def lanes(g):
    return slice(g * 128, g * 128 + 128)


def sum_rows(first, second):
    both = jnp.concatenate([first, second], axis=0)
    column = jnp.broadcast_to(jnp.sum(both, axis=1, keepdims=True), (128, 128))
    return column.T[0:8, :]


def columns_of(row):
    turned = jnp.broadcast_to(row, (128, 128)).T
    return turned[0:64], turned[64:128]


def total_of(parts, rows):
    a, b, c, d = parts
    return (a[rows, :] + b[rows, :]) + (c[rows, :] + d[rows, :])


def after_first(a, b, c, d, r_ref, err_ref, w_ref, diag_ref):
    parts = (a, b, c, d)
    diag = err_ref[0:4, :] + total_of(parts, slice(BODY, BODY + 4))
    diag_ref[0:4, :] = diag
    diag_ref[4:8, :] = jnp.zeros((4, 128), F32)
    rr, rw = jnp.zeros((64, 128), F32), jnp.zeros((64, 128), F32)
    for g in range(4):
        r = r_ref[:, lanes(g)]
        w = diag[g : g + 1, :] * r + total_of(parts, group(g))
        w_ref[group(g), :] = w
        rr, rw = rr + r * r, rw + r * w
    w_ref[BODY:ROWS, :] = sum_rows(rr, rw)


def after_second(a, b, c, d, r_ref, w_ref, diag_ref, next_ref, r1_ref, q_ref, past_ref):
    parts = (a, b, c, d)
    rr0, rw0 = columns_of(total_of(parts, slice(BODY, BODY + 1)))
    alpha = rr0 / rw0
    past_ref[0:64, :] = alpha
    past_ref[64:128, :] = rr0
    rr, rw = jnp.zeros((64, 128), F32), jnp.zeros((64, 128), F32)
    for g in range(4):
        w0 = w_ref[group(g), :]
        q = diag_ref[g : g + 1, :] * w0 + total_of(parts, group(g))
        r = r_ref[:, lanes(g)] - alpha * w0
        w = w0 - alpha * q
        q_ref[group(g), :] = q
        r1_ref[group(g), :] = r
        next_ref[group(g), :] = w
        rr, rw = rr + r * r, rw + r * w
    next_ref[BODY:ROWS, :] = sum_rows(rr, rw)


def after_third(
    a, b, c, d, r_ref, w0_ref, diag_ref, w1_ref, r1_ref, q_ref, past_ref,
    sums_ref, r2_ref, w2_ref, s1_ref, p1_ref, x_ref, now_ref,
):
    parts = (a, b, c, d)
    rr1, rw1 = columns_of(total_of(parts, slice(BODY, BODY + 1)))
    alpha0, rr0 = past_ref[0:64, :], past_ref[64:128, :]
    beta = rr1 / rr0
    alpha = rr1 / (rw1 - beta * rr1 / alpha0)
    now_ref[0:64, :] = alpha
    now_ref[64:128, :] = rr1
    rr, rw = jnp.zeros((64, 128), F32), jnp.zeros((64, 128), F32)
    for g in range(4):
        w1, r1, r0 = w1_ref[group(g), :], r1_ref[group(g), :], r_ref[:, lanes(g)]
        q1 = diag_ref[g : g + 1, :] * w1 + total_of(parts, group(g))
        s = w1 + beta * w0_ref[group(g), :]
        z = q1 + beta * q_ref[group(g), :]
        p = r1 + beta * r0
        r = r1 - alpha * s
        w = w1 - alpha * z
        s1_ref[group(g), :] = s
        p1_ref[group(g), :] = p
        x_ref[group(g), :] = alpha0 * r0 + alpha * p
        r2_ref[group(g), :] = r
        w2_ref[group(g), :] = w
        rr, rw = rr + r * r, rw + r * w
    sums_ref[...] = sum_rows(rr, rw)


def finish(sums_ref, r2_ref, w2_ref, s1_ref, p1_ref, x_ref, now_ref, inc_ref, res_ref):
    rr2, rw2 = columns_of(sums_ref[...])
    alpha1, rr1 = now_ref[0:64, :], now_ref[64:128, :]
    beta = rr2 / rr1
    alpha = rr2 / (rw2 - beta * rr2 / alpha1)
    for g in range(4):
        r = r2_ref[group(g), :]
        p = r + beta * p1_ref[group(g), :]
        s = w2_ref[group(g), :] + beta * s1_ref[group(g), :]
        inc_ref[:, lanes(g)] = x_ref[group(g), :] + alpha * p
        res_ref[:, lanes(g)] = r - alpha * s


VMEM = pl.BlockSpec(memory_space=pltpu.VMEM)
SMEM = pl.BlockSpec(memory_space=pltpu.SMEM)
ANY = pl.BlockSpec(memory_space=pl.ANY)


def small_call(body, shapes, args):
    out = [jax.ShapeDtypeStruct(s, F32) for s in shapes]
    return pl.pallas_call(
        body,
        out_shape=out,
        in_specs=[VMEM] * len(args),
        out_specs=[VMEM] * len(shapes),
        cost_estimate=pl.CostEstimate(flops=4_000_000, bytes_accessed=2_000_000, transcendentals=0),
    )(*args)


PART = jax.ShapeDtypeStruct((4, ROWS, 128), F32)


def first_operate(info, log_coupling, pieces, outs):
    return pl.pallas_call(
        first_kernel,
        out_shape=[
            PART,
            PART,
            jax.ShapeDtypeStruct((SLOTS_OUT,), jnp.int32),
            jax.ShapeDtypeStruct((KEPT, 2, TILE, TILE), BF16),
            jax.ShapeDtypeStruct((16, 72, TILE), F32),
        ],
        in_specs=[SMEM, SMEM] + [VMEM] * 6,
        out_specs=[VMEM, VMEM, SMEM, ANY, ANY],
        scratch_shapes=[
            pltpu.VMEM((16, 72, TILE), F32),
            pltpu.VMEM((16, 128, TILE), BF16),
            pltpu.VMEM((TILE, TILE), F32),
            pltpu.VMEM((2, 2, TILE, TILE), BF16),
            pltpu.VMEM((8, ROWS, 128), F32),
            pltpu.SemaphoreType.DMA((2,)),
            pltpu.SemaphoreType.DMA,
        ],
        compiler_params=pltpu.CompilerParams(vmem_limit_bytes=40 << 20),
        cost_estimate=pl.CostEstimate(flops=8_000_000_000, bytes_accessed=20_000_000, transcendentals=2_000_000),
    )(info, log_coupling, *pieces, outs)


def later_operate(listed, log_coupling, pieces, store, facts, outs):
    return pl.pallas_call(
        operate_kernel,
        out_shape=[PART, PART],
        in_specs=[SMEM, SMEM] + [VMEM] * 5 + [ANY] * 3,
        out_specs=[VMEM, VMEM],
        scratch_shapes=[
            pltpu.VMEM((72, TILE), F32),
            pltpu.VMEM((72, TILE), F32),
            pltpu.VMEM((16, 128, TILE), BF16),
            pltpu.VMEM((TILE, TILE), F32),
            pltpu.VMEM((DEPTH, 2, TILE, TILE), BF16),
            pltpu.VMEM((8, ROWS, 128), F32),
            pltpu.SemaphoreType.DMA((DEPTH,)),
            pltpu.SemaphoreType.DMA((2,)),
        ],
        compiler_params=pltpu.CompilerParams(vmem_limit_bytes=40 << 20),
        cost_estimate=pl.CostEstimate(flops=4_000_000_000, bytes_accessed=12_000_000, transcendentals=0),
    )(listed, log_coupling, *pieces, store, facts, outs)


def worklist(slots, seen, place):
    x, z, y, c = place
    mine = 128 + (y * 2 + c) * 16 + x * 4 + z
    turned = jnp.any(seen == mine, axis=1).astype(jnp.int32)
    index = jnp.arange(128, dtype=jnp.int32)
    a = jnp.concatenate([slots[:, 0], index & 7])
    b = jnp.concatenate([slots[:, 1], index >> 3])
    flag = jnp.concatenate([jnp.zeros((8,), jnp.int32), jnp.ones((128,), jnp.int32)])
    k = ((a & 1) ^ c) * 4 + (((a >> 1) - y) & 3)
    dx, dz = ((b >> 2) - x) & 3, ((b & 3) - z) & 3
    s1, s2 = jnp.where(c == 0, dx, dz), jnp.where(c == 0, dz, dx)
    entry = k + 8 * (s2 * 4 + s1) + 128 * flag + 256 * a
    live = jnp.concatenate([slots[:, 2], turned])
    return jnp.pad(jnp.stack([entry, live]), ((0, 0), (0, SLOTS_OUT - LISTED)))


def to_everyone(row, count, axes):
    copies = jnp.broadcast_to(row.reshape(1, 1, 128), (count, 1, 128))
    return lax.all_to_all(copies, axes, split_axis=0, concat_axis=0, tiled=True)


def shards(innovations, obs_factors, component, obs_error, coupling, tile_slots):
    place = tuple(lax.axis_index(axis) for axis in ALL)
    labels = jnp.broadcast_to(component.astype(F32)[None, :], (8, TILE))
    payload = jnp.concatenate([obs_factors, innovations, labels], axis=0)
    pieces = gather_row(payload)
    facts = jnp.concatenate([obs_factors, labels], axis=0)
    copies = jnp.broadcast_to(facts[None], (8, *facts.shape))
    outs = lax.all_to_all(copies, COL, split_axis=0, concat_axis=0, tiled=True)
    slots = tile_slots[0, 0]
    code = slots[:, 2] * 128 + slots[:, 0] * 16 + slots[:, 1]
    seen = to_everyone(jnp.pad(code, (0, 120)), 128, ALL)[:, 0, 0:8]
    info = worklist(slots, seen, place)
    log_coupling = jnp.log2(coupling).reshape(4)
    error_rows = jnp.pad(obs_error.reshape(4, 128), ((0, 4), (0, 0)))

    vec, body, two = (ROWS, 128), (BODY, 128), (128, 128)
    keep, other, listed, store, kept_facts = first_operate(info, log_coupling, pieces, outs)
    parts = reduce_col(keep, other)
    w0, diag = small_call(after_first, [vec, (8, 128)], (*parts, innovations, error_rows))

    keep, other = later_operate(listed, log_coupling, gather_row(w0), store, kept_facts, outs)
    parts = reduce_col(keep, other)
    w1, r1, q0, past = small_call(after_second, [vec, body, body, two], (*parts, innovations, w0, diag))

    keep, other = later_operate(listed, log_coupling, gather_row(w1), store, kept_facts, outs)
    parts = reduce_col(keep, other)
    sums, r2, w2, s1, p1, x2, now = small_call(
        after_third,
        [(8, 128), body, body, body, body, body, two],
        (*parts, innovations, w0, diag, w1, r1, q0, past),
    )
    sums = jnp.sum(to_everyone(sums[0:1], 128, ALL), axis=0)
    increment, residual = small_call(finish, [(64, TILE)] * 2, (sums, r2, w2, s1, p1, x2, now))
    return increment, residual


def solution(mesh):
    finer = Mesh(mesh.devices.reshape(4, 4, 4, 2), ALL)
    in_specs = (P(None, ALL), P(None, ALL), P(ALL), P(ALL), P(), P(ROW, COL, None, None))
    out_specs = (P(None, ALL), P(None, ALL))
    return jax.shard_map(shards, mesh=finer, in_specs=in_specs, out_specs=out_specs, check_vma=False)
```

time: 724 us -> 215 us (0.30)
  blocking collectives: 181 us -> 16.5 us
  matrix products: 132 us -> 0 us
  local copies, waits for them, and re-layouts: 79.3 us -> 11.8 us
  waiting for transfers between devices: 146 us -> 85.6 us
  other arithmetic: 61.5 us -> 6.65 us
  loops' own time: 41.6 us -> 0 us
  Pallas kernels: 0 us -> 25.4 us
  between operations: 14.4 us -> 0.9 us
    dot_general x56 -> x0, matrix products: 132 us -> none  [the longest x24 58 us: work(): lax.dot_general(take_segment(column_values, column_block), block_matrix,...]
    psum x12 -> x0, blocking collectives: 96.8 us -> none  [over_axes(): shard = lax.psum(shard, axis)]
    all_to_all x11 -> x2, waiting for transfers between devices: 114 us -> 20.8 us  [the longest x1 11.4 us: shards(): outs = lax.all_to_all(copies, COL, split_axis=0, concat_axis=0, tiled=True)]
    all_gather x12 -> x0, blocking collectives: 83.9 us -> none  [stacked_from(): blocks = lax.all_gather(blocks, axes[k])]
    ppermute x0 -> x33, waiting for transfers between devices: none -> 64.8 us  [the longest x21 38.8 us: hop(): return lax.ppermute(a, ALL, along_row(stage, step))]
    ppermute x0 -> x33, starting transfers between devices: none -> 51.4 us  [the longest x21 28.9 us: hop(): return lax.ppermute(a, ALL, along_row(stage, step))]
    all_to_all x11 -> x2, starting transfers between devices: 63.4 us -> 14.1 us  [the longest x1 9.58 us: to_everyone(): return lax.all_to_all(copies, axes, split_axis=0, concat_axis=0, tiled=True)]
    another operation x4 -> x0, loops' own time: 41.6 us -> none  [the longest x3 31.5 us: operate(): row_image, column_image = lax.fori_loop(0, count, sweep, start_image)]
  transfers between devices with their start and end apart: 13 -> 35, of which waited for: 10 -> 25; matrix products, arithmetic and copies ran while one was open for 24% -> 2% of each run, Pallas kernels for 0% -> 0%
where the time goes in v1:
time: 215 us; the launch traced here: 212 us
  waiting for transfers between devices  85.6 us (40%)
  starting transfers between devices  65.4 us (30%)
  Pallas kernels  25.4 us (12%)
  blocking collectives  16.5 us (8%)
  local copies, waits for them, and re-layouts  11.8 us (5%)
  other arithmetic  6.65 us (3%)
    ppermute x21, waiting for transfers between devices, hop(): return lax.ppermute(a, ALL, along_row(stage, step))  38.8 us
    ppermute x21, starting transfers between devices, hop(): return lax.ppermute(a, ALL, along_row(stage, step))  28.9 us
    ppermute x9, waiting for transfers between devices, shift_y(): return lax.ppermute(a, Y, [(i, (i + step) % 4) for i in range(4)])  21.3 us
    all_to_all x1, blocking collectives, to_everyone(): return lax.all_to_all(copies, axes, split_axis=0, concat_axis=0, tiled=True)  16.5 us
    ppermute x3, starting transfers between devices, reduce_col(): got = lax.ppermute(other, C, [(0, 1), (1, 0)])  15.7 us
    all_to_all x1, waiting for transfers between devices, shards(): outs = lax.all_to_all(copies, COL, split_axis=0, concat_axis=0, tiled=True)  11.4 us
    all_to_all x1, starting transfers between devices, to_everyone(): return lax.all_to_all(copies, axes, split_axis=0, concat_axis=0, tiled=True)  9.58 us
    all_to_all x1, waiting for transfers between devices, to_everyone(): return lax.all_to_all(copies, axes, split_axis=0, concat_axis=0, tiled=True)  9.38 us
  transfers between devices with their start and end apart: 35, of which 25 were waited for; matrix products, arithmetic and copies ran while one was open for 2% of the time, Pallas kernels for 0%

profile of v1, /device:TPU:1, one launch (start us, length us, event | category | flops | bytes accessed | tf_op | source)
XLA Modules:
  0.0 212.3 jit_solution(9326539423454954532)
XLA Ops:
  2.3 4.5 %collective-permute-start.1 = (f32[136,512]{1,0:T(8,128)S(1)}, f32[136,512]{1,0:T(8,128)S(1)}, u32[]{:S(2)}, u32[]{:S(2)}) collective-permute-start(f32[136,512]{1,0:T(8,128)S(1)} %get-tuple-element.59), channel_id=1, source_target_pairs={{0,64},{1,17},{2,66},{3,19},{4,68},{5,21},{6,70},{7,23},{8,72},{9,... | collective-permute-start | bytes 835592 | tf_op jit(solution)/shard_map/ppermute | solution.py:40
  7.6 1.9 collective-permute-start
  9.5 1.6 collective-permute-done.1
  11.1 3.0 %collective-permute-done.2 = f32[136,512]{1,0:T(8,128)S(1)} collective-permute-done((f32[136,512]{1,0:T(8,128)S(1)}, f32[136,512]{1,0:T(8,128)S(1)}, u32[]{:S(2)}, u32[]{:S(2)}) %collective-permute-start.2) | collective-permute-done | bytes 278560 | tf_op jit(solution)/shard_map/ppermute | solution.py:40
  14.8 1.3 collective-permute-start.4
  16.0 1.5 collective-permute-start.3
  18.2 9.6 %all-to-all-start = ((s32[128,1,128]{2,1,0:T(1,128)}), s32[128,1,128]{2,1,0:T(1,128)S(1)}, u32[]{:S(2)}, u32[]{:S(2)}) async-start(s32[128,1,128]{2,1,0:T(1,128)} %broadcast_in_dim.10), calls=%async_computation | async-start | bytes 131072 | tf_op jit(solution)/shard_map/all_to_all | solution.py:436
  27.9 9.4 %all-to-all-done = s32[128,1,128]{2,1,0:T(1,128)S(1)} async-done(((s32[128,1,128]{2,1,0:T(1,128)}), s32[128,1,128]{2,1,0:T(1,128)S(1)}, u32[]{:S(2)}, u32[]{:S(2)}) %all-to-all-start) | async-done | bytes 65568 | tf_op jit(solution)/shard_map/all_to_all | solution.py:436
  38.4 4.5 %all-to-all-start.1 = ((f32[8,72,512]{2,1,0:T(8,128)}), f32[8,72,512]{2,1,0:T(8,128)S(1)}, u32[]{:S(2)}, u32[]{:S(2)}) async-start(f32[8,72,512]{2,1,0:T(8,128)} %broadcast_in_dim.12), calls=%async_computation.1 | async-start | bytes 2359296 | tf_op jit(solution)/shard_map/all_to_all | solution.py:446
  45.3 2.4 %collective-permute-start.6 = (f32[2,136,512]{2,1,0:T(8,128)S(1)}, f32[2,136,512]{2,1,0:T(8,128)S(1)}, u32[]{:S(2)}, u32[]{:S(2)}) collective-permute-start(f32[2,136,512]{2,1,0:T(8,128)S(1)} %slice.145), channel_id=1, source_target_pairs={{0,24},{1,97},{2,26},{3,99},{4,28},{5,101},{6,30},{7,103},{8,0},{9... | collective-permute-start | bytes 1671176 | tf_op jit(solution)/shard_map/ppermute | solution.py:40
  48.0 11.4 %all-to-all-done.1.outs_ref = f32[8,72,512]{2,1,0:T(8,128)S(1)} async-done(((f32[8,72,512]{2,1,0:T(8,128)}), f32[8,72,512]{2,1,0:T(8,128)S(1)}, u32[]{:S(2)}, u32[]{:S(2)}) %all-to-all-start.1) | async-done | bytes 1179680 | tf_op jit(solution)/shard_map/all_to_all | solution.py:446
  63.8 8.9 %shard_map.77 = (f32[4,264,128]{2,1,0:T(8,128)S(1)}, f32[4,264,128]{2,1,0:T(8,128)S(1)}, s32[144]{0:T(256)S(1)}, bf16[32,2,512,512]{3,2,1,0:T(8,128)(2,1)}, f32[16,72,512]{2,1,0:T(8,128)S(1)}) custom-call(s32[2,144]{1,0:T(2,128)S(1)} %pad.13.info_ref, f32[4]{0:T(128)S(1)} %reshape.205.lc_ref, f32[4,136,512]{2,1,0:T(8,128)S(1)} %copy-done.1, ...), custom_call_target="tpu_custom_call" | custom-call | flops 8000000000 | bytes 20000000 | tf_op jit(solution)/shard_map/pallas_call | solution.py:372
  72.7 4.3 %collective-permute-start.7 = (f32[4,264,128]{2,1,0:T(8,128)S(1)}, f32[4,264,128]{2,1,0:T(8,128)S(1)}, u32[]{:S(2)}, u32[]{:S(2)}) collective-permute-start(f32[4,264,128]{2,1,0:T(8,128)S(1)} %get-tuple-element.26), channel_id=1, source_target_pairs={{0,1},{1,0},{2,3},{3,2},{4,5},{5,4},{6,7},{7,6},{8,9},{9,8},{10,11... | collective-permute-start | bytes 1622024 | tf_op jit(solution)/shard_map/ppermute | solution.py:60
  77.0 1.6 collective-permute-done.7
  79.3 1.5 collective-permute-start.9
  81.4 2.7 %collective-permute-done.10.d = f32[264,128]{1,0:T(8,128)S(1)} collective-permute-done((f32[264,128]{1,0:T(8,128)S(1)}, f32[264,128]{1,0:T(8,128)S(1)}, u32[]{:S(2)}, u32[]{:S(2)}) %collective-permute-start.10) | collective-permute-done | bytes 135200 | tf_op jit(solution)/shard_map/ppermute | solution.py:56
  84.1 1.5 collective-permute-done.8.b
  85.6 3.6 %collective-permute-done.9.c = f32[264,128]{1,0:T(8,128)S(1)} collective-permute-done((f32[264,128]{1,0:T(8,128)S(1)}, f32[264,128]{1,0:T(8,128)S(1)}, u32[]{:S(2)}, u32[]{:S(2)}) %collective-permute-start.9) | collective-permute-done | bytes 135200 | tf_op jit(solution)/shard_map/ppermute | solution.py:56
  89.9 2.0 shard_map.78
  91.8 1.7 collective-permute-start.11
  95.9 3.5 %collective-permute-done.12 = f32[264,128]{1,0:T(8,128)S(1)} collective-permute-done((f32[264,128]{1,0:T(8,128)}, f32[264,128]{1,0:T(8,128)S(1)}, u32[]{:S(2)}, u32[]{:S(2)}) %collective-permute-start.12) | collective-permute-done | bytes 135200 | tf_op jit(solution)/shard_map/ppermute | solution.py:40
  102.3 2.0 collective-permute-start.14
  104.3 7.0 %collective-permute-done.15.left = f32[4,264,128]{2,1,0:T(8,128)S(1)} collective-permute-done((f32[4,264,128]{2,1,0:T(8,128)S(1)}, f32[4,264,128]{2,1,0:T(8,128)S(1)}, u32[]{:S(2)}, u32[]{:S(2)}) %collective-permute-start.15) | collective-permute-done | bytes 540704 | tf_op jit(solution)/shard_map/ppermute | solution.py:40
  111.4 2.7 %collective-permute-start.17 = (f32[2,264,128]{2,1,0:T(8,128)S(1)}, f32[2,264,128]{2,1,0:T(8,128)S(1)}, u32[]{:S(2)}, u32[]{:S(2)}) collective-permute-start(f32[2,264,128]{2,1,0:T(8,128)S(1)} %slice.151), channel_id=1, source_target_pairs={{0,24},{1,97},{2,26},{3,99},{4,28},{5,101},{6,30},{7,103},{8,0},{9... | collective-permute-start | bytes 811016 | tf_op jit(solution)/shard_map/ppermute | solution.py:40
  114.2 3.7 %collective-permute-done.16.far_left = f32[2,264,128]{2,1,0:T(8,128)S(1)} collective-permute-done((f32[2,264,128]{2,1,0:T(8,128)S(1)}, f32[2,264,128]{2,1,0:T(8,128)S(1)}, u32[]{:S(2)}, u32[]{:S(2)}) %collective-permute-start.16) | collective-permute-done | bytes 270368 | tf_op jit(solution)/shard_map/ppermute | solution.py:40
  117.9 4.1 %shard_map.79 = (f32[4,264,128]{2,1,0:T(8,128)S(1)}, f32[4,264,128]{2,1,0:T(8,128)S(1)}) custom-call(s32[144]{0:T(256)S(1)} %get-tuple-element.24.list_ref, f32[4]{0:T(128)S(1)} %reshape.205.lc_ref, f32[4,264,128]{2,1,0:T(8,128)S(1)} %pad_maximum_fusion.1.line, f32[4,264,128]{2,1,0:T(8,128)S(1)} %collective-permute-done.14.right, ...), custom_call_target="tpu_custom_call" | custom-call | flops 4000000000 | bytes 12000000 | tf_op jit(solution)/shard_map/pallas_call | solution.py:398
  122.0 6.8 %collective-permute-start.18 = (f32[4,264,128]{2,1,0:T(8,128)S(1)}, f32[4,264,128]{2,1,0:T(8,128)S(1)}, u32[]{:S(2)}, u32[]{:S(2)}) collective-permute-start(f32[4,264,128]{2,1,0:T(8,128)S(1)} %get-tuple-element.31), channel_id=1, source_target_pairs={{0,1},{1,0},{2,3},{3,2},{4,5},{5,4},{6,7},{7,6},{8,9},{9,8},{10,11... | collective-permute-start | bytes 1622024 | tf_op jit(solution)/shard_map/ppermute | solution.py:60
  128.8 1.6 collective-permute-done.18
  131.0 2.7 %collective-permute-start.21 = (f32[264,128]{1,0:T(8,128)S(1)}, f32[264,128]{1,0:T(8,128)S(1)}, u32[]{:S(2)}, u32[]{:S(2)}) collective-permute-start(f32[264,128]{1,0:T(8,128)S(1)} %get-tuple-element.50), channel_id=1, source_target_pairs={{0,6},{2,0},{4,2},{6,4},{1,7},{3,1},{5,3},{7,5},{8,14},{10,8},{12,... | collective-permute-start | bytes 405512 | tf_op jit(solution)/shard_map/ppermute | solution.py:56
  133.7 3.8 %collective-permute-done.19.b = f32[264,128]{1,0:T(8,128)} collective-permute-done((f32[264,128]{1,0:T(8,128)S(1)}, f32[264,128]{1,0:T(8,128)}, u32[]{:S(2)}, u32[]{:S(2)}) %collective-permute-start.19) | collective-permute-done | bytes 135200 | tf_op jit(solution)/shard_map/ppermute | solution.py:56
  137.5 3.0 %collective-permute-done.20.c = f32[264,128]{1,0:T(8,128)} collective-permute-done((f32[264,128]{1,0:T(8,128)S(1)}, f32[264,128]{1,0:T(8,128)}, u32[]{:S(2)}, u32[]{:S(2)}) %collective-permute-start.20) | collective-permute-done | bytes 135200 | tf_op jit(solution)/shard_map/ppermute | solution.py:56
  141.1 2.1 %shard_map.80 = (f32[264,128]{1,0:T(8,128)}, f32[256,128]{1,0:T(8,128)}, f32[256,128]{1,0:T(8,128)}, f32[128,128]{1,0:T(8,128)}) custom-call(f32[264,128]{1,0:T(8,128)} %get-tuple-element.53.a, f32[264,128]{1,0:T(8,128)} %collective-permute-done.19.b, f32[264,128]{1,0:T(8,128)} %collective-permute-done.20.c, f32[264,128]{1,0:T(8,128)} %copy-done.10, ...), custom_call_target="tpu_custom_call" | custom-call | flops 4000000 | bytes 2000000 | tf_op jit(solution)/shard_map/pallas_call | solution.py:359
  144.8 2.8 %collective-permute-done.22 = f32[264,128]{1,0:T(8,128)S(1)} collective-permute-done((f32[264,128]{1,0:T(8,128)}, f32[264,128]{1,0:T(8,128)S(1)}, u32[]{:S(2)}, u32[]{:S(2)}) %collective-permute-start.22) | collective-permute-done | bytes 135200 | tf_op jit(solution)/shard_map/ppermute | solution.py:40
  147.6 2.4 %collective-permute-done.23 = f32[264,128]{1,0:T(8,128)S(1)} collective-permute-done((f32[264,128]{1,0:T(8,128)}, f32[264,128]{1,0:T(8,128)S(1)}, u32[]{:S(2)}, u32[]{:S(2)}) %collective-permute-start.23) | collective-permute-done | bytes 135200 | tf_op jit(solution)/shard_map/ppermute | solution.py:40
  150.0 1.4 collective-permute-done.24
  152.8 2.4 %collective-permute-start.25 = (f32[4,264,128]{2,1,0:T(8,128)S(1)}, f32[4,264,128]{2,1,0:T(8,128)S(1)}, u32[]{:S(2)}, u32[]{:S(2)}) collective-permute-start(f32[4,264,128]{2,1,0:T(8,128)S(1)} %pad_maximum_fusion.2.line), channel_id=1, source_target_pairs={{0,24},{1,97},{2,26},{3,99},{4,28},{5,101},{6,30},{7,103},{8,0},{9... | collective-permute-start | bytes 1622024 | tf_op jit(solution)/shard_map/ppermute | solution.py:40
  155.2 7.0 %collective-permute-done.26.left = f32[4,264,128]{2,1,0:T(8,128)S(1)} collective-permute-done((f32[4,264,128]{2,1,0:T(8,128)S(1)}, f32[4,264,128]{2,1,0:T(8,128)S(1)}, u32[]{:S(2)}, u32[]{:S(2)}) %collective-permute-start.26) | collective-permute-done | bytes 540704 | tf_op jit(solution)/shard_map/ppermute | solution.py:40
  162.4 2.7 %collective-permute-start.28 = (f32[2,264,128]{2,1,0:T(8,128)S(1)}, f32[2,264,128]{2,1,0:T(8,128)S(1)}, u32[]{:S(2)}, u32[]{:S(2)}) collective-permute-start(f32[2,264,128]{2,1,0:T(8,128)S(1)} %slice.157), channel_id=1, source_target_pairs={{0,24},{1,97},{2,26},{3,99},{4,28},{5,101},{6,30},{7,103},{8,0},{9... | collective-permute-start | bytes 811016 | tf_op jit(solution)/shard_map/ppermute | solution.py:40
  165.1 4.0 %collective-permute-done.27.far_left = f32[2,264,128]{2,1,0:T(8,128)S(1)} collective-permute-done((f32[2,264,128]{2,1,0:T(8,128)S(1)}, f32[2,264,128]{2,1,0:T(8,128)S(1)}, u32[]{:S(2)}, u32[]{:S(2)}) %collective-permute-start.27) | collective-permute-done | bytes 270368 | tf_op jit(solution)/shard_map/ppermute | solution.py:40
  169.1 4.1 %shard_map.81 = (f32[4,264,128]{2,1,0:T(8,128)S(1)}, f32[4,264,128]{2,1,0:T(8,128)S(1)}) custom-call(s32[144]{0:T(256)S(1)} %get-tuple-element.24.list_ref, f32[4]{0:T(128)S(1)} %reshape.205.lc_ref, f32[4,264,128]{2,1,0:T(8,128)S(1)} %pad_maximum_fusion.2.line, f32[4,264,128]{2,1,0:T(8,128)S(1)} %collective-permute-done.25.right, ...), custom_call_target="tpu_custom_call" | custom-call | flops 4000000000 | bytes 12000000 | tf_op jit(solution)/shard_map/pallas_call | solution.py:398
  173.2 4.6 %collective-permute-start.29 = (f32[4,264,128]{2,1,0:T(8,128)S(1)}, f32[4,264,128]{2,1,0:T(8,128)S(1)}, u32[]{:S(2)}, u32[]{:S(2)}) collective-permute-start(f32[4,264,128]{2,1,0:T(8,128)S(1)} %get-tuple-element.35), channel_id=1, source_target_pairs={{0,1},{1,0},{2,3},{3,2},{4,5},{5,4},{6,7},{7,6},{8,9},{9,8},{10,11... | collective-permute-start | bytes 1622024 | tf_op jit(solution)/shard_map/ppermute | solution.py:60
  177.8 1.6 collective-permute-done.29
  180.1 2.7 %collective-permute-start.32 = (f32[264,128]{1,0:T(8,128)S(1)}, f32[264,128]{1,0:T(8,128)S(1)}, u32[]{:S(2)}, u32[]{:S(2)}) collective-permute-start(f32[264,128]{1,0:T(8,128)S(1)} %get-tuple-element.46), channel_id=1, source_target_pairs={{0,6},{2,0},{4,2},{6,4},{1,7},{3,1},{5,3},{7,5},{8,14},{10,8},{12,... | collective-permute-start | bytes 405512 | tf_op jit(solution)/shard_map/ppermute | solution.py:56
  182.8 3.7 %collective-permute-done.30.b = f32[264,128]{1,0:T(8,128)S(1)} collective-permute-done((f32[264,128]{1,0:T(8,128)S(1)}, f32[264,128]{1,0:T(8,128)S(1)}, u32[]{:S(2)}, u32[]{:S(2)}) %collective-permute-start.30) | collective-permute-done | bytes 135200 | tf_op jit(solution)/shard_map/ppermute | solution.py:56
  186.5 3.0 %collective-permute-done.31.c = f32[264,128]{1,0:T(8,128)S(1)} collective-permute-done((f32[264,128]{1,0:T(8,128)S(1)}, f32[264,128]{1,0:T(8,128)S(1)}, u32[]{:S(2)}, u32[]{:S(2)}) %collective-permute-start.31) | collective-permute-done | bytes 135200 | tf_op jit(solution)/shard_map/ppermute | solution.py:56
  190.2 2.4 %shard_map.82 = (f32[8,128]{1,0:T(8,128)}, f32[256,128]{1,0:T(8,128)}, f32[256,128]{1,0:T(8,128)}, f32[256,128]{1,0:T(8,128)}, f32[256,128]{1,0:T(8,128)}, /*index=5*/f32[256,128]{1,0:T(8,128)}, f32[128,128]{1,0:T(8,128)}) custom-call(f32[264,128]{1,0:T(8,128)} %get-tuple-element.49.a, f32[264,128]{1,0:T(8,128)} %copy-done.7, f32[264,128]{1,0:T(8,128)} %copy-done.8, ...), custom_call_target="tpu_custom_call" | custom-call | flops 4000000 | bytes 2000000 | tf_op jit(solution)/shard_map/pallas_call | solution.py:359
  193.3 16.5 %all_to_all.15 = f32[128,1,128]{2,1,0:T(1,128)S(1)} all-to-all(f32[128,1,128]{2,1,0:T(1,128)S(1)} %broadcast_in_dim.28), channel_id=1, replica_groups=mesh['row_0'=4,'row_1'=4,'col_0'=4,'col_1'=2] {'row_0','row_1','col_0','..., dimensions={0} | all-to-all | bytes 131072 | tf_op jit(solution)/shard_map/all_to_all | solution.py:436
  210.3 2.0 shard_map.83
  (102 shorter events, 26.5 us)
Async XLA Ops:
  2.3 8.7 %collective-permute-start.1 = (f32[136,512]{1,0:T(8,128)S(1)}, f32[136,512]{1,0:T(8,128)S(1)}, u32[]{:S(2)}, u32[]{:S(2)}) collective-permute-start(f32[136,512]{1,0:T(8,128)S(1)} %get-tuple-element.59), channel_id=1, source_target_pairs={{0,64},{1,17},{2,66},{3,19},{4,68},{5,21},{6,70},{7,23},{8,72},{9,... | collective-permute-start | bytes 835592 | tf_op jit(solution)/shard_map/ppermute | solution.py:40
  6.8 7.2 %collective-permute-start.2 = (f32[136,512]{1,0:T(8,128)S(1)}, f32[136,512]{1,0:T(8,128)S(1)}, u32[]{:S(2)}, u32[]{:S(2)}) collective-permute-start(f32[136,512]{1,0:T(8,128)S(1)} %get-tuple-element.59), channel_id=1, source_target_pairs={{0,32},{1,9},{2,34},{3,11},{4,36},{5,13},{6,38},{7,15},{8,40},{9,1... | collective-permute-start | bytes 835592 | tf_op jit(solution)/shard_map/ppermute | solution.py:40
  7.6 7.1 %collective-permute-start = (f32[136,512]{1,0:T(8,128)S(1)}, f32[136,512]{1,0:T(8,128)S(1)}, u32[]{:S(2)}, u32[]{:S(2)}) collective-permute-start(f32[136,512]{1,0:T(8,128)S(1)} %get-tuple-element.59), channel_id=1, source_target_pairs={{0,96},{1,25},{2,98},{3,27},{4,100},{5,29},{6,102},{7,31},{8,104},... | collective-permute-start | bytes 835592 | tf_op jit(solution)/shard_map/ppermute | solution.py:40
  14.6 2.9 %copy-start.15 = (s32[1,1,8,3]{2,1,3,0:T(1,128)S(1)}, s32[1,1,8,3]{2,1,3,0:T(1,128)}, u32[]{:S(2)}) copy-start(s32[1,1,8,3]{2,1,3,0:T(1,128)} %param.11) | copy-start | bytes 292
  14.6 13.2 %copy-start.6 = (f32[64,512]{1,0:T(8,128)S(1)}, f32[64,512]{1,0:T(8,128)}, u32[]{:S(2)}) copy-start(f32[64,512]{1,0:T(8,128)} %param.7) | copy-start | bytes 393220
  14.7 23.7 %copy-start = (f32[4,136,512]{2,1,0:T(8,128)}, f32[4,136,512]{2,1,0:T(8,128)S(1)}, u32[]{:S(2)}) copy-start(f32[4,136,512]{2,1,0:T(8,128)S(1)} %pad_maximum_fusion.line) | copy-start | bytes 3342340
  14.8 28.3 %collective-permute-start.4 = (f32[4,136,512]{2,1,0:T(8,128)S(1)}, f32[4,136,512]{2,1,0:T(8,128)S(1)}, u32[]{:S(2)}, u32[]{:S(2)}) collective-permute-start(f32[4,136,512]{2,1,0:T(8,128)S(1)} %pad_maximum_fusion.line), channel_id=1, source_target_pairs={{0,8},{1,33},{2,10},{3,35},{4,12},{5,37},{6,14},{7,39},{8,16},{9,4... | collective-permute-start | bytes 3342344 | tf_op jit(solution)/shard_map/ppermute | solution.py:40
  16.0 28.2 %collective-permute-start.3 = (f32[4,136,512]{2,1,0:T(8,128)S(1)}, f32[4,136,512]{2,1,0:T(8,128)}, u32[]{:S(2)}, u32[]{:S(2)}) collective-permute-start(f32[4,136,512]{2,1,0:T(8,128)S(1)} %pad_maximum_fusion.line), channel_id=1, source_target_pairs={{0,24},{1,97},{2,26},{3,99},{4,28},{5,101},{6,30},{7,103},{8,0},{9... | collective-permute-start | bytes 3342344 | tf_op jit(solution)/shard_map/ppermute | solution.py:40
  18.2 19.0 %all-to-all-start = ((s32[128,1,128]{2,1,0:T(1,128)}), s32[128,1,128]{2,1,0:T(1,128)S(1)}, u32[]{:S(2)}, u32[]{:S(2)}) async-start(s32[128,1,128]{2,1,0:T(1,128)} %broadcast_in_dim.10), calls=%async_computation | async-start | bytes 131072 | tf_op jit(solution)/shard_map/all_to_all | solution.py:436
  38.4 4.5 %copy-start.16 = (f32[2,2]{1,0:T(2,128)S(1)}, f32[2,2]{1,0:T(2,128)}, u32[]{:S(2)}) copy-start(f32[2,2]{1,0:T(2,128)} %param.10) | copy-start | bytes 52
  38.4 21.0 %all-to-all-start.1 = ((f32[8,72,512]{2,1,0:T(8,128)}), f32[8,72,512]{2,1,0:T(8,128)S(1)}, u32[]{:S(2)}, u32[]{:S(2)}) async-start(f32[8,72,512]{2,1,0:T(8,128)} %broadcast_in_dim.12), calls=%async_computation.1 | async-start | bytes 2359296 | tf_op jit(solution)/shard_map/all_to_all | solution.py:446
  43.0 4.7 %copy-start.17 = (s32[1,136]{1,0:T(1,128)S(1)}, s32[1,136]{1,0:T(1,128)}, u32[]{:S(2)}) copy-start(s32[1,136]{1,0:T(1,128)} %constant.49.clone.1) | copy-start | bytes 1636
  43.0 2.3 %copy-start.2 = (f32[4,136,512]{2,1,0:T(8,128)}, f32[4,136,512]{2,1,0:T(8,128)S(1)}, u32[]{:S(2)}) copy-start(f32[4,136,512]{2,1,0:T(8,128)S(1)} %collective-permute-done.4.left) | copy-start | bytes 3342340
  43.9 15.6 %collective-permute-start.5 = (f32[2,136,512]{2,1,0:T(8,128)}, f32[2,136,512]{2,1,0:T(8,128)}, u32[]{:S(2)}, u32[]{:S(2)}) collective-permute-start(f32[2,136,512]{2,1,0:T(8,128)} %slice.144), channel_id=1, source_target_pairs={{0,8},{1,33},{2,10},{3,35},{4,12},{5,37},{6,14},{7,39},{8,16},{9,4... | collective-permute-start | bytes 1671176 | tf_op jit(solution)/shard_map/ppermute | solution.py:40
  45.3 14.2 %collective-permute-start.6 = (f32[2,136,512]{2,1,0:T(8,128)S(1)}, f32[2,136,512]{2,1,0:T(8,128)S(1)}, u32[]{:S(2)}, u32[]{:S(2)}) collective-permute-start(f32[2,136,512]{2,1,0:T(8,128)S(1)} %slice.145), channel_id=1, source_target_pairs={{0,24},{1,97},{2,26},{3,99},{4,28},{5,101},{6,30},{7,103},{8,0},{9... | collective-permute-start | bytes 1671176 | tf_op jit(solution)/shard_map/ppermute | solution.py:40
  60.3 1.2 copy-start.1
  61.5 1.2 copy-start.3
  62.8 1.1 copy-start.5
  72.7 8.1 %copy-start.14 = (f32[512]{0:T(512)S(1)}, f32[512]{0:T(512)}, u32[]{:S(2)}) copy-start(f32[512]{0:T(512)} %param.9) | copy-start | bytes 6148
  72.7 5.9 %collective-permute-start.7 = (f32[4,264,128]{2,1,0:T(8,128)S(1)}, f32[4,264,128]{2,1,0:T(8,128)S(1)}, u32[]{:S(2)}, u32[]{:S(2)}) collective-permute-start(f32[4,264,128]{2,1,0:T(8,128)S(1)} %get-tuple-element.26), channel_id=1, source_target_pairs={{0,1},{1,0},{2,3},{3,2},{4,5},{5,4},{6,7},{7,6},{8,9},{9,8},{10,11... | collective-permute-start | bytes 1622024 | tf_op jit(solution)/shard_map/ppermute | solution.py:60
  79.3 4.8 %collective-permute-start.10 = (f32[264,128]{1,0:T(8,128)S(1)}, f32[264,128]{1,0:T(8,128)S(1)}, u32[]{:S(2)}, u32[]{:S(2)}) collective-permute-start(f32[264,128]{1,0:T(8,128)S(1)} %get-tuple-element.54), channel_id=1, source_target_pairs={{0,6},{2,0},{4,2},{6,4},{1,7},{3,1},{5,3},{7,5},{8,14},{10,8},{12,... | collective-permute-start | bytes 405512 | tf_op jit(solution)/shard_map/ppermute | solution.py:56
  79.3 6.3 %collective-permute-start.8 = (f32[264,128]{1,0:T(8,128)S(1)}, f32[264,128]{1,0:T(8,128)S(1)}, u32[]{:S(2)}, u32[]{:S(2)}) collective-permute-start(f32[264,128]{1,0:T(8,128)S(1)} %get-tuple-element.56), channel_id=1, source_target_pairs={{0,4},{2,6},{4,0},{6,2},{1,5},{3,7},{5,1},{7,3},{8,12},{10,14},{12... | collective-permute-start | bytes 405512 | tf_op jit(solution)/shard_map/ppermute | solution.py:56
  79.3 9.9 %collective-permute-start.9 = (f32[264,128]{1,0:T(8,128)S(1)}, f32[264,128]{1,0:T(8,128)S(1)}, u32[]{:S(2)}, u32[]{:S(2)}) collective-permute-start(f32[264,128]{1,0:T(8,128)S(1)} %get-tuple-element.55), channel_id=1, source_target_pairs={{0,2},{2,4},{4,6},{6,0},{1,3},{3,5},{5,7},{7,1},{8,10},{10,12},{12... | collective-permute-start | bytes 405512 | tf_op jit(solution)/shard_map/ppermute | solution.py:56
  84.1 5.1 %copy-start.11 = (f32[264,128]{1,0:T(8,128)}, f32[264,128]{1,0:T(8,128)S(1)}, u32[]{:S(2)}) copy-start(f32[264,128]{1,0:T(8,128)S(1)} %collective-permute-done.10.d) | copy-start | bytes 405508
  85.6 3.6 %copy-start.12 = (f32[264,128]{1,0:T(8,128)}, f32[264,128]{1,0:T(8,128)S(1)}, u32[]{:S(2)}) copy-start(f32[264,128]{1,0:T(8,128)S(1)} %collective-permute-done.8.b) | copy-start | bytes 405508
  91.8 4.1 %collective-permute-start.11 = (f32[264,128]{1,0:T(8,128)}, f32[264,128]{1,0:T(8,128)S(1)}, u32[]{:S(2)}, u32[]{:S(2)}) collective-permute-start(f32[264,128]{1,0:T(8,128)} %get-tuple-element.27.w_ref.w0_ref), channel_id=1, source_target_pairs={{0,96},{1,25},{2,98},{3,27},{4,100},{5,29},{6,102},{7,31},{8,104},... | collective-permute-start | bytes 405512 | tf_op jit(solution)/shard_map/ppermute | solution.py:40
  93.5 5.9 %collective-permute-start.12 = (f32[264,128]{1,0:T(8,128)}, f32[264,128]{1,0:T(8,128)S(1)}, u32[]{:S(2)}, u32[]{:S(2)}) collective-permute-start(f32[264,128]{1,0:T(8,128)} %get-tuple-element.27.w_ref.w0_ref), channel_id=1, source_target_pairs={{0,64},{1,17},{2,66},{3,19},{4,68},{5,21},{6,70},{7,23},{8,72},{9,... | collective-permute-start | bytes 405512 | tf_op jit(solution)/shard_map/ppermute | solution.py:40
  94.5 6.0 %collective-permute-start.13 = (f32[264,128]{1,0:T(8,128)}, f32[264,128]{1,0:T(8,128)S(1)}, u32[]{:S(2)}, u32[]{:S(2)}) collective-permute-start(f32[264,128]{1,0:T(8,128)} %get-tuple-element.27.w_ref.w0_ref), channel_id=1, source_target_pairs={{0,32},{1,9},{2,34},{3,11},{4,36},{5,13},{6,38},{7,15},{8,40},{9,1... | collective-permute-start | bytes 405512 | tf_op jit(solution)/shard_map/ppermute | solution.py:40
  101.5 9.8 %collective-permute-start.15 = (f32[4,264,128]{2,1,0:T(8,128)S(1)}, f32[4,264,128]{2,1,0:T(8,128)S(1)}, u32[]{:S(2)}, u32[]{:S(2)}) collective-permute-start(f32[4,264,128]{2,1,0:T(8,128)S(1)} %pad_maximum_fusion.1.line), channel_id=1, source_target_pairs={{0,8},{1,33},{2,10},{3,35},{4,12},{5,37},{6,14},{7,39},{8,16},{9,4... | collective-permute-start | bytes 1622024 | tf_op jit(solution)/shard_map/ppermute | solution.py:40
  102.3 9.1 %collective-permute-start.14 = (f32[4,264,128]{2,1,0:T(8,128)S(1)}, f32[4,264,128]{2,1,0:T(8,128)S(1)}, u32[]{:S(2)}, u32[]{:S(2)}) collective-permute-start(f32[4,264,128]{2,1,0:T(8,128)S(1)} %pad_maximum_fusion.1.line), channel_id=1, source_target_pairs={{0,24},{1,97},{2,26},{3,99},{4,28},{5,101},{6,30},{7,103},{8,0},{9... | collective-permute-start | bytes 1622024 | tf_op jit(solution)/shard_map/ppermute | solution.py:40
  111.3 6.6 %collective-permute-start.16 = (f32[2,264,128]{2,1,0:T(8,128)S(1)}, f32[2,264,128]{2,1,0:T(8,128)S(1)}, u32[]{:S(2)}, u32[]{:S(2)}) collective-permute-start(f32[2,264,128]{2,1,0:T(8,128)S(1)} %slice.150), channel_id=1, source_target_pairs={{0,8},{1,33},{2,10},{3,35},{4,12},{5,37},{6,14},{7,39},{8,16},{9,4... | collective-permute-start | bytes 811016 | tf_op jit(solution)/shard_map/ppermute | solution.py:40
  111.4 6.5 %collective-permute-start.17 = (f32[2,264,128]{2,1,0:T(8,128)S(1)}, f32[2,264,128]{2,1,0:T(8,128)S(1)}, u32[]{:S(2)}, u32[]{:S(2)}) collective-permute-start(f32[2,264,128]{2,1,0:T(8,128)S(1)} %slice.151), channel_id=1, source_target_pairs={{0,24},{1,97},{2,26},{3,99},{4,28},{5,101},{6,30},{7,103},{8,0},{9... | collective-permute-start | bytes 811016 | tf_op jit(solution)/shard_map/ppermute | solution.py:40
  122.0 8.3 %collective-permute-start.18 = (f32[4,264,128]{2,1,0:T(8,128)S(1)}, f32[4,264,128]{2,1,0:T(8,128)S(1)}, u32[]{:S(2)}, u32[]{:S(2)}) collective-permute-start(f32[4,264,128]{2,1,0:T(8,128)S(1)} %get-tuple-element.31), channel_id=1, source_target_pairs={{0,1},{1,0},{2,3},{3,2},{4,5},{5,4},{6,7},{7,6},{8,9},{9,8},{10,11... | collective-permute-start | bytes 1622024 | tf_op jit(solution)/shard_map/ppermute | solution.py:60
  131.0 6.5 %collective-permute-start.19 = (f32[264,128]{1,0:T(8,128)S(1)}, f32[264,128]{1,0:T(8,128)}, u32[]{:S(2)}, u32[]{:S(2)}) collective-permute-start(f32[264,128]{1,0:T(8,128)S(1)} %get-tuple-element.52), channel_id=1, source_target_pairs={{0,4},{2,6},{4,0},{6,2},{1,5},{3,7},{5,1},{7,3},{8,12},{10,14},{12... | collective-permute-start | bytes 405512 | tf_op jit(solution)/shard_map/ppermute | solution.py:56
  131.0 9.5 %collective-permute-start.20 = (f32[264,128]{1,0:T(8,128)S(1)}, f32[264,128]{1,0:T(8,128)}, u32[]{:S(2)}, u32[]{:S(2)}) collective-permute-start(f32[264,128]{1,0:T(8,128)S(1)} %get-tuple-element.51), channel_id=1, source_target_pairs={{0,2},{2,4},{4,6},{6,0},{1,3},{3,5},{5,7},{7,1},{8,10},{10,12},{12... | collective-permute-start | bytes 405512 | tf_op jit(solution)/shard_map/ppermute | solution.py:56
  131.0 9.5 %collective-permute-start.21 = (f32[264,128]{1,0:T(8,128)S(1)}, f32[264,128]{1,0:T(8,128)S(1)}, u32[]{:S(2)}, u32[]{:S(2)}) collective-permute-start(f32[264,128]{1,0:T(8,128)S(1)} %get-tuple-element.50), channel_id=1, source_target_pairs={{0,6},{2,0},{4,2},{6,4},{1,7},{3,1},{5,3},{7,5},{8,14},{10,8},{12,... | collective-permute-start | bytes 405512 | tf_op jit(solution)/shard_map/ppermute | solution.py:56
  143.3 4.4 %collective-permute-start.22 = (f32[264,128]{1,0:T(8,128)}, f32[264,128]{1,0:T(8,128)S(1)}, u32[]{:S(2)}, u32[]{:S(2)}) collective-permute-start(f32[264,128]{1,0:T(8,128)} %get-tuple-element.33.w1_ref), channel_id=1, source_target_pairs={{0,96},{1,25},{2,98},{3,27},{4,100},{5,29},{6,102},{7,31},{8,104},... | collective-permute-start | bytes 405512 | tf_op jit(solution)/shard_map/ppermute | solution.py:40
  144.2 5.9 %collective-permute-start.23 = (f32[264,128]{1,0:T(8,128)}, f32[264,128]{1,0:T(8,128)S(1)}, u32[]{:S(2)}, u32[]{:S(2)}) collective-permute-start(f32[264,128]{1,0:T(8,128)} %get-tuple-element.33.w1_ref), channel_id=1, source_target_pairs={{0,64},{1,17},{2,66},{3,19},{4,68},{5,21},{6,70},{7,23},{8,72},{9,... | collective-permute-start | bytes 405512 | tf_op jit(solution)/shard_map/ppermute | solution.py:40
  144.2 7.3 %collective-permute-start.24 = (f32[264,128]{1,0:T(8,128)}, f32[264,128]{1,0:T(8,128)S(1)}, u32[]{:S(2)}, u32[]{:S(2)}) collective-permute-start(f32[264,128]{1,0:T(8,128)} %get-tuple-element.33.w1_ref), channel_id=1, source_target_pairs={{0,32},{1,9},{2,34},{3,11},{4,36},{5,13},{6,38},{7,15},{8,40},{9,1... | collective-permute-start | bytes 405512 | tf_op jit(solution)/shard_map/ppermute | solution.py:40
  152.4 9.8 %collective-permute-start.26 = (f32[4,264,128]{2,1,0:T(8,128)S(1)}, f32[4,264,128]{2,1,0:T(8,128)S(1)}, u32[]{:S(2)}, u32[]{:S(2)}) collective-permute-start(f32[4,264,128]{2,1,0:T(8,128)S(1)} %pad_maximum_fusion.2.line), channel_id=1, source_target_pairs={{0,8},{1,33},{2,10},{3,35},{4,12},{5,37},{6,14},{7,39},{8,16},{9,4... | collective-permute-start | bytes 1622024 | tf_op jit(solution)/shard_map/ppermute | solution.py:40
  152.8 9.5 %collective-permute-start.25 = (f32[4,264,128]{2,1,0:T(8,128)S(1)}, f32[4,264,128]{2,1,0:T(8,128)S(1)}, u32[]{:S(2)}, u32[]{:S(2)}) collective-permute-start(f32[4,264,128]{2,1,0:T(8,128)S(1)} %pad_maximum_fusion.2.line), channel_id=1, source_target_pairs={{0,24},{1,97},{2,26},{3,99},{4,28},{5,101},{6,30},{7,103},{8,0},{9... | collective-permute-start | bytes 1622024 | tf_op jit(solution)/shard_map/ppermute | solution.py:40
  162.2 6.9 %collective-permute-start.27 = (f32[2,264,128]{2,1,0:T(8,128)S(1)}, f32[2,264,128]{2,1,0:T(8,128)S(1)}, u32[]{:S(2)}, u32[]{:S(2)}) collective-permute-start(f32[2,264,128]{2,1,0:T(8,128)S(1)} %slice.156), channel_id=1, source_target_pairs={{0,8},{1,33},{2,10},{3,35},{4,12},{5,37},{6,14},{7,39},{8,16},{9,4... | collective-permute-start | bytes 811016 | tf_op jit(solution)/shard_map/ppermute | solution.py:40
  162.4 6.8 %collective-permute-start.28 = (f32[2,264,128]{2,1,0:T(8,128)S(1)}, f32[2,264,128]{2,1,0:T(8,128)S(1)}, u32[]{:S(2)}, u32[]{:S(2)}) collective-permute-start(f32[2,264,128]{2,1,0:T(8,128)S(1)} %slice.157), channel_id=1, source_target_pairs={{0,24},{1,97},{2,26},{3,99},{4,28},{5,101},{6,30},{7,103},{8,0},{9... | collective-permute-start | bytes 811016 | tf_op jit(solution)/shard_map/ppermute | solution.py:40
  173.2 6.2 %collective-permute-start.29 = (f32[4,264,128]{2,1,0:T(8,128)S(1)}, f32[4,264,128]{2,1,0:T(8,128)S(1)}, u32[]{:S(2)}, u32[]{:S(2)}) collective-permute-start(f32[4,264,128]{2,1,0:T(8,128)S(1)} %get-tuple-element.35), channel_id=1, source_target_pairs={{0,1},{1,0},{2,3},{3,2},{4,5},{5,4},{6,7},{7,6},{8,9},{9,8},{10,11... | collective-permute-start | bytes 1622024 | tf_op jit(solution)/shard_map/ppermute | solution.py:60
  180.1 6.3 %collective-permute-start.30 = (f32[264,128]{1,0:T(8,128)S(1)}, f32[264,128]{1,0:T(8,128)S(1)}, u32[]{:S(2)}, u32[]{:S(2)}) collective-permute-start(f32[264,128]{1,0:T(8,128)S(1)} %get-tuple-element.48), channel_id=1, source_target_pairs={{0,4},{2,6},{4,0},{6,2},{1,5},{3,7},{5,1},{7,3},{8,12},{10,14},{12... | collective-permute-start | bytes 405512 | tf_op jit(solution)/shard_map/ppermute | solution.py:56
  180.1 9.4 %collective-permute-start.31 = (f32[264,128]{1,0:T(8,128)S(1)}, f32[264,128]{1,0:T(8,128)S(1)}, u32[]{:S(2)}, u32[]{:S(2)}) collective-permute-start(f32[264,128]{1,0:T(8,128)S(1)} %get-tuple-element.47), channel_id=1, source_target_pairs={{0,2},{2,4},{4,6},{6,0},{1,3},{3,5},{5,7},{7,1},{8,10},{10,12},{12... | collective-permute-start | bytes 405512 | tf_op jit(solution)/shard_map/ppermute | solution.py:56
  180.1 9.4 %collective-permute-start.32 = (f32[264,128]{1,0:T(8,128)S(1)}, f32[264,128]{1,0:T(8,128)S(1)}, u32[]{:S(2)}, u32[]{:S(2)}) collective-permute-start(f32[264,128]{1,0:T(8,128)S(1)} %get-tuple-element.46), channel_id=1, source_target_pairs={{0,6},{2,0},{4,2},{6,4},{1,7},{3,1},{5,3},{7,5},{8,14},{10,8},{12,... | collective-permute-start | bytes 405512 | tf_op jit(solution)/shard_map/ppermute | solution.py:56
  186.5 3.0 %copy-start.7 = (f32[264,128]{1,0:T(8,128)}, f32[264,128]{1,0:T(8,128)S(1)}, u32[]{:S(2)}) copy-start(f32[264,128]{1,0:T(8,128)S(1)} %collective-permute-done.30.b) | copy-start | bytes 405508
  (5 other events, 3.5 us)

commit v2 on v1

v2 whole, which is shorter than its diff:
```python
import functools
import math

import jax
import jax.numpy as jnp
from jax import lax
from jax.experimental import pallas as pl
from jax.experimental.pallas import tpu as pltpu
from jax.sharding import Mesh
from jax.sharding import PartitionSpec as P

TILE = 512
X, Z, Y, C = "row_0", "row_1", "col_0", "col_1"
ALL = (X, Z, Y, C)
ROW, COL = (X, Z), (Y, C)
BODY = 256
ROWS = BODY + 8
KEPT = 32
SLOTS_OUT = 144
KAPPA = math.log2(math.e) / 12.0
F32, BF16 = jnp.float32, jnp.bfloat16


def along_row(stage, step):
    pairs = []
    for x in range(4):
        for z in range(4):
            for y in range(4):
                for c in range(2):
                    if (c == 0) == (stage == 1):
                        to = ((x + step) % 4, z)
                    else:
                        to = (x, (z + step) % 4)
                    pairs.append((((x * 4 + z) * 4 + y) * 2 + c, ((to[0] * 4 + to[1]) * 4 + y) * 2 + c))
    return pairs


def hop(a, stage, step):
    return lax.ppermute(a, ALL, along_row(stage, step))


def gather_line(block):
    far = hop(block, 1, 2)
    ahead = hop(block, 1, -1)
    behind = hop(block, 1, 1)
    return block, ahead, far, behind


def gather_plane(line):
    low, high = jnp.stack(line[0:2]), jnp.stack(line[2:4])
    left_low = hop(low, 2, 1)
    right_high = hop(high, 2, -1)
    left_high = hop(high, 2, 1)
    right_low = hop(low, 2, -1)
    far_low = hop(left_low, 2, 1)
    far_high = hop(right_high, 2, -1)
    return low, high, right_low, right_high, far_low, far_high, left_low, left_high


def gather_row(block):
    return gather_plane(gather_line(block))


def swap_core(a):
    return lax.ppermute(a, C, [(0, 1), (1, 0)])


def shift_y(a, step):
    return lax.ppermute(a, Y, [(i, (i + step) % 4) for i in range(4)])


def reduce_col(keep, other):
    got = swap_core(other)
    one, two, three = [keep[j] + got[j] for j in (1, 2, 3)]
    far = shift_y(two, 2)
    return keep, got, shift_y(one, 1)[None], shift_y(three, -1)[None], far[None]


def halves(v):
    h = v.astype(BF16).astype(F32)
    m = (v - h).astype(BF16).astype(F32)
    return h, m, v - h - m


def rows_of(values, count, width):
    at = lax.broadcasted_iota(jnp.int32, (count, width), 0)
    out = jnp.zeros((count, width), F32)
    for k, value in enumerate(values):
        out = jnp.where(at == k, value, out)
    return out


def make_tile(fin, lin, fout, lout, turned, lc_ref, e_ref, pair_ref):
    h, m, l = halves(fin)
    norms = halves(-KAPPA * jnp.sum(fin * fin, axis=0, keepdims=True))
    aug = rows_of([*norms, 1.0, 1.0, 1.0, *[1.0 - lin, lin] * 3], 16, TILE)
    hm = jnp.concatenate([h, m], axis=0).T.astype(BF16)
    hl = jnp.concatenate([h, l], axis=0).T.astype(BF16)
    au = jnp.concatenate([aug, jnp.zeros((112, TILE), F32)], axis=0).T.astype(BF16)
    left = jnp.concatenate([hm, hm, hl, au], axis=1)
    g, n, k = halves(fout * (2.0 * KAPPA))
    norms = halves(-KAPPA * jnp.sum(fout * fout, axis=0, keepdims=True))
    levels = []
    for i in range(2):
        first = jnp.where(turned, lc_ref[i, 0], lc_ref[0, i])
        second = jnp.where(turned, lc_ref[i, 1], lc_ref[1, i])
        levels.append(halves(jnp.where(lout > 0.5, second, first)))
    logs = [levels[i][j] for j in range(3) for i in range(2)]
    aug = rows_of([1.0, 1.0, 1.0, *norms, *logs], 16, TILE)
    right = jnp.concatenate([g, g, n, n, k, g, aug, jnp.zeros((112, TILE), F32)], axis=0).astype(BF16)
    e_ref[...] = jnp.dot(left, right, preferred_element_type=F32)
    total = jnp.zeros((8, TILE), F32)
    for at in range(0, TILE, 64):
        t = jnp.exp2(e_ref[at : at + 64, :])
        hi = t.astype(BF16)
        pair_ref[0, at : at + 64, :] = hi
        pair_ref[1, at : at + 64, :] = (t - hi.astype(F32)).astype(BF16)
        total = total + jnp.sum(t.reshape(8, 8, TILE), axis=0)
    return jnp.sum(total, axis=0, keepdims=True)


def add_product(xs_ref, place, pair_ref, acc_ref, k):
    x = xs_ref[place]
    both = jnp.dot(x, pair_ref[0], preferred_element_type=F32)
    low = jnp.dot(x[:64], pair_ref[1], preferred_element_type=F32)
    out = both[:64] + both[64:] + low
    for g in range(4):
        acc_ref[k, g * 64 : g * 64 + 64, :] += out[:, g * 128 : g * 128 + 128]


def split_into(xs_ref, place, lanes, value):
    hi = value.astype(BF16)
    xs_ref[place, 0:64, lanes] = hi
    xs_ref[place, 64:128, lanes] = (value - hi.astype(F32)).astype(BF16)


def unpack(entry):
    return entry & 7, (entry >> 3) & 15, ((entry >> 7) & 1) == 1, entry >> 8


def first_kernel(
    own_ref, turned_ref, lc_ref, p0, p1, p2, p3, p4, p5, p6, p7, same, across,
    keep_ref, other_ref, list_ref, store_ref, facts_ref,
    fin_ref, x_ref, xs_ref, e_ref, pair_ref, acc_ref, sems, fact_sem, load_sems,
):
    loads = []
    for q, piece in enumerate((p0, p1, p2, p3, p4, p5, p6, p7)):
        at = pl.ds(2 * q, 2)
        loads.append(pltpu.make_async_copy(piece.at[:, pl.ds(0, 72), :], fin_ref.at[at], load_sems.at[q]))
        loads.append(pltpu.make_async_copy(piece.at[:, pl.ds(72, 64), :], x_ref.at[at], load_sems.at[8 + q]))
    loads.append(pltpu.make_async_copy(same.at[:, pl.ds(0, 72), :], fin_ref.at[pl.ds(16, 4)], load_sems.at[16]))
    loads.append(pltpu.make_async_copy(across.at[:, pl.ds(0, 72), :], fin_ref.at[pl.ds(20, 4)], load_sems.at[17]))
    for load in loads:
        load.start()
    acc_ref[...] = jnp.zeros_like(acc_ref)

    n = jnp.int32(0)
    for far in (False, True):
        for slot in range(8):
            list_ref[n] = own_ref[0, slot]
            n = n + own_ref[2 if far else 1, slot]
        for k in range(8):
            for there in range(16):
                place = there if k < 4 else (there & 3) * 4 + (there >> 2)
                if (place >> 2 == 2) == far:
                    list_ref[n] = k + 8 * place + 128 + 256 * (16 + k)
                    n = n + turned_ref[k, there]
        if not far:
            near = n
    list_ref[SLOTS_OUT - 2] = near
    list_ref[SLOTS_OUT - 1] = n
    for load in loads:
        load.wait()
    facts = pltpu.make_async_copy(fin_ref, facts_ref, fact_sem)
    facts.start()
    for place in range(16):
        split_into(xs_ref, place, slice(None), x_ref[place])

    def saved(t):
        slot = t & 1
        return pltpu.make_async_copy(pair_ref.at[slot], store_ref.at[jnp.minimum(t, KEPT - 1)], sems.at[slot])

    def visit(t, carry):
        k, place, turned, block = unpack(list_ref[t])
        slot = t & 1

        @pl.when((t >= 2) & (t - 2 < KEPT))
        def _():
            saved(t - 2).wait()

        pair = pair_ref.at[slot]
        sums = make_tile(
            fin_ref[place, 0:64, :], fin_ref[place, 64:65, :], fin_ref[block, 0:64, :], fin_ref[block, 64:65, :],
            turned, lc_ref, e_ref, pair,
        )

        @pl.when(t < KEPT)
        def _():
            saved(t).start()

        add_product(xs_ref, place, pair, acc_ref, k)
        spread = jnp.concatenate([sums[:, g * 128 : g * 128 + 128] for g in range(4)] + [jnp.zeros((4, 128), F32)], axis=0)
        acc_ref[k, BODY:ROWS, :] += spread
        return carry

    lax.fori_loop(0, n, visit, jnp.int32(0))
    for back in (2, 1):

        @pl.when((n >= back) & (n - back < KEPT))
        def _():
            saved(n - back).wait()

    keep_ref[...] = acc_ref[0:4]
    other_ref[...] = acc_ref[4:8]
    facts.wait()


DEPTH = 4


def products(
    first, last, local, list_ref, lc_ref, store_ref, facts_ref,
    fin_ref, fout_ref, xs_ref, e_ref, pair_ref, acc_ref, sems, fact_sems, fill,
):
    kept = jnp.clip(KEPT, first, last)

    def loaded(t):
        slot = (t - first) & (DEPTH - 1)
        return pltpu.make_async_copy(store_ref.at[jnp.minimum(t, KEPT - 1)], pair_ref.at[slot], sems.at[slot])

    for ahead in range(DEPTH):

        @pl.when(first + ahead < kept)
        def _():
            loaded(first + ahead).start()

    fill()

    def visit(t, carry):
        k, place, _, _ = unpack(list_ref[t])
        loaded(t).wait()
        add_product(xs_ref, local(place), pair_ref.at[(t - first) & (DEPTH - 1)], acc_ref, k)

        @pl.when(t + DEPTH < kept)
        def _():
            loaded(t + DEPTH).start()

        return carry

    lax.fori_loop(first, kept, visit, jnp.int32(0))

    def visit_again(t, carry):
        k, place, turned, block = unpack(list_ref[t])
        one = pltpu.make_async_copy(facts_ref.at[place], fin_ref, fact_sems.at[0])
        two = pltpu.make_async_copy(facts_ref.at[block], fout_ref, fact_sems.at[1])
        one.start()
        two.start()
        one.wait()
        two.wait()
        pair = pair_ref.at[0]
        make_tile(fin_ref[0:64, :], fin_ref[64:65, :], fout_ref[0:64, :], fout_ref[64:65, :], turned, lc_ref, e_ref, pair)
        add_product(xs_ref, local(place), pair, acc_ref, k)
        return carry

    lax.fori_loop(kept, last, visit_again, jnp.int32(0))


def fill_from(pieces, xs_ref):
    sums = jnp.zeros((8, 128), F32)
    for q, piece in enumerate(pieces):
        for j in range(2):
            for g in range(4):
                split_into(xs_ref, 2 * q + j, slice(g * 128, g * 128 + 128), piece[j, g * 64 : g * 64 + 64, :])
            sums = sums + piece[j, BODY:ROWS, :]
    return sums


def near_kernel(
    list_ref, lc_ref, p0, p1, p2, p3, p6, p7, store_ref, facts_ref, acc_ref,
    fin_ref, fout_ref, xs_ref, e_ref, pair_ref, sems, fact_sems,
):
    def fill():
        acc_ref[...] = jnp.zeros_like(acc_ref)
        sums = fill_from((p0, p1, p2, p3, p6, p7), xs_ref)
        for k in range(8):
            acc_ref[k, BODY:ROWS, :] = sums

    products(
        jnp.int32(0), list_ref[SLOTS_OUT - 2], lambda p: jnp.where(p >= 12, p - 4, p),
        list_ref, lc_ref, store_ref, facts_ref,
        fin_ref, fout_ref, xs_ref, e_ref, pair_ref, acc_ref, sems, fact_sems, fill,
    )


def far_kernel(
    list_ref, lc_ref, p4, p5, near_ref, store_ref, facts_ref, keep_ref, other_ref,
    fin_ref, fout_ref, xs_ref, e_ref, pair_ref, acc_ref, sems, fact_sems,
):
    def fill():
        acc_ref[...] = near_ref[...]
        sums = fill_from((p4, p5), xs_ref)
        for k in range(8):
            acc_ref[k, BODY:ROWS, :] += sums

    products(
        list_ref[SLOTS_OUT - 2], list_ref[SLOTS_OUT - 1], lambda p: p - 8,
        list_ref, lc_ref, store_ref, facts_ref,
        fin_ref, fout_ref, xs_ref, e_ref, pair_ref, acc_ref, sems, fact_sems, fill,
    )
    keep_ref[...] = acc_ref[0:4]
    other_ref[...] = acc_ref[4:8]


def group(g):
    return slice(g * 64, g * 64 + 64)


def lanes(g):
    return slice(g * 128, g * 128 + 128)


def sum_rows(first, second):
    both = jnp.concatenate([first, second], axis=0)
    column = jnp.broadcast_to(jnp.sum(both, axis=1, keepdims=True), (128, 128))
    return column.T[0:8, :]


def columns_of(row):
    turned = jnp.broadcast_to(row, (128, 128)).T
    return turned[0:64], turned[64:128]


def total_of(parts, rows):
    a, b, c, d, e = (part[0, rows, :] for part in parts)
    return (a + b) + (c + d) + e


def after_first(a, b, c, d, e, r_ref, err_ref, w_ref, diag_ref):
    parts = (a, b, c, d, e)
    errors = jnp.concatenate([err_ref[:, lanes(g)] for g in range(4)], axis=0)
    diag = errors + total_of(parts, slice(BODY, BODY + 4))
    diag_ref[0:4, :] = diag
    diag_ref[4:8, :] = jnp.zeros((4, 128), F32)
    rr, rw = jnp.zeros((64, 128), F32), jnp.zeros((64, 128), F32)
    for g in range(4):
        r = r_ref[:, lanes(g)]
        w = diag[g : g + 1, :] * r + total_of(parts, group(g))
        w_ref[group(g), :] = w
        rr, rw = rr + r * r, rw + r * w
    w_ref[BODY:ROWS, :] = sum_rows(rr, rw)


def after_second(a, b, c, d, e, r_ref, w_ref, diag_ref, next_ref, r1_ref, q_ref, past_ref):
    parts = (a, b, c, d, e)
    rr0, rw0 = columns_of(total_of(parts, slice(BODY, BODY + 1)))
    alpha = rr0 / rw0
    past_ref[0:64, :] = alpha
    past_ref[64:128, :] = rr0
    rr, rw = jnp.zeros((64, 128), F32), jnp.zeros((64, 128), F32)
    for g in range(4):
        w0 = w_ref[group(g), :]
        q = diag_ref[g : g + 1, :] * w0 + total_of(parts, group(g))
        r = r_ref[:, lanes(g)] - alpha * w0
        w = w0 - alpha * q
        q_ref[group(g), :] = q
        r1_ref[group(g), :] = r
        next_ref[group(g), :] = w
        rr, rw = rr + r * r, rw + r * w
    next_ref[BODY:ROWS, :] = sum_rows(rr, rw)


def after_third(
    a, b, c, d, e, r_ref, w0_ref, diag_ref, w1_ref, r1_ref, q_ref, past_ref,
    sums_ref, r2_ref, w2_ref, s1_ref, p1_ref, x_ref, now_ref,
):
    parts = (a, b, c, d, e)
    rr1, rw1 = columns_of(total_of(parts, slice(BODY, BODY + 1)))
    alpha0, rr0 = past_ref[0:64, :], past_ref[64:128, :]
    beta = rr1 / rr0
    alpha = rr1 / (rw1 - beta * rr1 / alpha0)
    now_ref[0:64, :] = alpha
    now_ref[64:128, :] = rr1
    rr, rw = jnp.zeros((64, 128), F32), jnp.zeros((64, 128), F32)
    for g in range(4):
        w1, r1, r0 = w1_ref[group(g), :], r1_ref[group(g), :], r_ref[:, lanes(g)]
        q1 = diag_ref[g : g + 1, :] * w1 + total_of(parts, group(g))
        s = w1 + beta * w0_ref[group(g), :]
        z = q1 + beta * q_ref[group(g), :]
        p = r1 + beta * r0
        r = r1 - alpha * s
        w = w1 - alpha * z
        s1_ref[group(g), :] = s
        p1_ref[group(g), :] = p
        x_ref[group(g), :] = alpha0 * r0 + alpha * p
        r2_ref[group(g), :] = r
        w2_ref[group(g), :] = w
        rr, rw = rr + r * r, rw + r * w
    sums_ref[...] = sum_rows(rr, rw)


def finish(sums_ref, r2_ref, w2_ref, s1_ref, p1_ref, x_ref, now_ref, inc_ref, res_ref):
    rr2, rw2 = columns_of(sums_ref[...])
    alpha1, rr1 = now_ref[0:64, :], now_ref[64:128, :]
    beta = rr2 / rr1
    alpha = rr2 / (rw2 - beta * rr2 / alpha1)
    for g in range(4):
        r = r2_ref[group(g), :]
        p = r + beta * p1_ref[group(g), :]
        s = w2_ref[group(g), :] + beta * s1_ref[group(g), :]
        inc_ref[:, lanes(g)] = x_ref[group(g), :] + alpha * p
        res_ref[:, lanes(g)] = r - alpha * s


VMEM = pl.BlockSpec(memory_space=pltpu.VMEM)
SMEM = pl.BlockSpec(memory_space=pltpu.SMEM)
ANY = pl.BlockSpec(memory_space=pl.ANY)


FIRST = pl.BlockSpec((1, ROWS, 128), lambda i: (0, 0, 0))


def small_call(body, shapes, args, parts=()):
    out = [jax.ShapeDtypeStruct(s, F32) for s in shapes]
    return pl.pallas_call(
        body,
        out_shape=out,
        grid=(1,),
        in_specs=[FIRST] * len(parts) + [VMEM] * len(args),
        out_specs=[VMEM] * len(shapes),
        compiler_params=pltpu.CompilerParams(vmem_limit_bytes=12 << 20),
        cost_estimate=pl.CostEstimate(flops=4_000_000, bytes_accessed=2_000_000, transcendentals=0),
    )(*parts, *args)


PART = jax.ShapeDtypeStruct((4, ROWS, 128), F32)


ACC = jax.ShapeDtypeStruct((8, ROWS, 128), F32)


def first_operate(own, turned, log_coupling, pieces, same, across):
    return pl.pallas_call(
        first_kernel,
        out_shape=[
            PART,
            PART,
            jax.ShapeDtypeStruct((SLOTS_OUT,), jnp.int32),
            jax.ShapeDtypeStruct((KEPT, 2, TILE, TILE), BF16),
            jax.ShapeDtypeStruct((24, 72, TILE), F32),
        ],
        in_specs=[SMEM, SMEM, SMEM] + [ANY] * 10,
        out_specs=[VMEM, VMEM, SMEM, ANY, ANY],
        scratch_shapes=[
            pltpu.VMEM((24, 72, TILE), F32),
            pltpu.VMEM((16, 64, TILE), F32),
            pltpu.VMEM((16, 128, TILE), BF16),
            pltpu.VMEM((TILE, TILE), F32),
            pltpu.VMEM((2, 2, TILE, TILE), BF16),
            pltpu.VMEM((8, ROWS, 128), F32),
            pltpu.SemaphoreType.DMA((2,)),
            pltpu.SemaphoreType.DMA,
            pltpu.SemaphoreType.DMA((18,)),
        ],
        compiler_params=pltpu.CompilerParams(vmem_limit_bytes=28 << 20),
        cost_estimate=pl.CostEstimate(flops=8_000_000_000, bytes_accessed=20_000_000, transcendentals=2_000_000),
    )(own, turned, log_coupling, *pieces, same, across)


def scratch(places):
    return [
        pltpu.VMEM((72, TILE), F32),
        pltpu.VMEM((72, TILE), F32),
        pltpu.VMEM((places, 128, TILE), BF16),
        pltpu.VMEM((TILE, TILE), F32),
        pltpu.VMEM((DEPTH, 2, TILE, TILE), BF16),
    ]


SEMS = [pltpu.SemaphoreType.DMA((DEPTH,)), pltpu.SemaphoreType.DMA((2,))]


def later_operate(listed, log_coupling, pieces, store, facts):
    near = pl.pallas_call(
        near_kernel,
        out_shape=ACC,
        in_specs=[SMEM, SMEM] + [VMEM] * 6 + [ANY] * 2,
        out_specs=VMEM,
        scratch_shapes=scratch(12) + SEMS,
        compiler_params=pltpu.CompilerParams(vmem_limit_bytes=24 << 20),
        cost_estimate=pl.CostEstimate(flops=3_000_000_000, bytes_accessed=12_000_000, transcendentals=0),
    )(listed, log_coupling, *pieces[0:4], *pieces[6:8], store, facts)
    return pl.pallas_call(
        far_kernel,
        out_shape=[PART, PART],
        in_specs=[SMEM, SMEM] + [VMEM] * 3 + [ANY] * 2,
        out_specs=[VMEM, VMEM],
        scratch_shapes=scratch(4) + [pltpu.VMEM((8, ROWS, 128), F32)] + SEMS,
        compiler_params=pltpu.CompilerParams(vmem_limit_bytes=24 << 20),
        cost_estimate=pl.CostEstimate(flops=1_000_000_000, bytes_accessed=6_000_000, transcendentals=0),
    )(listed, log_coupling, *pieces[4:6], near, store, facts)


def own_entries(slots, place):
    x, z, y, c = place
    a, b = slots[:, 0], slots[:, 1]
    dx, dz = ((b >> 2) - x) & 3, ((b & 3) - z) & 3
    s1, s2 = jnp.where(c == 0, dx, dz), jnp.where(c == 0, dz, dx)
    k = ((a & 1) ^ c) * 4 + (((a >> 1) - y) & 3)
    entry = k + 8 * (s2 * 4 + s1) + 256 * (16 + k)
    far = (s2 == 2).astype(jnp.int32)
    return jnp.stack([entry, slots[:, 2] * (1 - far), slots[:, 2] * far])


def to_everyone(row, count, axes):
    copies = jnp.broadcast_to(row.reshape(1, 1, 128), (count, 1, 128))
    return lax.all_to_all(copies, axes, split_axis=0, concat_axis=0, tiled=True)


def laid(parts, height, width):
    total, at = 0.0, 0
    for part in parts:
        total = total + jnp.pad(part, ((at, height - at - part.shape[0]), (0, width - part.shape[1])))
        at += part.shape[0]
    return total


def below(rows):
    padded = [jnp.pad(row, ((0, 0), (0, TILE - row.shape[1]))) for row in rows]
    return jnp.concatenate([*padded, jnp.zeros((8 - len(rows), TILE), F32)])


def shards(innovations, obs_factors, component, obs_error, coupling, tile_slots):
    place = tuple(lax.axis_index(axis) for axis in ALL)
    x, z, y, c = place
    label = component.astype(F32)[None, :]
    slots = tile_slots[0, 0]
    lane = lax.broadcasted_iota(jnp.int32, (1, 128), 1)
    cell = slots[:, 0:1] * 16 + slots[:, 1:2]
    cells = jnp.sum(jnp.where(cell == lane, slots[:, 2:3], 0), axis=0, keepdims=True).astype(F32)
    payload = jnp.concatenate([obs_factors, below([label, cells]), innovations], axis=0)
    line = gather_line(payload)
    pieces = gather_plane(line)
    cells = laid([block[65:66, 0:128] for block in line], 4, 128)
    cells = [cells, hop(cells, 2, -1), hop(cells, 2, 2), hop(cells, 2, 1)]
    facts = laid([obs_factors, below([label]), *cells], 88, TILE)
    same = jnp.stack([facts, shift_y(facts, -1), shift_y(facts, 2), shift_y(facts, 1)])
    across = swap_core(same)
    mine = (lane == (y * 2 + c) * 16 + x * 4 + z).astype(F32)
    seen = [jnp.sum(facts[:, 72:88, 0:128] * mine[None], axis=2) for facts in (same, across)]
    turned = (jnp.concatenate(seen) > 0.5).astype(jnp.int32)
    own = own_entries(slots, place)
    log_coupling = jnp.log2(coupling)
    error_row = obs_error[None, :]

    vec, body, two = (ROWS, 128), (BODY, 128), (128, 128)
    keep, other, listed, store, kept_facts = first_operate(own, turned, log_coupling, pieces, same, across)
    parts = reduce_col(keep, other)
    w0, diag = small_call(after_first, [vec, (8, 128)], (innovations, error_row), parts)

    keep, other = later_operate(listed, log_coupling, gather_row(w0), store, kept_facts)
    parts = reduce_col(keep, other)
    w1, r1, q0, past = small_call(after_second, [vec, body, body, two], (innovations, w0, diag), parts)

    keep, other = later_operate(listed, log_coupling, gather_row(w1), store, kept_facts)
    parts = reduce_col(keep, other)
    sums, r2, w2, s1, p1, x2, now = small_call(
        after_third,
        [(8, 128), body, body, body, body, body, two],
        (innovations, w0, diag, w1, r1, q0, past),
        parts,
    )
    sums = jnp.sum(to_everyone(sums[0:1], 128, ALL), axis=0)
    increment, residual = small_call(finish, [(64, TILE)] * 2, (sums, r2, w2, s1, p1, x2, now))
    return increment, residual


def solution(mesh):
    finer = Mesh(mesh.devices.reshape(4, 4, 4, 2), ALL)
    in_specs = (P(None, ALL), P(None, ALL), P(ALL), P(ALL), P(), P(ROW, COL, None, None))
    out_specs = (P(None, ALL), P(None, ALL))
    return jax.shard_map(shards, mesh=finer, in_specs=in_specs, out_specs=out_specs, check_vma=False)
```

time: 215 us -> 179 us (0.83); the launches traced: 212 us -> 180 us
  waiting for transfers between devices: 85.6 us -> 71.4 us
  local copies, waits for them, and re-layouts: 11.8 us -> 2.64 us
  other arithmetic: 6.65 us -> 2.23 us
  blocking collectives: 16.5 us -> 13.8 us
    all_to_all x2 -> x0, waiting for transfers between devices: 20.8 us -> none  [the longest x1 11.4 us: shards(): outs = lax.all_to_all(copies, COL, split_axis=0, concat_axis=0, tiled=True)]
    all_to_all x2 -> x0, starting transfers between devices: 14.1 us -> none  [the longest x1 9.58 us: to_everyone(): return lax.all_to_all(copies, axes, split_axis=0, concat_axis=0, tiled=True)]
    ppermute x9 -> x12, waiting for transfers between devices: 21.3 us -> 28 us  [shift_y(): return lax.ppermute(a, Y, [(i, (i + step) % 4) for i in range(4)])]
    ppermute x21 -> x30, starting transfers between devices: 28.9 us -> 34.7 us  [hop(): return lax.ppermute(a, ALL, along_row(stage, step))]
    ppermute x3 -> x4, starting transfers between devices: 15.7 us -> 21.5 us  [swap_core(): return lax.ppermute(a, C, [(0, 1), (1, 0)])]
    unnamed x38 -> x7, local copies, waits for them, and re-layouts: 6.48 us -> 0.7 us
    pallas_call x6 -> x8, Pallas kernels: 16.6 us -> 13.4 us  [the longest x2 6.16 us: later_operate(): pl.pallas_call(near_kernel, out_shape=ACC, in_specs=[SMEM, SMEM] + [VMEM]...]
    ppermute x9 -> x12, starting transfers between devices: 6.83 us -> 9.89 us  [shift_y(): return lax.ppermute(a, Y, [(i, (i + step) % 4) for i in range(4)])]
  transfers between devices with their start and end apart: 35 -> 46, of which waited for: 25 -> 30; matrix products, arithmetic and copies ran while one was open for 2% -> 0% of each run, Pallas kernels for 0% -> 3%
where the time goes in v2:
time: 179 us; the launch traced here: 180 us
  waiting for transfers between devices  71.4 us (40%)
  starting transfers between devices  66.1 us (37%)
  Pallas kernels  23.3 us (13%)
  blocking collectives  13.8 us (8%)
  local copies, waits for them, and re-layouts  2.64 us (1%)
  other arithmetic  2.23 us (1%)
    ppermute x30, waiting for transfers between devices, hop(): return lax.ppermute(a, ALL, along_row(stage, step))  38.8 us
    ppermute x30, starting transfers between devices, hop(): return lax.ppermute(a, ALL, along_row(stage, step))  34.7 us
    ppermute x12, waiting for transfers between devices, shift_y(): return lax.ppermute(a, Y, [(i, (i + step) % 4) for i in range(4)])  28 us
    ppermute x4, starting transfers between devices, swap_core(): return lax.ppermute(a, C, [(0, 1), (1, 0)])  21.5 us
    all_to_all x1, blocking collectives, to_everyone(): return lax.all_to_all(copies, axes, split_axis=0, concat_axis=0, tiled=True)  13.8 us
    ppermute x12, starting transfers between devices, shift_y(): return lax.ppermute(a, Y, [(i, (i + step) % 4) for i in range(4)])  9.89 us
    pallas_call x1, Pallas kernels, first_operate(): pl.pallas_call(first_kernel, out_shape=[PART, PART, jax.ShapeDtypeStruct(...  9.88 us
    pallas_call x2, Pallas kernels, later_operate(): pl.pallas_call(near_kernel, out_shape=ACC, in_specs=[SMEM, SMEM] + [VMEM]...  6.16 us
  transfers between devices with their start and end apart: 46, of which 30 were waited for; matrix products, arithmetic and copies ran while one was open for 0% of the time, Pallas kernels for 3%

profile of v2, /device:TPU:1, one launch (start us, length us, event | category | flops | bytes accessed | tf_op | source)
XLA Modules:
  0.0 180.3 jit_solution(10594987699319550836)
XLA Ops:
  2.1 1.9 %concatenate.10 = f32[136,512]{1,0:T(8,128)S(1)} concatenate(f32[64,512]{1,0:T(8,128)} %param.7, f32[1,512]{1,0:T(1,128)S(1)} %bitcast.98, f32[1,512]{1,0:T(1,128)S(1)} %pad.48, f32[6,512]{1,0:T(8,128)S(1)} %broadcast_in_dim.65, f32[64,512]{1,0:T(8,128)} %r_ref.5), dimensions={0} | concatenate | bytes 557056 | tf_op jit(solution)/shard_map/concatenate | solution.py:540
  4.0 2.5 %collective-permute-start.2 = (f32[136,512]{1,0:T(8,128)S(1)}, f32[136,512]{1,0:T(8,128)S(1)}, u32[]{:S(2)}, u32[]{:S(2)}) collective-permute-start(f32[136,512]{1,0:T(8,128)S(1)} %concatenate.10), channel_id=1, source_target_pairs={{0,32},{1,9},{2,34},{3,11},{4,36},{5,13},{6,38},{7,15},{8,40},{9,1... | collective-permute-start | bytes 835592 | tf_op jit(solution)/shard_map/ppermute | solution.py:39
  6.5 3.3 %collective-permute-start.1 = (f32[136,512]{1,0:T(8,128)S(1)}, f32[136,512]{1,0:T(8,128)S(1)}, u32[]{:S(2)}, u32[]{:S(2)}) collective-permute-start(f32[136,512]{1,0:T(8,128)S(1)} %concatenate.10), channel_id=1, source_target_pairs={{0,64},{1,17},{2,66},{3,19},{4,68},{5,21},{6,70},{7,23},{8,72},{9,... | collective-permute-start | bytes 835592 | tf_op jit(solution)/shard_map/ppermute | solution.py:39
  10.6 2.3 %collective-permute-done.2 = f32[136,512]{1,0:T(8,128)S(1)} collective-permute-done((f32[136,512]{1,0:T(8,128)S(1)}, f32[136,512]{1,0:T(8,128)S(1)}, u32[]{:S(2)}, u32[]{:S(2)}) %collective-permute-start.2) | collective-permute-done | bytes 278560 | tf_op jit(solution)/shard_map/ppermute | solution.py:39
  12.9 4.0 %collective-permute-done.1 = f32[136,512]{1,0:T(8,128)S(1)} collective-permute-done((f32[136,512]{1,0:T(8,128)S(1)}, f32[136,512]{1,0:T(8,128)S(1)}, u32[]{:S(2)}, u32[]{:S(2)}) %collective-permute-start.1) | collective-permute-done | bytes 278560 | tf_op jit(solution)/shard_map/ppermute | solution.py:39
  18.1 2.5 %collective-permute-start.4 = (f32[4,128]{1,0:T(4,128)S(1)}, f32[4,128]{1,0:T(4,128)S(1)}, u32[]{:S(2)}, u32[]{:S(2)}) collective-permute-start(f32[4,128]{1,0:T(4,128)S(1)} %pad_add_fusion.2), channel_id=1, source_target_pairs={{0,16},{1,65},{2,18},{3,67},{4,20},{5,69},{6,22},{7,71},{8,24},{9,... | collective-permute-start | bytes 6152 | tf_op jit(solution)/shard_map/ppermute | solution.py:39
  22.0 1.2 collective-permute-done.3
  24.2 3.0 %collective-permute-start.7 = (f32[88,512]{1,0:T(8,128)S(1)}, f32[88,512]{1,0:T(8,128)S(1)}, u32[]{:S(2)}, u32[]{:S(2)}) collective-permute-start(f32[88,512]{1,0:T(8,128)S(1)} %get-tuple-element.60), channel_id=1, source_target_pairs={{0,4},{2,6},{4,0},{6,2},{1,5},{3,7},{5,1},{7,3},{8,12},{10,14},{12... | collective-permute-start | bytes 540680 | tf_op jit(solution)/shard_map/ppermute | solution.py:69
  28.8 2.7 %collective-permute-start.11 = (f32[2,136,512]{2,1,0:T(8,128)S(1)}, f32[2,136,512]{2,1,0:T(8,128)}, u32[]{:S(2)}, u32[]{:S(2)}) collective-permute-start(f32[2,136,512]{2,1,0:T(8,128)S(1)} %pad_maximum_fusion.2.p1), channel_id=1, source_target_pairs={{0,24},{1,97},{2,26},{3,99},{4,28},{5,101},{6,30},{7,103},{8,0},{9... | collective-permute-start | bytes 1671176 | tf_op jit(solution)/shard_map/ppermute | solution.py:39
  32.8 2.7 %collective-permute-done.8 = f32[88,512]{1,0:T(8,128)S(1)} collective-permute-done((f32[88,512]{1,0:T(8,128)S(1)}, f32[88,512]{1,0:T(8,128)S(1)}, u32[]{:S(2)}, u32[]{:S(2)}) %collective-permute-start.8) | collective-permute-done | bytes 180256 | tf_op jit(solution)/shard_map/ppermute | solution.py:69
  35.5 3.1 %collective-permute-start.9 = (f32[4,88,512]{2,1,0:T(8,128)S(1)}, f32[4,88,512]{2,1,0:T(8,128)S(1)}, u32[]{:S(2)}, u32[]{:S(2)}) collective-permute-start(f32[4,88,512]{2,1,0:T(8,128)S(1)} %pad_maximum_fusion.same), channel_id=1, source_target_pairs={{0,1},{1,0},{2,3},{3,2},{4,5},{5,4},{6,7},{7,6},{8,9},{9,8},{10,11... | collective-permute-start | bytes 2162696 | tf_op jit(solution)/shard_map/ppermute | solution.py:65
  38.6 2.3 %collective-permute-start.10 = (f32[2,136,512]{2,1,0:T(8,128)S(1)}, f32[2,136,512]{2,1,0:T(8,128)S(1)}, u32[]{:S(2)}, u32[]{:S(2)}) collective-permute-start(f32[2,136,512]{2,1,0:T(8,128)S(1)} %pad_maximum_fusion.1.p0), channel_id=1, source_target_pairs={{0,24},{1,97},{2,26},{3,99},{4,28},{5,101},{6,30},{7,103},{8,0},{9... | collective-permute-start | bytes 1671176 | tf_op jit(solution)/shard_map/ppermute | solution.py:39
  41.8 1.9 %collective-permute-start.14 = (f32[2,136,512]{2,1,0:T(8,128)}, f32[2,136,512]{2,1,0:T(8,128)S(1)}, u32[]{:S(2)}, u32[]{:S(2)}) collective-permute-start(f32[2,136,512]{2,1,0:T(8,128)} %collective-permute-done.11.p3), channel_id=1, source_target_pairs={{0,24},{1,97},{2,26},{3,99},{4,28},{5,101},{6,30},{7,103},{8,0},{9... | collective-permute-start | bytes 1671176 | tf_op jit(solution)/shard_map/ppermute | solution.py:39
  43.8 3.6 %collective-permute-done.10.p2 = f32[2,136,512]{2,1,0:T(8,128)S(1)} collective-permute-done((f32[2,136,512]{2,1,0:T(8,128)S(1)}, f32[2,136,512]{2,1,0:T(8,128)S(1)}, u32[]{:S(2)}, u32[]{:S(2)}) %collective-permute-start.10) | collective-permute-done | bytes 557088 | tf_op jit(solution)/shard_map/ppermute | solution.py:39
  47.5 3.3 %collective-permute-done.15.p7 = f32[2,136,512]{2,1,0:T(8,128)S(1)} collective-permute-done((f32[2,136,512]{2,1,0:T(8,128)S(1)}, f32[2,136,512]{2,1,0:T(8,128)S(1)}, u32[]{:S(2)}, u32[]{:S(2)}) %collective-permute-start.15) | collective-permute-done | bytes 557088 | tf_op jit(solution)/shard_map/ppermute | solution.py:39
  50.8 6.0 %collective-permute-done.13.p4 = f32[2,136,512]{2,1,0:T(8,128)S(1)} collective-permute-done((f32[2,136,512]{2,1,0:T(8,128)S(1)}, f32[2,136,512]{2,1,0:T(8,128)S(1)}, u32[]{:S(2)}, u32[]{:S(2)}) %collective-permute-start.13) | collective-permute-done | bytes 557088 | tf_op jit(solution)/shard_map/ppermute | solution.py:39
  56.8 9.9 %shard_map.77 = (f32[4,264,128]{2,1,0:T(8,128)S(1)}, f32[4,264,128]{2,1,0:T(8,128)S(1)}, s32[144]{0:T(256)S(1)}, bf16[32,2,512,512]{3,2,1,0:T(8,128)(2,1)}, f32[24,72,512]{2,1,0:T(8,128)S(1)}) custom-call(s32[3,8]{1,0:T(4,128)S(1)} %pad_add_fusion.1.own_ref, s32[8,16]{1,0:T(8,128)S(1)} %fusion.15.turned_ref, f32[2,2]{1,0:T(2,128)S(1)} %log_multiply_fusion.lc_ref, ...), custom_call_target="tpu_custom_call" | custom-call | flops 8000000000 | bytes 20000000 | tf_op jit(solution)/shard_map/pallas_call | solution.py:442
  66.7 5.1 %collective-permute-start.16 = (f32[4,264,128]{2,1,0:T(8,128)S(1)}, f32[4,264,128]{2,1,0:T(8,128)S(1)}, u32[]{:S(2)}, u32[]{:S(2)}) collective-permute-start(f32[4,264,128]{2,1,0:T(8,128)S(1)} %get-tuple-element.26), channel_id=1, source_target_pairs={{0,1},{1,0},{2,3},{3,2},{4,5},{5,4},{6,7},{7,6},{8,9},{9,8},{10,11... | collective-permute-start | bytes 1622024 | tf_op jit(solution)/shard_map/ppermute | solution.py:65
  71.8 1.6 collective-permute-done.16.b
  73.5 2.1 %collective-permute-start.18 = (f32[264,128]{1,0:T(8,128)S(1)}, f32[264,128]{1,0:T(8,128)S(1)}, u32[]{:S(2)}, u32[]{:S(2)}) collective-permute-start(f32[264,128]{1,0:T(8,128)S(1)} %get-tuple-element.57), channel_id=1, source_target_pairs={{0,6},{2,0},{4,2},{6,4},{1,7},{3,1},{5,3},{7,5},{8,14},{10,8},{12,... | collective-permute-start | bytes 405512 | tf_op jit(solution)/shard_map/ppermute | solution.py:69
  75.6 4.2 %collective-permute-done.19 = f32[264,128]{1,0:T(8,128)S(1)} collective-permute-done((f32[264,128]{1,0:T(8,128)S(1)}, f32[264,128]{1,0:T(8,128)S(1)}, u32[]{:S(2)}, u32[]{:S(2)}) %collective-permute-start.19) | collective-permute-done | bytes 135200 | tf_op jit(solution)/shard_map/ppermute | solution.py:69
  79.9 3.1 %collective-permute-done.17 = f32[264,128]{1,0:T(8,128)S(1)} collective-permute-done((f32[264,128]{1,0:T(8,128)S(1)}, f32[264,128]{1,0:T(8,128)S(1)}, u32[]{:S(2)}, u32[]{:S(2)}) %collective-permute-start.17) | collective-permute-done | bytes 135200 | tf_op jit(solution)/shard_map/ppermute | solution.py:69
  83.2 1.5 collective-permute-start.24
  84.7 2.4 %collective-permute-done.20 = f32[264,128]{1,0:T(8,128)S(1)} collective-permute-done((f32[264,128]{1,0:T(8,128)S(1)}, f32[264,128]{1,0:T(8,128)S(1)}, u32[]{:S(2)}, u32[]{:S(2)}) %collective-permute-start.20) | collective-permute-done | bytes 135200 | tf_op jit(solution)/shard_map/ppermute | solution.py:39
  87.1 3.1 %collective-permute-start.21 = (f32[2,264,128]{2,1,0:T(8,128)S(1)}, f32[2,264,128]{2,1,0:T(8,128)S(1)}, u32[]{:S(2)}, u32[]{:S(2)}) collective-permute-start(f32[2,264,128]{2,1,0:T(8,128)S(1)} %pad_maximum_fusion.3.p0), channel_id=1, source_target_pairs={{0,8},{1,33},{2,10},{3,35},{4,12},{5,37},{6,14},{7,39},{8,16},{9,4... | collective-permute-start | bytes 811016 | tf_op jit(solution)/shard_map/ppermute | solution.py:39
  91.5 2.5 %collective-permute-start.28 = (f32[2,264,128]{2,1,0:T(8,128)S(1)}, f32[2,264,128]{2,1,0:T(8,128)S(1)}, u32[]{:S(2)}, u32[]{:S(2)}) collective-permute-start(f32[2,264,128]{2,1,0:T(8,128)S(1)} %pad_maximum_fusion.4.p1), channel_id=1, source_target_pairs={{0,8},{1,33},{2,10},{3,35},{4,12},{5,37},{6,14},{7,39},{8,16},{9,4... | collective-permute-start | bytes 811016 | tf_op jit(solution)/shard_map/ppermute | solution.py:39
  96.0 1.7 collective-permute-done.25.p3
  98.2 2.7 %collective-permute-done.27.p2 = f32[2,264,128]{2,1,0:T(8,128)S(1)} collective-permute-done((f32[2,264,128]{2,1,0:T(8,128)S(1)}, f32[2,264,128]{2,1,0:T(8,128)S(1)}, u32[]{:S(2)}, u32[]{:S(2)}) %collective-permute-start.27) | collective-permute-done | bytes 270368 | tf_op jit(solution)/shard_map/ppermute | solution.py:39
  100.9 3.1 %shard_map.79.near_ref = f32[8,264,128]{2,1,0:T(8,128)S(1)} custom-call(s32[144]{0:T(256)S(1)} %get-tuple-element.24.list_ref, f32[2,2]{1,0:T(2,128)S(1)} %log_multiply_fusion.lc_ref, f32[2,264,128]{2,1,0:T(8,128)S(1)} %pad_maximum_fusion.3.p0, f32[2,264,128]{2,1,0:T(8,128)S(1)} %pad_maximum_fusion.4.p1, f32[2,264,128]{2,1,0:T(8,128)S(1)} %collective-permute-done.27.p2, ...), custom_call_target="tpu_custom_call" | custom-call | flops 3000000000 | bytes 12000000 | tf_op jit(solution)/shard_map/pallas_call | solution.py:483
  104.0 2.8 %shard_map.80 = (f32[4,264,128]{2,1,0:T(8,128)S(1)}, f32[4,264,128]{2,1,0:T(8,128)S(1)}) custom-call(s32[144]{0:T(256)S(1)} %get-tuple-element.24.list_ref, f32[2,2]{1,0:T(2,128)S(1)} %log_multiply_fusion.lc_ref, f32[2,264,128]{2,1,0:T(8,128)S(1)} %collective-permute-done.22.p4, f32[2,264,128]{2,1,0:T(8,128)S(1)} %collective-permute-done.26.p5, ...), custom_call_target="tpu_custom_call" | custom-call | flops 1000000000 | bytes 6000000 | tf_op jit(solution)/shard_map/pallas_call | solution.py:492
  106.8 6.8 %collective-permute-start.29 = (f32[4,264,128]{2,1,0:T(8,128)S(1)}, f32[4,264,128]{2,1,0:T(8,128)S(1)}, u32[]{:S(2)}, u32[]{:S(2)}) collective-permute-start(f32[4,264,128]{2,1,0:T(8,128)S(1)} %get-tuple-element.31), channel_id=1, source_target_pairs={{0,1},{1,0},{2,3},{3,2},{4,5},{5,4},{6,7},{7,6},{8,9},{9,8},{10,11... | collective-permute-start | bytes 1622024 | tf_op jit(solution)/shard_map/ppermute | solution.py:65
  113.6 1.6 collective-permute-done.29.b
  116.9 4.8 %collective-permute-done.32 = f32[264,128]{1,0:T(8,128)S(1)} collective-permute-done((f32[264,128]{1,0:T(8,128)S(1)}, f32[264,128]{1,0:T(8,128)S(1)}, u32[]{:S(2)}, u32[]{:S(2)}) %collective-permute-start.32) | collective-permute-done | bytes 135200 | tf_op jit(solution)/shard_map/ppermute | solution.py:69
  121.6 3.6 %collective-permute-done.30 = f32[264,128]{1,0:T(8,128)S(1)} collective-permute-done((f32[264,128]{1,0:T(8,128)S(1)}, f32[264,128]{1,0:T(8,128)S(1)}, u32[]{:S(2)}, u32[]{:S(2)}) %collective-permute-start.30) | collective-permute-done | bytes 135200 | tf_op jit(solution)/shard_map/ppermute | solution.py:69
  125.5 1.5 collective-permute-start.37
  127.0 2.7 %collective-permute-done.33 = f32[264,128]{1,0:T(8,128)S(1)} collective-permute-done((f32[264,128]{1,0:T(8,128)S(1)}, f32[264,128]{1,0:T(8,128)S(1)}, u32[]{:S(2)}, u32[]{:S(2)}) %collective-permute-start.33) | collective-permute-done | bytes 135200 | tf_op jit(solution)/shard_map/ppermute | solution.py:39
  131.0 1.4 collective-permute-done.36
  132.6 1.4 collective-permute-start.41
  134.0 3.6 %collective-permute-done.34.p6 = f32[2,264,128]{2,1,0:T(8,128)S(1)} collective-permute-done((f32[2,264,128]{2,1,0:T(8,128)S(1)}, f32[2,264,128]{2,1,0:T(8,128)S(1)}, u32[]{:S(2)}, u32[]{:S(2)}) %collective-permute-start.34) | collective-permute-done | bytes 270368 | tf_op jit(solution)/shard_map/ppermute | solution.py:39
  138.1 2.2 %collective-permute-start.39 = (f32[2,264,128]{2,1,0:T(8,128)S(1)}, f32[2,264,128]{2,1,0:T(8,128)S(1)}, u32[]{:S(2)}, u32[]{:S(2)}) collective-permute-start(f32[2,264,128]{2,1,0:T(8,128)S(1)} %collective-permute-done.38.p3), channel_id=1, source_target_pairs={{0,24},{1,97},{2,26},{3,99},{4,28},{5,101},{6,30},{7,103},{8,0},{9... | collective-permute-start | bytes 811016 | tf_op jit(solution)/shard_map/ppermute | solution.py:39
  141.0 3.1 %shard_map.82.near_ref = f32[8,264,128]{2,1,0:T(8,128)S(1)} custom-call(s32[144]{0:T(256)S(1)} %get-tuple-element.24.list_ref, f32[2,2]{1,0:T(2,128)S(1)} %log_multiply_fusion.lc_ref, f32[2,264,128]{2,1,0:T(8,128)S(1)} %pad_maximum_fusion.5.p0, f32[2,264,128]{2,1,0:T(8,128)S(1)} %pad_maximum_fusion.6.p1, f32[2,264,128]{2,1,0:T(8,128)S(1)} %collective-permute-done.40.p2, ...), custom_call_target="tpu_custom_call" | custom-call | flops 3000000000 | bytes 12000000 | tf_op jit(solution)/shard_map/pallas_call | solution.py:483
  144.4 2.8 %shard_map.83 = (f32[4,264,128]{2,1,0:T(8,128)S(1)}, f32[4,264,128]{2,1,0:T(8,128)S(1)}) custom-call(s32[144]{0:T(256)S(1)} %get-tuple-element.24.list_ref, f32[2,2]{1,0:T(2,128)S(1)} %log_multiply_fusion.lc_ref, f32[2,264,128]{2,1,0:T(8,128)S(1)} %collective-permute-done.35.p4, f32[2,264,128]{2,1,0:T(8,128)S(1)} %collective-permute-done.39.p5, ...), custom_call_target="tpu_custom_call" | custom-call | flops 1000000000 | bytes 6000000 | tf_op jit(solution)/shard_map/pallas_call | solution.py:492
  147.3 6.5 %collective-permute-start.42 = (f32[4,264,128]{2,1,0:T(8,128)S(1)}, f32[4,264,128]{2,1,0:T(8,128)S(1)}, u32[]{:S(2)}, u32[]{:S(2)}) collective-permute-start(f32[4,264,128]{2,1,0:T(8,128)S(1)} %get-tuple-element.35), channel_id=1, source_target_pairs={{0,1},{1,0},{2,3},{3,2},{4,5},{5,4},{6,7},{7,6},{8,9},{9,8},{10,11... | collective-permute-start | bytes 1622024 | tf_op jit(solution)/shard_map/ppermute | solution.py:65
  153.8 1.6 collective-permute-done.42.b
  155.5 1.2 collective-permute-start.44
  157.0 4.8 %collective-permute-done.45 = f32[264,128]{1,0:T(8,128)S(1)} collective-permute-done((f32[264,128]{1,0:T(8,128)S(1)}, f32[264,128]{1,0:T(8,128)S(1)}, u32[]{:S(2)}, u32[]{:S(2)}) %collective-permute-start.45) | collective-permute-done | bytes 135200 | tf_op jit(solution)/shard_map/ppermute | solution.py:69
  161.7 3.5 %collective-permute-done.43 = f32[264,128]{1,0:T(8,128)S(1)} collective-permute-done((f32[264,128]{1,0:T(8,128)S(1)}, f32[264,128]{1,0:T(8,128)S(1)}, u32[]{:S(2)}, u32[]{:S(2)}) %collective-permute-start.43) | collective-permute-done | bytes 135200 | tf_op jit(solution)/shard_map/ppermute | solution.py:69
  165.7 13.8 %all_to_all.5 = f32[128,1,128]{2,1,0:T(1,128)S(1)} all-to-all(f32[128,1,128]{2,1,0:T(1,128)S(1)} %broadcast_in_dim.77), channel_id=1, replica_groups=mesh['row_0'=4,'row_1'=4,'col_0'=4,'col_1'=2] {'row_0','row_1','col_0','..., dimensions={0} | all-to-all | bytes 131072 | tf_op jit(solution)/shard_map/all_to_all | solution.py:516
  (92 shorter events, 20.7 us)
Async XLA Ops:
  0.6 43.1 %copy-start.2 = (f32[2,2]{1,0:T(2,128)S(1)}, f32[2,2]{1,0:T(2,128)}, u32[]{:S(2)}) copy-start(f32[2,2]{1,0:T(2,128)} %param.10) | copy-start | bytes 52
  4.0 8.9 %collective-permute-start.2 = (f32[136,512]{1,0:T(8,128)S(1)}, f32[136,512]{1,0:T(8,128)S(1)}, u32[]{:S(2)}, u32[]{:S(2)}) collective-permute-start(f32[136,512]{1,0:T(8,128)S(1)} %concatenate.10), channel_id=1, source_target_pairs={{0,32},{1,9},{2,34},{3,11},{4,36},{5,13},{6,38},{7,15},{8,40},{9,1... | collective-permute-start | bytes 835592 | tf_op jit(solution)/shard_map/ppermute | solution.py:39
  6.5 10.4 %collective-permute-start.1 = (f32[136,512]{1,0:T(8,128)S(1)}, f32[136,512]{1,0:T(8,128)S(1)}, u32[]{:S(2)}, u32[]{:S(2)}) collective-permute-start(f32[136,512]{1,0:T(8,128)S(1)} %concatenate.10), channel_id=1, source_target_pairs={{0,64},{1,17},{2,66},{3,19},{4,68},{5,21},{6,70},{7,23},{8,72},{9,... | collective-permute-start | bytes 835592 | tf_op jit(solution)/shard_map/ppermute | solution.py:39
  9.8 7.1 %collective-permute-start = (f32[136,512]{1,0:T(8,128)S(1)}, f32[136,512]{1,0:T(8,128)S(1)}, u32[]{:S(2)}, u32[]{:S(2)}) collective-permute-start(f32[136,512]{1,0:T(8,128)S(1)} %concatenate.10), channel_id=1, source_target_pairs={{0,96},{1,25},{2,98},{3,27},{4,100},{5,29},{6,102},{7,31},{8,104},... | collective-permute-start | bytes 835592 | tf_op jit(solution)/shard_map/ppermute | solution.py:39
  16.9 4.7 %collective-permute-start.5 = (f32[4,128]{1,0:T(4,128)S(1)}, f32[4,128]{1,0:T(4,128)S(1)}, u32[]{:S(2)}, u32[]{:S(2)}) collective-permute-start(f32[4,128]{1,0:T(4,128)S(1)} %pad_add_fusion.2), channel_id=1, source_target_pairs={{0,8},{1,33},{2,10},{3,35},{4,12},{5,37},{6,14},{7,39},{8,16},{9,4... | collective-permute-start | bytes 6152 | tf_op jit(solution)/shard_map/ppermute | solution.py:39
  18.1 3.9 %collective-permute-start.4 = (f32[4,128]{1,0:T(4,128)S(1)}, f32[4,128]{1,0:T(4,128)S(1)}, u32[]{:S(2)}, u32[]{:S(2)}) collective-permute-start(f32[4,128]{1,0:T(4,128)S(1)} %pad_add_fusion.2), channel_id=1, source_target_pairs={{0,16},{1,65},{2,18},{3,67},{4,20},{5,69},{6,22},{7,71},{8,24},{9,... | collective-permute-start | bytes 6152 | tf_op jit(solution)/shard_map/ppermute | solution.py:39
  20.5 2.7 %collective-permute-start.3 = (f32[4,128]{1,0:T(4,128)S(1)}, f32[4,128]{1,0:T(4,128)S(1)}, u32[]{:S(2)}, u32[]{:S(2)}) collective-permute-start(f32[4,128]{1,0:T(4,128)S(1)} %pad_add_fusion.2), channel_id=1, source_target_pairs={{0,24},{1,97},{2,26},{3,99},{4,28},{5,101},{6,30},{7,103},{8,0},{9... | collective-permute-start | bytes 6152 | tf_op jit(solution)/shard_map/ppermute | solution.py:39
  24.2 7.4 %collective-permute-start.7 = (f32[88,512]{1,0:T(8,128)S(1)}, f32[88,512]{1,0:T(8,128)S(1)}, u32[]{:S(2)}, u32[]{:S(2)}) collective-permute-start(f32[88,512]{1,0:T(8,128)S(1)} %get-tuple-element.60), channel_id=1, source_target_pairs={{0,4},{2,6},{4,0},{6,2},{1,5},{3,7},{5,1},{7,3},{8,12},{10,14},{12... | collective-permute-start | bytes 540680 | tf_op jit(solution)/shard_map/ppermute | solution.py:69
  27.2 5.6 %collective-permute-start.6 = (f32[88,512]{1,0:T(8,128)S(1)}, f32[88,512]{1,0:T(8,128)S(1)}, u32[]{:S(2)}, u32[]{:S(2)}) collective-permute-start(f32[88,512]{1,0:T(8,128)S(1)} %get-tuple-element.60), channel_id=1, source_target_pairs={{0,6},{2,0},{4,2},{6,4},{1,7},{3,1},{5,3},{7,5},{8,14},{10,8},{12,... | collective-permute-start | bytes 540680 | tf_op jit(solution)/shard_map/ppermute | solution.py:69
  27.9 7.5 %collective-permute-start.8 = (f32[88,512]{1,0:T(8,128)S(1)}, f32[88,512]{1,0:T(8,128)S(1)}, u32[]{:S(2)}, u32[]{:S(2)}) collective-permute-start(f32[88,512]{1,0:T(8,128)S(1)} %get-tuple-element.60), channel_id=1, source_target_pairs={{0,2},{2,4},{4,6},{6,0},{1,3},{3,5},{5,7},{7,1},{8,10},{10,12},{12... | collective-permute-start | bytes 540680 | tf_op jit(solution)/shard_map/ppermute | solution.py:69
  28.7 12.3 %collective-permute-start.12 = (f32[2,136,512]{2,1,0:T(8,128)S(1)}, f32[2,136,512]{2,1,0:T(8,128)S(1)}, u32[]{:S(2)}, u32[]{:S(2)}) collective-permute-start(f32[2,136,512]{2,1,0:T(8,128)S(1)} %pad_maximum_fusion.1.p0), channel_id=1, source_target_pairs={{0,8},{1,33},{2,10},{3,35},{4,12},{5,37},{6,14},{7,39},{8,16},{9,4... | collective-permute-start | bytes 1671176 | tf_op jit(solution)/shard_map/ppermute | solution.py:39
  28.8 12.9 %collective-permute-start.11 = (f32[2,136,512]{2,1,0:T(8,128)S(1)}, f32[2,136,512]{2,1,0:T(8,128)}, u32[]{:S(2)}, u32[]{:S(2)}) collective-permute-start(f32[2,136,512]{2,1,0:T(8,128)S(1)} %pad_maximum_fusion.2.p1), channel_id=1, source_target_pairs={{0,24},{1,97},{2,26},{3,99},{4,28},{5,101},{6,30},{7,103},{8,0},{9... | collective-permute-start | bytes 1671176 | tf_op jit(solution)/shard_map/ppermute | solution.py:39
  35.5 8.2 %collective-permute-start.9 = (f32[4,88,512]{2,1,0:T(8,128)S(1)}, f32[4,88,512]{2,1,0:T(8,128)S(1)}, u32[]{:S(2)}, u32[]{:S(2)}) collective-permute-start(f32[4,88,512]{2,1,0:T(8,128)S(1)} %pad_maximum_fusion.same), channel_id=1, source_target_pairs={{0,1},{1,0},{2,3},{3,2},{4,5},{5,4},{6,7},{7,6},{8,9},{9,8},{10,11... | collective-permute-start | bytes 2162696 | tf_op jit(solution)/shard_map/ppermute | solution.py:65
  38.6 8.9 %collective-permute-start.10 = (f32[2,136,512]{2,1,0:T(8,128)S(1)}, f32[2,136,512]{2,1,0:T(8,128)S(1)}, u32[]{:S(2)}, u32[]{:S(2)}) collective-permute-start(f32[2,136,512]{2,1,0:T(8,128)S(1)} %pad_maximum_fusion.1.p0), channel_id=1, source_target_pairs={{0,24},{1,97},{2,26},{3,99},{4,28},{5,101},{6,30},{7,103},{8,0},{9... | collective-permute-start | bytes 1671176 | tf_op jit(solution)/shard_map/ppermute | solution.py:39
  40.9 9.9 %collective-permute-start.15 = (f32[2,136,512]{2,1,0:T(8,128)S(1)}, f32[2,136,512]{2,1,0:T(8,128)S(1)}, u32[]{:S(2)}, u32[]{:S(2)}) collective-permute-start(f32[2,136,512]{2,1,0:T(8,128)S(1)} %pad_maximum_fusion.2.p1), channel_id=1, source_target_pairs={{0,8},{1,33},{2,10},{3,35},{4,12},{5,37},{6,14},{7,39},{8,16},{9,4... | collective-permute-start | bytes 1671176 | tf_op jit(solution)/shard_map/ppermute | solution.py:39
  40.9 15.9 %collective-permute-start.13 = (f32[2,136,512]{2,1,0:T(8,128)S(1)}, f32[2,136,512]{2,1,0:T(8,128)S(1)}, u32[]{:S(2)}, u32[]{:S(2)}) collective-permute-start(f32[2,136,512]{2,1,0:T(8,128)S(1)} %collective-permute-done.12.p6), channel_id=1, source_target_pairs={{0,8},{1,33},{2,10},{3,35},{4,12},{5,37},{6,14},{7,39},{8,16},{9,4... | collective-permute-start | bytes 1671176 | tf_op jit(solution)/shard_map/ppermute | solution.py:39
  41.8 15.0 %collective-permute-start.14 = (f32[2,136,512]{2,1,0:T(8,128)}, f32[2,136,512]{2,1,0:T(8,128)S(1)}, u32[]{:S(2)}, u32[]{:S(2)}) collective-permute-start(f32[2,136,512]{2,1,0:T(8,128)} %collective-permute-done.11.p3), channel_id=1, source_target_pairs={{0,24},{1,97},{2,26},{3,99},{4,28},{5,101},{6,30},{7,103},{8,0},{9... | collective-permute-start | bytes 1671176 | tf_op jit(solution)/shard_map/ppermute | solution.py:39
  43.8 39.2 %copy-start = (f32[64,512]{1,0:T(8,128)S(1)}, f32[64,512]{1,0:T(8,128)}, u32[]{:S(2)}) copy-start(f32[64,512]{1,0:T(8,128)} %r_ref.5) | copy-start | bytes 393220
  66.7 6.7 %collective-permute-start.16 = (f32[4,264,128]{2,1,0:T(8,128)S(1)}, f32[4,264,128]{2,1,0:T(8,128)S(1)}, u32[]{:S(2)}, u32[]{:S(2)}) collective-permute-start(f32[4,264,128]{2,1,0:T(8,128)S(1)} %get-tuple-element.26), channel_id=1, source_target_pairs={{0,1},{1,0},{2,3},{3,2},{4,5},{5,4},{6,7},{7,6},{8,9},{9,8},{10,11... | collective-permute-start | bytes 1622024 | tf_op jit(solution)/shard_map/ppermute | solution.py:65
  73.4 6.4 %collective-permute-start.19 = (f32[264,128]{1,0:T(8,128)S(1)}, f32[264,128]{1,0:T(8,128)S(1)}, u32[]{:S(2)}, u32[]{:S(2)}) collective-permute-start(f32[264,128]{1,0:T(8,128)S(1)} %get-tuple-element.56), channel_id=1, source_target_pairs={{0,4},{2,6},{4,0},{6,2},{1,5},{3,7},{5,1},{7,3},{8,12},{10,14},{12... | collective-permute-start | bytes 405512 | tf_op jit(solution)/shard_map/ppermute | solution.py:69
  73.5 6.4 %collective-permute-start.18 = (f32[264,128]{1,0:T(8,128)S(1)}, f32[264,128]{1,0:T(8,128)S(1)}, u32[]{:S(2)}, u32[]{:S(2)}) collective-permute-start(f32[264,128]{1,0:T(8,128)S(1)} %get-tuple-element.57), channel_id=1, source_target_pairs={{0,6},{2,0},{4,2},{6,4},{1,7},{3,1},{5,3},{7,5},{8,14},{10,8},{12,... | collective-permute-start | bytes 405512 | tf_op jit(solution)/shard_map/ppermute | solution.py:69
  75.6 7.4 %collective-permute-start.17 = (f32[264,128]{1,0:T(8,128)S(1)}, f32[264,128]{1,0:T(8,128)S(1)}, u32[]{:S(2)}, u32[]{:S(2)}) collective-permute-start(f32[264,128]{1,0:T(8,128)S(1)} %get-tuple-element.58), channel_id=1, source_target_pairs={{0,2},{2,4},{4,6},{6,0},{1,3},{3,5},{5,7},{7,1},{8,10},{10,12},{12... | collective-permute-start | bytes 405512 | tf_op jit(solution)/shard_map/ppermute | solution.py:69
  83.2 3.9 %collective-permute-start.20 = (f32[264,128]{1,0:T(8,128)S(1)}, f32[264,128]{1,0:T(8,128)S(1)}, u32[]{:S(2)}, u32[]{:S(2)}) collective-permute-start(f32[264,128]{1,0:T(8,128)S(1)} %get-tuple-element.27.w_ref.w0_ref), channel_id=1, source_target_pairs={{0,96},{1,25},{2,98},{3,27},{4,100},{5,29},{6,102},{7,31},{8,104},... | collective-permute-start | bytes 405512 | tf_op jit(solution)/shard_map/ppermute | solution.py:39
  83.2 6.9 %collective-permute-start.24 = (f32[264,128]{1,0:T(8,128)S(1)}, f32[264,128]{1,0:T(8,128)S(1)}, u32[]{:S(2)}, u32[]{:S(2)}) collective-permute-start(f32[264,128]{1,0:T(8,128)S(1)} %get-tuple-element.27.w_ref.w0_ref), channel_id=1, source_target_pairs={{0,32},{1,9},{2,34},{3,11},{4,36},{5,13},{6,38},{7,15},{8,40},{9,1... | collective-permute-start | bytes 405512 | tf_op jit(solution)/shard_map/ppermute | solution.py:39
  84.7 5.5 %collective-permute-start.23 = (f32[264,128]{1,0:T(8,128)S(1)}, f32[264,128]{1,0:T(8,128)S(1)}, u32[]{:S(2)}, u32[]{:S(2)}) collective-permute-start(f32[264,128]{1,0:T(8,128)S(1)} %get-tuple-element.27.w_ref.w0_ref), channel_id=1, source_target_pairs={{0,64},{1,17},{2,66},{3,19},{4,68},{5,21},{6,70},{7,23},{8,72},{9,... | collective-permute-start | bytes 405512 | tf_op jit(solution)/shard_map/ppermute | solution.py:39
  87.1 8.1 %collective-permute-start.21 = (f32[2,264,128]{2,1,0:T(8,128)S(1)}, f32[2,264,128]{2,1,0:T(8,128)S(1)}, u32[]{:S(2)}, u32[]{:S(2)}) collective-permute-start(f32[2,264,128]{2,1,0:T(8,128)S(1)} %pad_maximum_fusion.3.p0), channel_id=1, source_target_pairs={{0,8},{1,33},{2,10},{3,35},{4,12},{5,37},{6,14},{7,39},{8,16},{9,4... | collective-permute-start | bytes 811016 | tf_op jit(solution)/shard_map/ppermute | solution.py:39
  90.2 7.5 %collective-permute-start.25 = (f32[2,264,128]{2,1,0:T(8,128)S(1)}, f32[2,264,128]{2,1,0:T(8,128)S(1)}, u32[]{:S(2)}, u32[]{:S(2)}) collective-permute-start(f32[2,264,128]{2,1,0:T(8,128)S(1)} %pad_maximum_fusion.4.p1), channel_id=1, source_target_pairs={{0,24},{1,97},{2,26},{3,99},{4,28},{5,101},{6,30},{7,103},{8,0},{9... | collective-permute-start | bytes 811016 | tf_op jit(solution)/shard_map/ppermute | solution.py:39
  91.4 9.5 %collective-permute-start.27 = (f32[2,264,128]{2,1,0:T(8,128)S(1)}, f32[2,264,128]{2,1,0:T(8,128)S(1)}, u32[]{:S(2)}, u32[]{:S(2)}) collective-permute-start(f32[2,264,128]{2,1,0:T(8,128)S(1)} %pad_maximum_fusion.3.p0), channel_id=1, source_target_pairs={{0,24},{1,97},{2,26},{3,99},{4,28},{5,101},{6,30},{7,103},{8,0},{9... | collective-permute-start | bytes 811016 | tf_op jit(solution)/shard_map/ppermute | solution.py:39
  91.5 9.3 %collective-permute-start.28 = (f32[2,264,128]{2,1,0:T(8,128)S(1)}, f32[2,264,128]{2,1,0:T(8,128)S(1)}, u32[]{:S(2)}, u32[]{:S(2)}) collective-permute-start(f32[2,264,128]{2,1,0:T(8,128)S(1)} %pad_maximum_fusion.4.p1), channel_id=1, source_target_pairs={{0,8},{1,33},{2,10},{3,35},{4,12},{5,37},{6,14},{7,39},{8,16},{9,4... | collective-permute-start | bytes 811016 | tf_op jit(solution)/shard_map/ppermute | solution.py:39
  95.2 8.7 %collective-permute-start.22 = (f32[2,264,128]{2,1,0:T(8,128)S(1)}, f32[2,264,128]{2,1,0:T(8,128)S(1)}, u32[]{:S(2)}, u32[]{:S(2)}) collective-permute-start(f32[2,264,128]{2,1,0:T(8,128)S(1)} %collective-permute-done.21.p6), channel_id=1, source_target_pairs={{0,8},{1,33},{2,10},{3,35},{4,12},{5,37},{6,14},{7,39},{8,16},{9,4... | collective-permute-start | bytes 811016 | tf_op jit(solution)/shard_map/ppermute | solution.py:39
  97.7 6.3 %collective-permute-start.26 = (f32[2,264,128]{2,1,0:T(8,128)S(1)}, f32[2,264,128]{2,1,0:T(8,128)S(1)}, u32[]{:S(2)}, u32[]{:S(2)}) collective-permute-start(f32[2,264,128]{2,1,0:T(8,128)S(1)} %collective-permute-done.25.p3), channel_id=1, source_target_pairs={{0,24},{1,97},{2,26},{3,99},{4,28},{5,101},{6,30},{7,103},{8,0},{9... | collective-permute-start | bytes 811016 | tf_op jit(solution)/shard_map/ppermute | solution.py:39
  106.8 8.4 %collective-permute-start.29 = (f32[4,264,128]{2,1,0:T(8,128)S(1)}, f32[4,264,128]{2,1,0:T(8,128)S(1)}, u32[]{:S(2)}, u32[]{:S(2)}) collective-permute-start(f32[4,264,128]{2,1,0:T(8,128)S(1)} %get-tuple-element.31), channel_id=1, source_target_pairs={{0,1},{1,0},{2,3},{3,2},{4,5},{5,4},{6,7},{7,6},{8,9},{9,8},{10,11... | collective-permute-start | bytes 1622024 | tf_op jit(solution)/shard_map/ppermute | solution.py:65
  115.3 6.4 %collective-permute-start.32 = (f32[264,128]{1,0:T(8,128)S(1)}, f32[264,128]{1,0:T(8,128)S(1)}, u32[]{:S(2)}, u32[]{:S(2)}) collective-permute-start(f32[264,128]{1,0:T(8,128)S(1)} %get-tuple-element.53), channel_id=1, source_target_pairs={{0,4},{2,6},{4,0},{6,2},{1,5},{3,7},{5,1},{7,3},{8,12},{10,14},{12... | collective-permute-start | bytes 405512 | tf_op jit(solution)/shard_map/ppermute | solution.py:69
  115.3 6.3 %collective-permute-start.31 = (f32[264,128]{1,0:T(8,128)S(1)}, f32[264,128]{1,0:T(8,128)S(1)}, u32[]{:S(2)}, u32[]{:S(2)}) collective-permute-start(f32[264,128]{1,0:T(8,128)S(1)} %get-tuple-element.54), channel_id=1, source_target_pairs={{0,6},{2,0},{4,2},{6,4},{1,7},{3,1},{5,3},{7,5},{8,14},{10,8},{12,... | collective-permute-start | bytes 405512 | tf_op jit(solution)/shard_map/ppermute | solution.py:69
  116.5 8.7 %collective-permute-start.30 = (f32[264,128]{1,0:T(8,128)S(1)}, f32[264,128]{1,0:T(8,128)S(1)}, u32[]{:S(2)}, u32[]{:S(2)}) collective-permute-start(f32[264,128]{1,0:T(8,128)S(1)} %get-tuple-element.55), channel_id=1, source_target_pairs={{0,2},{2,4},{4,6},{6,0},{1,3},{3,5},{5,7},{7,1},{8,10},{10,12},{12... | collective-permute-start | bytes 405512 | tf_op jit(solution)/shard_map/ppermute | solution.py:69
  125.5 4.2 %collective-permute-start.33 = (f32[264,128]{1,0:T(8,128)S(1)}, f32[264,128]{1,0:T(8,128)S(1)}, u32[]{:S(2)}, u32[]{:S(2)}) collective-permute-start(f32[264,128]{1,0:T(8,128)S(1)} %get-tuple-element.33.w1_ref), channel_id=1, source_target_pairs={{0,96},{1,25},{2,98},{3,27},{4,100},{5,29},{6,102},{7,31},{8,104},... | collective-permute-start | bytes 405512 | tf_op jit(solution)/shard_map/ppermute | solution.py:39
  125.5 5.4 %collective-permute-start.37 = (f32[264,128]{1,0:T(8,128)S(1)}, f32[264,128]{1,0:T(8,128)S(1)}, u32[]{:S(2)}, u32[]{:S(2)}) collective-permute-start(f32[264,128]{1,0:T(8,128)S(1)} %get-tuple-element.33.w1_ref), channel_id=1, source_target_pairs={{0,32},{1,9},{2,34},{3,11},{4,36},{5,13},{6,38},{7,15},{8,40},{9,1... | collective-permute-start | bytes 405512 | tf_op jit(solution)/shard_map/ppermute | solution.py:39
  127.0 5.4 %collective-permute-start.36 = (f32[264,128]{1,0:T(8,128)S(1)}, f32[264,128]{1,0:T(8,128)S(1)}, u32[]{:S(2)}, u32[]{:S(2)}) collective-permute-start(f32[264,128]{1,0:T(8,128)S(1)} %get-tuple-element.33.w1_ref), channel_id=1, source_target_pairs={{0,64},{1,17},{2,66},{3,19},{4,68},{5,21},{6,70},{7,23},{8,72},{9,... | collective-permute-start | bytes 405512 | tf_op jit(solution)/shard_map/ppermute | solution.py:39
  129.7 7.9 %collective-permute-start.34 = (f32[2,264,128]{2,1,0:T(8,128)S(1)}, f32[2,264,128]{2,1,0:T(8,128)S(1)}, u32[]{:S(2)}, u32[]{:S(2)}) collective-permute-start(f32[2,264,128]{2,1,0:T(8,128)S(1)} %pad_maximum_fusion.5.p0), channel_id=1, source_target_pairs={{0,8},{1,33},{2,10},{3,35},{4,12},{5,37},{6,14},{7,39},{8,16},{9,4... | collective-permute-start | bytes 811016 | tf_op jit(solution)/shard_map/ppermute | solution.py:39
  132.4 5.7 %collective-permute-start.38 = (f32[2,264,128]{2,1,0:T(8,128)S(1)}, f32[2,264,128]{2,1,0:T(8,128)S(1)}, u32[]{:S(2)}, u32[]{:S(2)}) collective-permute-start(f32[2,264,128]{2,1,0:T(8,128)S(1)} %pad_maximum_fusion.6.p1), channel_id=1, source_target_pairs={{0,24},{1,97},{2,26},{3,99},{4,28},{5,101},{6,30},{7,103},{8,0},{9... | collective-permute-start | bytes 811016 | tf_op jit(solution)/shard_map/ppermute | solution.py:39
  132.6 8.4 %collective-permute-start.40 = (f32[2,264,128]{2,1,0:T(8,128)S(1)}, f32[2,264,128]{2,1,0:T(8,128)S(1)}, u32[]{:S(2)}, u32[]{:S(2)}) collective-permute-start(f32[2,264,128]{2,1,0:T(8,128)S(1)} %pad_maximum_fusion.5.p0), channel_id=1, source_target_pairs={{0,24},{1,97},{2,26},{3,99},{4,28},{5,101},{6,30},{7,103},{8,0},{9... | collective-permute-start | bytes 811016 | tf_op jit(solution)/shard_map/ppermute | solution.py:39
  132.6 8.3 %collective-permute-start.41 = (f32[2,264,128]{2,1,0:T(8,128)S(1)}, f32[2,264,128]{2,1,0:T(8,128)S(1)}, u32[]{:S(2)}, u32[]{:S(2)}) collective-permute-start(f32[2,264,128]{2,1,0:T(8,128)S(1)} %pad_maximum_fusion.6.p1), channel_id=1, source_target_pairs={{0,8},{1,33},{2,10},{3,35},{4,12},{5,37},{6,14},{7,39},{8,16},{9,4... | collective-permute-start | bytes 811016 | tf_op jit(solution)/shard_map/ppermute | solution.py:39
  137.6 6.8 %collective-permute-start.35 = (f32[2,264,128]{2,1,0:T(8,128)S(1)}, f32[2,264,128]{2,1,0:T(8,128)S(1)}, u32[]{:S(2)}, u32[]{:S(2)}) collective-permute-start(f32[2,264,128]{2,1,0:T(8,128)S(1)} %collective-permute-done.34.p6), channel_id=1, source_target_pairs={{0,8},{1,33},{2,10},{3,35},{4,12},{5,37},{6,14},{7,39},{8,16},{9,4... | collective-permute-start | bytes 811016 | tf_op jit(solution)/shard_map/ppermute | solution.py:39
  138.1 6.4 %collective-permute-start.39 = (f32[2,264,128]{2,1,0:T(8,128)S(1)}, f32[2,264,128]{2,1,0:T(8,128)S(1)}, u32[]{:S(2)}, u32[]{:S(2)}) collective-permute-start(f32[2,264,128]{2,1,0:T(8,128)S(1)} %collective-permute-done.38.p3), channel_id=1, source_target_pairs={{0,24},{1,97},{2,26},{3,99},{4,28},{5,101},{6,30},{7,103},{8,0},{9... | collective-permute-start | bytes 811016 | tf_op jit(solution)/shard_map/ppermute | solution.py:39
  147.3 8.0 %collective-permute-start.42 = (f32[4,264,128]{2,1,0:T(8,128)S(1)}, f32[4,264,128]{2,1,0:T(8,128)S(1)}, u32[]{:S(2)}, u32[]{:S(2)}) collective-permute-start(f32[4,264,128]{2,1,0:T(8,128)S(1)} %get-tuple-element.35), channel_id=1, source_target_pairs={{0,1},{1,0},{2,3},{3,2},{4,5},{5,4},{6,7},{7,6},{8,9},{9,8},{10,11... | collective-permute-start | bytes 1622024 | tf_op jit(solution)/shard_map/ppermute | solution.py:65
  155.4 6.4 %collective-permute-start.45 = (f32[264,128]{1,0:T(8,128)S(1)}, f32[264,128]{1,0:T(8,128)S(1)}, u32[]{:S(2)}, u32[]{:S(2)}) collective-permute-start(f32[264,128]{1,0:T(8,128)S(1)} %get-tuple-element.50), channel_id=1, source_target_pairs={{0,4},{2,6},{4,0},{6,2},{1,5},{3,7},{5,1},{7,3},{8,12},{10,14},{12... | collective-permute-start | bytes 405512 | tf_op jit(solution)/shard_map/ppermute | solution.py:69
  155.5 6.2 %collective-permute-start.44 = (f32[264,128]{1,0:T(8,128)S(1)}, f32[264,128]{1,0:T(8,128)S(1)}, u32[]{:S(2)}, u32[]{:S(2)}) collective-permute-start(f32[264,128]{1,0:T(8,128)S(1)} %get-tuple-element.51), channel_id=1, source_target_pairs={{0,6},{2,0},{4,2},{6,4},{1,7},{3,1},{5,3},{7,5},{8,14},{10,8},{12,... | collective-permute-start | bytes 405512 | tf_op jit(solution)/shard_map/ppermute | solution.py:69
  156.8 8.5 %collective-permute-start.43 = (f32[264,128]{1,0:T(8,128)S(1)}, f32[264,128]{1,0:T(8,128)S(1)}, u32[]{:S(2)}, u32[]{:S(2)}) collective-permute-start(f32[264,128]{1,0:T(8,128)S(1)} %get-tuple-element.52), channel_id=1, source_target_pairs={{0,2},{2,4},{4,6},{6,0},{1,3},{3,5},{5,7},{7,1},{8,10},{10,12},{12... | collective-permute-start | bytes 405512 | tf_op jit(solution)/shard_map/ppermute | solution.py:69
  (1 other events, 39.2 us)

commit v3 on v2

--- a/solution.py
+++ b/solution.py
@@ -15,7 +15,7 @@
 ROW, COL = (X, Z), (Y, C)
 BODY = 256
 ROWS = BODY + 8
-KEPT = 32
+KEPT = 48
 SLOTS_OUT = 144
 KAPPA = math.log2(math.e) / 12.0
 F32, BF16 = jnp.float32, jnp.bfloat16
@@ -139,37 +139,56 @@
 
 
 def first_kernel(
-    own_ref, turned_ref, lc_ref, p0, p1, p2, p3, p4, p5, p6, p7, same, across,
+    place_ref, slots_ref, lc_ref, p0, p1, p2, p3, p4, p5, p6, p7, cells, same, across,
     keep_ref, other_ref, list_ref, store_ref, facts_ref,
-    fin_ref, x_ref, xs_ref, e_ref, pair_ref, acc_ref, sems, fact_sem, load_sems,
+    fin_ref, x_ref, xs_ref, cells_ref, hits_ref, hit_ref, e_ref, pair_ref, acc_ref, fact_sem, load_sems, save_sems,
 ):
     loads = []
     for q, piece in enumerate((p0, p1, p2, p3, p4, p5, p6, p7)):
         at = pl.ds(2 * q, 2)
-        loads.append(pltpu.make_async_copy(piece.at[:, pl.ds(0, 72), :], fin_ref.at[at], load_sems.at[q]))
-        loads.append(pltpu.make_async_copy(piece.at[:, pl.ds(72, 64), :], x_ref.at[at], load_sems.at[8 + q]))
-    loads.append(pltpu.make_async_copy(same.at[:, pl.ds(0, 72), :], fin_ref.at[pl.ds(16, 4)], load_sems.at[16]))
-    loads.append(pltpu.make_async_copy(across.at[:, pl.ds(0, 72), :], fin_ref.at[pl.ds(20, 4)], load_sems.at[17]))
+        loads.append(pltpu.make_async_copy(piece.at[:, pl.ds(0, 72), :], fin_ref.at[at], load_sems.at[8 + q]))
+        loads.append(pltpu.make_async_copy(piece.at[:, pl.ds(72, 64), :], x_ref.at[at], load_sems.at[16 + q]))
+    loads.append(pltpu.make_async_copy(same, fin_ref.at[pl.ds(16, 4)], load_sems.at[24]))
+    loads.append(pltpu.make_async_copy(across, fin_ref.at[pl.ds(20, 4)], load_sems.at[25]))
+    x, z, y, c = (place_ref[axis] for axis in range(4))
+    for place in range(16):
+        s1, s2 = place & 3, place >> 2
+        dx, dz = jnp.where(c == 0, s1, s2), jnp.where(c == 0, s2, s1)
+        row = ((x + dx) & 3) * 4 + ((z + dz) & 3)
+        loads.append(pltpu.make_async_copy(cells.at[row], cells_ref.at[pl.ds(8 * place, 8)], load_sems.at[26 + place]))
     for load in loads:
         load.start()
     acc_ref[...] = jnp.zeros_like(acc_ref)
-
+    for load in loads[18:34]:
+        load.wait()
+    mine = lax.broadcasted_iota(jnp.int32, (128, 128), 1) == (y * 2 + c) * 16 + x * 4 + z
+    found = jnp.where(mine, cells_ref[...], 0.0)
+    found = jnp.broadcast_to(jnp.sum(found, axis=1, keepdims=True), (128, 128))
+    hits_ref[...] = found.T[0:8, :].astype(jnp.int32)
+    hits = pltpu.make_async_copy(hits_ref, hit_ref, fact_sem)
+    hits.start()
+    own = []
+    for slot in range(8):
+        a, b, live = (slots_ref[0, 0, slot, field] for field in range(3))
+        dx, dz = ((b >> 2) - x) & 3, ((b & 3) - z) & 3
+        s1, s2 = jnp.where(c == 0, dx, dz), jnp.where(c == 0, dz, dx)
+        k = ((a & 1) ^ c) * 4 + (((a >> 1) - y) & 3)
+        own.append((k + 8 * (s2 * 4 + s1) + 256 * (16 + k), live, jnp.where(s2 == 2, 1, 0)))
+    hits.wait()
     n = jnp.int32(0)
     for far in (False, True):
-        for slot in range(8):
-            list_ref[n] = own_ref[0, slot]
-            n = n + own_ref[2 if far else 1, slot]
-        for k in range(8):
-            for there in range(16):
-                place = there if k < 4 else (there & 3) * 4 + (there >> 2)
-                if (place >> 2 == 2) == far:
-                    list_ref[n] = k + 8 * place + 128 + 256 * (16 + k)
-                    n = n + turned_ref[k, there]
+        for entry, live, there in own:
+            list_ref[n] = entry
+            n = n + live * (there if far else 1 - there)
+        for place in range(8, 12) if far else (*range(8), *range(12, 16)):
+            for k in range(8):
+                list_ref[n] = k + 8 * place + 128 + 256 * (16 + k)
+                n = n + hit_ref[0, place * 8 + k]
         if not far:
             near = n
     list_ref[SLOTS_OUT - 2] = near
     list_ref[SLOTS_OUT - 1] = n
-    for load in loads:
+    for load in loads[0:18]:
         load.wait()
     facts = pltpu.make_async_copy(fin_ref, facts_ref, fact_sem)
     facts.start()
@@ -178,7 +197,7 @@
 
     def saved(t):
         slot = t & 1
-        return pltpu.make_async_copy(pair_ref.at[slot], store_ref.at[jnp.minimum(t, KEPT - 1)], sems.at[slot])
+        return pltpu.make_async_copy(pair_ref.at[slot], store_ref.at[jnp.minimum(t, KEPT - 1)], save_sems.at[slot])
 
     def visit(t, carry):
         k, place, turned, block = unpack(list_ref[t])
@@ -411,6 +430,28 @@
         res_ref[:, lanes(g)] = r - alpha * s
 
 
+def pack_kernel(slots_ref, factors_ref, component_ref, values_ref, out_ref, facts_ref, label_ref, sems):
+    loads = [
+        pltpu.make_async_copy(component_ref, label_ref, sems.at[0]),
+        pltpu.make_async_copy(factors_ref, out_ref.at[pl.ds(0, 64), :], sems.at[1]),
+        pltpu.make_async_copy(values_ref, out_ref.at[pl.ds(72, 64), :], sems.at[2]),
+    ]
+    for load in loads:
+        load.start()
+    lane = lax.broadcasted_iota(jnp.int32, (8, TILE), 1)
+    row = lax.broadcasted_iota(jnp.int32, (8, TILE), 0)
+    cells = jnp.zeros((8, TILE), jnp.int32)
+    for slot in range(8):
+        cell = slots_ref[0, 0, slot, 0] * 16 + slots_ref[0, 0, slot, 1]
+        cells = cells + jnp.where(lane == cell, slots_ref[0, 0, slot, 2], 0)
+    for load in loads:
+        load.wait()
+    below = jnp.where(row == 0, label_ref[...], jnp.where(row == 1, cells, 0)).astype(F32)
+    out_ref[64:72, :] = below
+    facts_ref[0:64, :] = out_ref[0:64, :]
+    facts_ref[64:72, :] = below
+
+
 VMEM = pl.BlockSpec(memory_space=pltpu.VMEM)
 SMEM = pl.BlockSpec(memory_space=pltpu.SMEM)
 ANY = pl.BlockSpec(memory_space=pl.ANY)
@@ -432,38 +473,62 @@
     )(*parts, *args)
 
 
+def pack(slots, factors, component, values):
+    return pl.pallas_call(
+        pack_kernel,
+        out_shape=[jax.ShapeDtypeStruct((136, TILE), F32), jax.ShapeDtypeStruct((72, TILE), F32)],
+        in_specs=[SMEM, ANY, ANY, ANY],
+        out_specs=[VMEM, VMEM],
+        scratch_shapes=[pltpu.VMEM((1, TILE), jnp.int32), pltpu.SemaphoreType.DMA((3,))],
+        compiler_params=pltpu.CompilerParams(vmem_limit_bytes=4 << 20),
+    )(slots, factors, component, values)
+
+
+def laid(parts):
+    height, total = parts[0].shape[0], 0.0
+    for k, part in enumerate(parts):
+        total = total + jnp.pad(part, ((k * height, (len(parts) - 1 - k) * height), (0, 0)))
+    return total
+
+
 PART = jax.ShapeDtypeStruct((4, ROWS, 128), F32)
 
 
 ACC = jax.ShapeDtypeStruct((8, ROWS, 128), F32)
 
 
-def first_operate(own, turned, log_coupling, pieces, same, across):
+STORE = jax.ShapeDtypeStruct((KEPT, 2, TILE, TILE), BF16)
+
+
+def first_operate(place, slots, log_coupling, pieces, cells, same, across):
     return pl.pallas_call(
         first_kernel,
         out_shape=[
             PART,
             PART,
             jax.ShapeDtypeStruct((SLOTS_OUT,), jnp.int32),
-            jax.ShapeDtypeStruct((KEPT, 2, TILE, TILE), BF16),
+            STORE,
             jax.ShapeDtypeStruct((24, 72, TILE), F32),
         ],
-        in_specs=[SMEM, SMEM, SMEM] + [ANY] * 10,
+        in_specs=[SMEM] * 3 + [ANY] * 11,
         out_specs=[VMEM, VMEM, SMEM, ANY, ANY],
         scratch_shapes=[
             pltpu.VMEM((24, 72, TILE), F32),
             pltpu.VMEM((16, 64, TILE), F32),
             pltpu.VMEM((16, 128, TILE), BF16),
+            pltpu.VMEM((128, 128), F32),
+            pltpu.VMEM((8, 128), jnp.int32),
+            pltpu.SMEM((8, 128), jnp.int32),
             pltpu.VMEM((TILE, TILE), F32),
             pltpu.VMEM((2, 2, TILE, TILE), BF16),
             pltpu.VMEM((8, ROWS, 128), F32),
+            pltpu.SemaphoreType.DMA,
+            pltpu.SemaphoreType.DMA((42,)),
             pltpu.SemaphoreType.DMA((2,)),
-            pltpu.SemaphoreType.DMA,
-            pltpu.SemaphoreType.DMA((18,)),
         ],
-        compiler_params=pltpu.CompilerParams(vmem_limit_bytes=28 << 20),
+        compiler_params=pltpu.CompilerParams(vmem_limit_bytes=18 << 20),
         cost_estimate=pl.CostEstimate(flops=8_000_000_000, bytes_accessed=20_000_000, transcendentals=2_000_000),
-    )(own, turned, log_coupling, *pieces, same, across)
+    )(place, slots, log_coupling, *pieces, cells, same, across)
 
 
 def scratch(places):
@@ -486,7 +551,7 @@
         in_specs=[SMEM, SMEM] + [VMEM] * 6 + [ANY] * 2,
         out_specs=VMEM,
         scratch_shapes=scratch(12) + SEMS,
-        compiler_params=pltpu.CompilerParams(vmem_limit_bytes=24 << 20),
+        compiler_params=pltpu.CompilerParams(vmem_limit_bytes=14 << 20),
         cost_estimate=pl.CostEstimate(flops=3_000_000_000, bytes_accessed=12_000_000, transcendentals=0),
     )(listed, log_coupling, *pieces[0:4], *pieces[6:8], store, facts)
     return pl.pallas_call(
@@ -495,20 +560,9 @@
         in_specs=[SMEM, SMEM] + [VMEM] * 3 + [ANY] * 2,
         out_specs=[VMEM, VMEM],
         scratch_shapes=scratch(4) + [pltpu.VMEM((8, ROWS, 128), F32)] + SEMS,
-        compiler_params=pltpu.CompilerParams(vmem_limit_bytes=24 << 20),
+        compiler_params=pltpu.CompilerParams(vmem_limit_bytes=14 << 20),
         cost_estimate=pl.CostEstimate(flops=1_000_000_000, bytes_accessed=6_000_000, transcendentals=0),
     )(listed, log_coupling, *pieces[4:6], near, store, facts)
-
-
-def own_entries(slots, place):
-    x, z, y, c = place
-    a, b = slots[:, 0], slots[:, 1]
-    dx, dz = ((b >> 2) - x) & 3, ((b & 3) - z) & 3
-    s1, s2 = jnp.where(c == 0, dx, dz), jnp.where(c == 0, dz, dx)
-    k = ((a & 1) ^ c) * 4 + (((a >> 1) - y) & 3)
-    entry = k + 8 * (s2 * 4 + s1) + 256 * (16 + k)
-    far = (s2 == 2).astype(jnp.int32)
-    return jnp.stack([entry, slots[:, 2] * (1 - far), slots[:, 2] * far])
 
 
 def to_everyone(row, count, axes):
@@ -516,44 +570,20 @@
     return lax.all_to_all(copies, axes, split_axis=0, concat_axis=0, tiled=True)
 
 
-def laid(parts, height, width):
-    total, at = 0.0, 0
-    for part in parts:
-        total = total + jnp.pad(part, ((at, height - at - part.shape[0]), (0, width - part.shape[1])))
-        at += part.shape[0]
-    return total
-
-
-def below(rows):
-    padded = [jnp.pad(row, ((0, 0), (0, TILE - row.shape[1]))) for row in rows]
-    return jnp.concatenate([*padded, jnp.zeros((8 - len(rows), TILE), F32)])
-
-
 def shards(innovations, obs_factors, component, obs_error, coupling, tile_slots):
-    place = tuple(lax.axis_index(axis) for axis in ALL)
-    x, z, y, c = place
-    label = component.astype(F32)[None, :]
-    slots = tile_slots[0, 0]
-    lane = lax.broadcasted_iota(jnp.int32, (1, 128), 1)
-    cell = slots[:, 0:1] * 16 + slots[:, 1:2]
-    cells = jnp.sum(jnp.where(cell == lane, slots[:, 2:3], 0), axis=0, keepdims=True).astype(F32)
-    payload = jnp.concatenate([obs_factors, below([label, cells]), innovations], axis=0)
-    line = gather_line(payload)
-    pieces = gather_plane(line)
-    cells = laid([block[65:66, 0:128] for block in line], 4, 128)
-    cells = [cells, hop(cells, 2, -1), hop(cells, 2, 2), hop(cells, 2, 1)]
-    facts = laid([obs_factors, below([label]), *cells], 88, TILE)
+    place = jnp.stack([lax.axis_index(axis) for axis in ALL]).astype(jnp.int32)
+    payload, facts = pack(tile_slots, obs_factors, component[None, :], innovations)
     same = jnp.stack([facts, shift_y(facts, -1), shift_y(facts, 2), shift_y(facts, 1)])
     across = swap_core(same)
-    mine = (lane == (y * 2 + c) * 16 + x * 4 + z).astype(F32)
-    seen = [jnp.sum(facts[:, 72:88, 0:128] * mine[None], axis=2) for facts in (same, across)]
-    turned = (jnp.concatenate(seen) > 0.5).astype(jnp.int32)
-    own = own_entries(slots, place)
+    pieces = gather_row(payload)
+    cells = laid([part[k, 65:66, 0:128] for part in (same, across) for k in range(4)])
+    cells = jnp.broadcast_to(cells[None], (16, 8, 128))
+    cells = lax.all_to_all(cells, ROW, split_axis=0, concat_axis=0, tiled=True)
     log_coupling = jnp.log2(coupling)
     error_row = obs_error[None, :]
 
     vec, body, two = (ROWS, 128), (BODY, 128), (128, 128)
-    keep, other, listed, store, kept_facts = first_operate(own, turned, log_coupling, pieces, same, across)
+    keep, other, listed, store, kept_facts = first_operate(place, tile_slots, log_coupling, pieces, cells, same, across)
     parts = reduce_col(keep, other)
     w0, diag = small_call(after_first, [vec, (8, 128)], (innovations, error_row), parts)
 

time: 179 us -> 180 us (level); the launches traced: 180 us -> 179 us
  Pallas kernels: 23.3 us -> 33.6 us
  starting transfers between devices: 66.1 us -> 56.8 us
  waiting for transfers between devices: 71.4 us -> 67.6 us
    ppermute x30 -> x27, waiting for transfers between devices: 38.8 us -> 28.3 us  [hop(): return lax.ppermute(a, ALL, along_row(stage, step))]
    all_to_all x0 -> x1, waiting for transfers between devices: none -> 9.53 us  [shards(): cells = lax.all_to_all(cells, ROW, split_axis=0, concat_axis=0, tiled=True)]
    ppermute x30 -> x27, starting transfers between devices: 34.7 us -> 25.3 us  [hop(): return lax.ppermute(a, ALL, along_row(stage, step))]
    pallas_call x1, Pallas kernels: 9.88 us -> 14.9 us  [first_operate(): pl.pallas_call(first_kernel, out_shape=[PART, PART, jax.ShapeDtypeStruct(...]
    ppermute x4, starting transfers between devices: 21.5 us -> 16.6 us  [swap_core(): return lax.ppermute(a, C, [(0, 1), (1, 0)])]
    all_to_all x0 -> x1, starting transfers between devices: none -> 4.09 us  [shards(): cells = lax.all_to_all(cells, ROW, split_axis=0, concat_axis=0, tiled=True)]
    ppermute x12, waiting for transfers between devices: 28 us -> 25.1 us  [shift_y(): return lax.ppermute(a, Y, [(i, (i + step) % 4) for i in range(4)])]
    unnamed x7 -> x11, local copies, waits for them, and re-layouts: 0.7 us -> 3.25 us
  transfers between devices with their start and end apart: 46 -> 44, of which waited for: 30 -> 24; matrix products, arithmetic and copies ran while one was open for 0% -> 1% of each run, Pallas kernels for 3% -> 5%
where the time goes in v3:
time: 180 us; the launch traced here: 179 us
  waiting for transfers between devices  67.6 us (38%)
  starting transfers between devices  56.8 us (32%)
  Pallas kernels  33.6 us (19%)
  blocking collectives  15.2 us (8%)
  local copies, waits for them, and re-layouts  3.97 us (2%)
    ppermute x27, waiting for transfers between devices, hop(): return lax.ppermute(a, ALL, along_row(stage, step))  28.3 us
    ppermute x27, starting transfers between devices, hop(): return lax.ppermute(a, ALL, along_row(stage, step))  25.3 us
    ppermute x12, waiting for transfers between devices, shift_y(): return lax.ppermute(a, Y, [(i, (i + step) % 4) for i in range(4)])  25.1 us
    ppermute x4, starting transfers between devices, swap_core(): return lax.ppermute(a, C, [(0, 1), (1, 0)])  16.6 us
    all_to_all x1, blocking collectives, to_everyone(): return lax.all_to_all(copies, axes, split_axis=0, concat_axis=0, tiled=True)  15.2 us
    pallas_call x1, Pallas kernels, first_operate(): pl.pallas_call(first_kernel, out_shape=[PART, PART, jax.ShapeDtypeStruct(...  14.9 us
    ppermute x12, starting transfers between devices, shift_y(): return lax.ppermute(a, Y, [(i, (i + step) % 4) for i in range(4)])  10.7 us
    all_to_all x1, waiting for transfers between devices, shards(): cells = lax.all_to_all(cells, ROW, split_axis=0, concat_axis=0, tiled=True)  9.53 us
  transfers between devices with their start and end apart: 44, of which 24 were waited for; matrix products, arithmetic and copies ran while one was open for 1% of the time, Pallas kernels for 5%

profile of v3, /device:TPU:1, one launch (start us, length us, event | category | flops | bytes accessed | tf_op | source)
XLA Modules:
  0.0 179.2 jit_solution(8614569299924112598)
XLA Ops:
  4.9 2.2 %collective-permute-start.11 = (f32[72,512]{1,0:T(8,128)S(1)}, f32[72,512]{1,0:T(8,128)S(1)}, u32[]{:S(2)}, u32[]{:S(2)}) collective-permute-start(f32[72,512]{1,0:T(8,128)S(1)} %get-tuple-element.27), channel_id=1, source_target_pairs={{0,2},{2,4},{4,6},{6,0},{1,3},{3,5},{5,7},{7,1},{8,10},{10,12},{12... | collective-permute-start | bytes 442376 | tf_op jit(solution)/shard_map/ppermute | solution.py:69
  7.1 2.6 %collective-permute-start.10 = (f32[72,512]{1,0:T(8,128)S(1)}, f32[72,512]{1,0:T(8,128)S(1)}, u32[]{:S(2)}, u32[]{:S(2)}) collective-permute-start(f32[72,512]{1,0:T(8,128)S(1)} %get-tuple-element.27), channel_id=1, source_target_pairs={{0,4},{2,6},{4,0},{6,2},{1,5},{3,7},{5,1},{7,3},{8,12},{10,14},{12... | collective-permute-start | bytes 442376 | tf_op jit(solution)/shard_map/ppermute | solution.py:69
  9.7 1.6 collective-permute-start.2
  11.3 3.3 %collective-permute-start.1 = (f32[136,512]{1,0:T(8,128)S(1)}, f32[136,512]{1,0:T(8,128)S(1)}, u32[]{:S(2)}, u32[]{:S(2)}) collective-permute-start(f32[136,512]{1,0:T(8,128)S(1)} %get-tuple-element.26), channel_id=1, source_target_pairs={{0,64},{1,17},{2,66},{3,19},{4,68},{5,21},{6,70},{7,23},{8,72},{9,... | collective-permute-start | bytes 835592 | tf_op jit(solution)/shard_map/ppermute | solution.py:39
  16.1 5.2 %collective-permute-done = f32[136,512]{1,0:T(8,128)S(1)} collective-permute-done((f32[136,512]{1,0:T(8,128)S(1)}, f32[136,512]{1,0:T(8,128)S(1)}, u32[]{:S(2)}, u32[]{:S(2)}) %collective-permute-start) | collective-permute-done | bytes 278560 | tf_op jit(solution)/shard_map/ppermute | solution.py:39
  22.4 1.3 collective-permute-start.5
  23.7 1.5 collective-permute-start.4
  25.3 3.0 %collective-permute-start.12 = (f32[4,72,512]{2,1,0:T(8,128)S(1)}, f32[4,72,512]{2,1,0:T(8,128)S(1)}, u32[]{:S(2)}, u32[]{:S(2)}) collective-permute-start(f32[4,72,512]{2,1,0:T(8,128)S(1)} %pad_maximum_fusion.same), channel_id=1, source_target_pairs={{0,1},{1,0},{2,3},{3,2},{4,5},{5,4},{6,7},{7,6},{8,9},{9,8},{10,11... | collective-permute-start | bytes 1769480 | tf_op jit(solution)/shard_map/ppermute | solution.py:65
  28.3 2.4 %collective-permute-start.3 = (f32[2,136,512]{2,1,0:T(8,128)S(1)}, f32[2,136,512]{2,1,0:T(8,128)}, u32[]{:S(2)}, u32[]{:S(2)}) collective-permute-start(f32[2,136,512]{2,1,0:T(8,128)S(1)} %pad_maximum_fusion.1.p0), channel_id=1, source_target_pairs={{0,24},{1,97},{2,26},{3,99},{4,28},{5,101},{6,30},{7,103},{8,0},{9... | collective-permute-start | bytes 1671176 | tf_op jit(solution)/shard_map/ppermute | solution.py:39
  30.7 1.6 collective-permute-done.5.p6
  32.5 2.6 %collective-permute-start.7 = (f32[2,136,512]{2,1,0:T(8,128)}, f32[2,136,512]{2,1,0:T(8,128)}, u32[]{:S(2)}, u32[]{:S(2)}) collective-permute-start(f32[2,136,512]{2,1,0:T(8,128)} %collective-permute-done.4.p3), channel_id=1, source_target_pairs={{0,24},{1,97},{2,26},{3,99},{4,28},{5,101},{6,30},{7,103},{8,0},{9... | collective-permute-start | bytes 1671176 | tf_op jit(solution)/shard_map/ppermute | solution.py:39
  35.8 4.1 %all-to-all-start = ((f32[16,8,128]{2,1,0:T(8,128)}), f32[16,8,128]{2,1,0:T(8,128)S(1)}, u32[]{:S(2)}, u32[]{:S(2)}) async-start(f32[16,8,128]{2,1,0:T(8,128)} %broadcast_in_dim.47), calls=%async_computation | async-start | bytes 131072 | tf_op jit(solution)/shard_map/all_to_all | solution.py:581
  40.0 9.5 %all-to-all-done.cells = f32[16,8,128]{2,1,0:T(8,128)S(1)} async-done(((f32[16,8,128]{2,1,0:T(8,128)}), f32[16,8,128]{2,1,0:T(8,128)S(1)}, u32[]{:S(2)}, u32[]{:S(2)}) %all-to-all-start) | async-done | bytes 65568 | tf_op jit(solution)/shard_map/all_to_all | solution.py:581
  49.5 14.9 %shard_map.78 = (f32[4,264,128]{2,1,0:T(8,128)S(1)}, f32[4,264,128]{2,1,0:T(8,128)S(1)}, s32[144]{0:T(256)S(1)}, bf16[48,2,512,512]{3,2,1,0:T(8,128)(2,1)}, f32[24,72,512]{2,1,0:T(8,128)S(1)}) custom-call(s32[4]{0:T(128)S(1)} %pad_add_fusion.1.place_ref, s32[1,1,8,3]{3,2,1,0:T(8,128)S(1)} %copy.13.slots_ref, f32[2,2]{1,0:T(2,128)S(1)} %log_multiply_fusion.lc_ref, ...), custom_call_target="tpu_custom_call" | custom-call | flops 8000000000 | bytes 20000000 | tf_op jit(solution)/shard_map/pallas_call | solution.py:504
  64.5 3.3 %collective-permute-start.13 = (f32[4,264,128]{2,1,0:T(8,128)S(1)}, f32[4,264,128]{2,1,0:T(8,128)S(1)}, u32[]{:S(2)}, u32[]{:S(2)}) collective-permute-start(f32[4,264,128]{2,1,0:T(8,128)S(1)} %get-tuple-element.30), channel_id=1, source_target_pairs={{0,1},{1,0},{2,3},{3,2},{4,5},{5,4},{6,7},{7,6},{8,9},{9,8},{10,11... | collective-permute-start | bytes 1622024 | tf_op jit(solution)/shard_map/ppermute | solution.py:65
  67.8 1.6 collective-permute-done.13.b
  69.6 1.5 collective-permute-start.14
  71.0 4.8 %collective-permute-done.16 = f32[264,128]{1,0:T(8,128)S(1)} collective-permute-done((f32[264,128]{1,0:T(8,128)S(1)}, f32[264,128]{1,0:T(8,128)S(1)}, u32[]{:S(2)}, u32[]{:S(2)}) %collective-permute-start.16) | collective-permute-done | bytes 135200 | tf_op jit(solution)/shard_map/ppermute | solution.py:69
  75.8 3.6 %collective-permute-done.14 = f32[264,128]{1,0:T(8,128)S(1)} collective-permute-done((f32[264,128]{1,0:T(8,128)S(1)}, f32[264,128]{1,0:T(8,128)S(1)}, u32[]{:S(2)}, u32[]{:S(2)}) %collective-permute-start.14) | collective-permute-done | bytes 135200 | tf_op jit(solution)/shard_map/ppermute | solution.py:69
  79.6 1.4 collective-permute-start.17
  81.1 1.2 collective-permute-start.20
  82.3 1.5 collective-permute-done.17
  83.9 4.0 %collective-permute-done.21 = f32[264,128]{1,0:T(8,128)S(1)} collective-permute-done((f32[264,128]{1,0:T(8,128)S(1)}, f32[264,128]{1,0:T(8,128)S(1)}, u32[]{:S(2)}, u32[]{:S(2)}) %collective-permute-start.21) | collective-permute-done | bytes 135200 | tf_op jit(solution)/shard_map/ppermute | solution.py:39
  88.4 1.1 collective-permute-start.25
  89.5 2.2 %collective-permute-done.18.p6 = f32[2,264,128]{2,1,0:T(8,128)S(1)} collective-permute-done((f32[2,264,128]{2,1,0:T(8,128)S(1)}, f32[2,264,128]{2,1,0:T(8,128)S(1)}, u32[]{:S(2)}, u32[]{:S(2)}) %collective-permute-start.18) | collective-permute-done | bytes 270368 | tf_op jit(solution)/shard_map/ppermute | solution.py:39
  91.7 1.9 %collective-permute-done.22.p3 = f32[2,264,128]{2,1,0:T(8,128)S(1)} collective-permute-done((f32[2,264,128]{2,1,0:T(8,128)S(1)}, f32[2,264,128]{2,1,0:T(8,128)S(1)}, u32[]{:S(2)}, u32[]{:S(2)}) %collective-permute-start.22) | collective-permute-done | bytes 270368 | tf_op jit(solution)/shard_map/ppermute | solution.py:39
  94.5 1.7 collective-permute-done.24.p2
  96.1 4.3 %shard_map.80.near_ref = f32[8,264,128]{2,1,0:T(8,128)S(1)} custom-call(s32[144]{0:T(256)S(1)} %get-tuple-element.28.list_ref, f32[2,2]{1,0:T(2,128)S(1)} %log_multiply_fusion.lc_ref, f32[2,264,128]{2,1,0:T(8,128)S(1)} %pad_maximum_fusion.3.p0, f32[2,264,128]{2,1,0:T(8,128)S(1)} %pad_maximum_fusion.4.p1, f32[2,264,128]{2,1,0:T(8,128)S(1)} %collective-permute-done.24.p2, ...), custom_call_target="tpu_custom_call" | custom-call | flops 3000000000 | bytes 12000000 | tf_op jit(solution)/shard_map/pallas_call | solution.py:548
  100.5 3.8 %shard_map.81 = (f32[4,264,128]{2,1,0:T(8,128)S(1)}, f32[4,264,128]{2,1,0:T(8,128)S(1)}) custom-call(s32[144]{0:T(256)S(1)} %get-tuple-element.28.list_ref, f32[2,2]{1,0:T(2,128)S(1)} %log_multiply_fusion.lc_ref, f32[2,264,128]{2,1,0:T(8,128)S(1)} %collective-permute-done.19.p4, f32[2,264,128]{2,1,0:T(8,128)S(1)} %collective-permute-done.23.p5, ...), custom_call_target="tpu_custom_call" | custom-call | flops 1000000000 | bytes 6000000 | tf_op jit(solution)/shard_map/pallas_call | solution.py:557
  104.3 5.6 %collective-permute-start.26 = (f32[4,264,128]{2,1,0:T(8,128)S(1)}, f32[4,264,128]{2,1,0:T(8,128)S(1)}, u32[]{:S(2)}, u32[]{:S(2)}) collective-permute-start(f32[4,264,128]{2,1,0:T(8,128)S(1)} %get-tuple-element.35), channel_id=1, source_target_pairs={{0,1},{1,0},{2,3},{3,2},{4,5},{5,4},{6,7},{7,6},{8,9},{9,8},{10,11... | collective-permute-start | bytes 1622024 | tf_op jit(solution)/shard_map/ppermute | solution.py:65
  109.9 1.6 collective-permute-done.26.b
  111.6 1.5 collective-permute-start.27
  113.1 4.8 %collective-permute-done.29 = f32[264,128]{1,0:T(8,128)S(1)} collective-permute-done((f32[264,128]{1,0:T(8,128)S(1)}, f32[264,128]{1,0:T(8,128)S(1)}, u32[]{:S(2)}, u32[]{:S(2)}) %collective-permute-start.29) | collective-permute-done | bytes 135200 | tf_op jit(solution)/shard_map/ppermute | solution.py:69
  117.9 3.6 %collective-permute-done.27 = f32[264,128]{1,0:T(8,128)S(1)} collective-permute-done((f32[264,128]{1,0:T(8,128)S(1)}, f32[264,128]{1,0:T(8,128)S(1)}, u32[]{:S(2)}, u32[]{:S(2)}) %collective-permute-start.27) | collective-permute-done | bytes 135200 | tf_op jit(solution)/shard_map/ppermute | solution.py:69
  123.7 2.2 %collective-permute-done.30 = f32[264,128]{1,0:T(8,128)S(1)} collective-permute-done((f32[264,128]{1,0:T(8,128)S(1)}, f32[264,128]{1,0:T(8,128)S(1)}, u32[]{:S(2)}, u32[]{:S(2)}) %collective-permute-start.30) | collective-permute-done | bytes 135200 | tf_op jit(solution)/shard_map/ppermute | solution.py:39
  126.0 3.2 %collective-permute-done.34 = f32[264,128]{1,0:T(8,128)S(1)} collective-permute-done((f32[264,128]{1,0:T(8,128)S(1)}, f32[264,128]{1,0:T(8,128)S(1)}, u32[]{:S(2)}, u32[]{:S(2)}) %collective-permute-start.34) | collective-permute-done | bytes 135200 | tf_op jit(solution)/shard_map/ppermute | solution.py:39
  129.6 2.3 %collective-permute-start.37 = (f32[2,264,128]{2,1,0:T(8,128)S(1)}, f32[2,264,128]{2,1,0:T(8,128)S(1)}, u32[]{:S(2)}, u32[]{:S(2)}) collective-permute-start(f32[2,264,128]{2,1,0:T(8,128)S(1)} %pad_maximum_fusion.5.p0), channel_id=1, source_target_pairs={{0,24},{1,97},{2,26},{3,99},{4,28},{5,101},{6,30},{7,103},{8,0},{9... | collective-permute-start | bytes 811016 | tf_op jit(solution)/shard_map/ppermute | solution.py:39
  131.9 1.9 %collective-permute-done.31.p6 = f32[2,264,128]{2,1,0:T(8,128)S(1)} collective-permute-done((f32[2,264,128]{2,1,0:T(8,128)S(1)}, f32[2,264,128]{2,1,0:T(8,128)S(1)}, u32[]{:S(2)}, u32[]{:S(2)}) %collective-permute-start.31) | collective-permute-done | bytes 270368 | tf_op jit(solution)/shard_map/ppermute | solution.py:39
  134.7 1.8 collective-permute-start.36
  136.4 1.4 collective-permute-done.37.p2
  138.4 4.3 %shard_map.83.near_ref = f32[8,264,128]{2,1,0:T(8,128)S(1)} custom-call(s32[144]{0:T(256)S(1)} %get-tuple-element.28.list_ref, f32[2,2]{1,0:T(2,128)S(1)} %log_multiply_fusion.lc_ref, f32[2,264,128]{2,1,0:T(8,128)S(1)} %pad_maximum_fusion.5.p0, f32[2,264,128]{2,1,0:T(8,128)S(1)} %pad_maximum_fusion.6.p1, f32[2,264,128]{2,1,0:T(8,128)S(1)} %collective-permute-done.37.p2, ...), custom_call_target="tpu_custom_call" | custom-call | flops 3000000000 | bytes 12000000 | tf_op jit(solution)/shard_map/pallas_call | solution.py:548
  142.7 3.8 %shard_map.84 = (f32[4,264,128]{2,1,0:T(8,128)S(1)}, f32[4,264,128]{2,1,0:T(8,128)S(1)}) custom-call(s32[144]{0:T(256)S(1)} %get-tuple-element.28.list_ref, f32[2,2]{1,0:T(2,128)S(1)} %log_multiply_fusion.lc_ref, f32[2,264,128]{2,1,0:T(8,128)S(1)} %collective-permute-done.32.p4, f32[2,264,128]{2,1,0:T(8,128)S(1)} %collective-permute-done.36.p5, ...), custom_call_target="tpu_custom_call" | custom-call | flops 1000000000 | bytes 6000000 | tf_op jit(solution)/shard_map/pallas_call | solution.py:557
  146.5 4.7 %collective-permute-start.39 = (f32[4,264,128]{2,1,0:T(8,128)S(1)}, f32[4,264,128]{2,1,0:T(8,128)S(1)}, u32[]{:S(2)}, u32[]{:S(2)}) collective-permute-start(f32[4,264,128]{2,1,0:T(8,128)S(1)} %get-tuple-element.39), channel_id=1, source_target_pairs={{0,1},{1,0},{2,3},{3,2},{4,5},{5,4},{6,7},{7,6},{8,9},{9,8},{10,11... | collective-permute-start | bytes 1622024 | tf_op jit(solution)/shard_map/ppermute | solution.py:65
  151.2 1.6 collective-permute-done.39.b
  153.0 1.5 collective-permute-start.40
  154.4 4.8 %collective-permute-done.42 = f32[264,128]{1,0:T(8,128)S(1)} collective-permute-done((f32[264,128]{1,0:T(8,128)S(1)}, f32[264,128]{1,0:T(8,128)S(1)}, u32[]{:S(2)}, u32[]{:S(2)}) %collective-permute-start.42) | collective-permute-done | bytes 135200 | tf_op jit(solution)/shard_map/ppermute | solution.py:69
  159.2 3.6 %collective-permute-done.40 = f32[264,128]{1,0:T(8,128)S(1)} collective-permute-done((f32[264,128]{1,0:T(8,128)S(1)}, f32[264,128]{1,0:T(8,128)S(1)}, u32[]{:S(2)}, u32[]{:S(2)}) %collective-permute-start.40) | collective-permute-done | bytes 135200 | tf_op jit(solution)/shard_map/ppermute | solution.py:69
  163.2 15.2 %all_to_all.10 = f32[128,1,128]{2,1,0:T(1,128)S(1)} all-to-all(f32[128,1,128]{2,1,0:T(1,128)S(1)} %broadcast_in_dim.59), channel_id=1, replica_groups=mesh['row_0'=4,'row_1'=4,'col_0'=4,'col_1'=2] {'row_0','row_1','col_0','..., dimensions={0} | all-to-all | bytes 131072 | tf_op jit(solution)/shard_map/all_to_all | solution.py:570
  (84 shorter events, 15.6 us)
Async XLA Ops:
  1.4 0.9 copy-start
  2.3 0.9 copy-start.2
  4.9 20.4 %collective-permute-start.11 = (f32[72,512]{1,0:T(8,128)S(1)}, f32[72,512]{1,0:T(8,128)S(1)}, u32[]{:S(2)}, u32[]{:S(2)}) collective-permute-start(f32[72,512]{1,0:T(8,128)S(1)} %get-tuple-element.27), channel_id=1, source_target_pairs={{0,2},{2,4},{4,6},{6,0},{1,3},{3,5},{5,7},{7,1},{8,10},{10,12},{12... | collective-permute-start | bytes 442376 | tf_op jit(solution)/shard_map/ppermute | solution.py:69
  7.1 18.2 %collective-permute-start.10 = (f32[72,512]{1,0:T(8,128)S(1)}, f32[72,512]{1,0:T(8,128)S(1)}, u32[]{:S(2)}, u32[]{:S(2)}) collective-permute-start(f32[72,512]{1,0:T(8,128)S(1)} %get-tuple-element.27), channel_id=1, source_target_pairs={{0,4},{2,6},{4,0},{6,2},{1,5},{3,7},{5,1},{7,3},{8,12},{10,14},{12... | collective-permute-start | bytes 442376 | tf_op jit(solution)/shard_map/ppermute | solution.py:69
  9.7 12.7 %collective-permute-start.2 = (f32[136,512]{1,0:T(8,128)S(1)}, f32[136,512]{1,0:T(8,128)S(1)}, u32[]{:S(2)}, u32[]{:S(2)}) collective-permute-start(f32[136,512]{1,0:T(8,128)S(1)} %get-tuple-element.26), channel_id=1, source_target_pairs={{0,32},{1,9},{2,34},{3,11},{4,36},{5,13},{6,38},{7,15},{8,40},{9,1... | collective-permute-start | bytes 835592 | tf_op jit(solution)/shard_map/ppermute | solution.py:39
  11.3 12.3 %collective-permute-start.1 = (f32[136,512]{1,0:T(8,128)S(1)}, f32[136,512]{1,0:T(8,128)S(1)}, u32[]{:S(2)}, u32[]{:S(2)}) collective-permute-start(f32[136,512]{1,0:T(8,128)S(1)} %get-tuple-element.26), channel_id=1, source_target_pairs={{0,64},{1,17},{2,66},{3,19},{4,68},{5,21},{6,70},{7,23},{8,72},{9,... | collective-permute-start | bytes 835592 | tf_op jit(solution)/shard_map/ppermute | solution.py:39
  14.6 6.6 %collective-permute-start = (f32[136,512]{1,0:T(8,128)S(1)}, f32[136,512]{1,0:T(8,128)S(1)}, u32[]{:S(2)}, u32[]{:S(2)}) collective-permute-start(f32[136,512]{1,0:T(8,128)S(1)} %get-tuple-element.26), channel_id=1, source_target_pairs={{0,96},{1,25},{2,98},{3,27},{4,100},{5,29},{6,102},{7,31},{8,104},... | collective-permute-start | bytes 835592 | tf_op jit(solution)/shard_map/ppermute | solution.py:39
  21.2 4.0 %collective-permute-start.9 = (f32[72,512]{1,0:T(8,128)S(1)}, f32[72,512]{1,0:T(8,128)S(1)}, u32[]{:S(2)}, u32[]{:S(2)}) collective-permute-start(f32[72,512]{1,0:T(8,128)S(1)} %get-tuple-element.27), channel_id=1, source_target_pairs={{0,6},{2,0},{4,2},{6,4},{1,7},{3,1},{5,3},{7,5},{8,14},{10,8},{12,... | collective-permute-start | bytes 442376 | tf_op jit(solution)/shard_map/ppermute | solution.py:69
  22.4 10.0 %collective-permute-start.5 = (f32[2,136,512]{2,1,0:T(8,128)S(1)}, f32[2,136,512]{2,1,0:T(8,128)S(1)}, u32[]{:S(2)}, u32[]{:S(2)}) collective-permute-start(f32[2,136,512]{2,1,0:T(8,128)S(1)} %pad_maximum_fusion.1.p0), channel_id=1, source_target_pairs={{0,8},{1,33},{2,10},{3,35},{4,12},{5,37},{6,14},{7,39},{8,16},{9,4... | collective-permute-start | bytes 1671176 | tf_op jit(solution)/shard_map/ppermute | solution.py:39
  23.7 8.9 %collective-permute-start.4 = (f32[2,136,512]{2,1,0:T(8,128)S(1)}, f32[2,136,512]{2,1,0:T(8,128)}, u32[]{:S(2)}, u32[]{:S(2)}) collective-permute-start(f32[2,136,512]{2,1,0:T(8,128)S(1)} %pad_maximum_fusion.2.p1), channel_id=1, source_target_pairs={{0,24},{1,97},{2,26},{3,99},{4,28},{5,101},{6,30},{7,103},{8,0},{9... | collective-permute-start | bytes 1671176 | tf_op jit(solution)/shard_map/ppermute | solution.py:39
  25.3 9.8 %collective-permute-start.12 = (f32[4,72,512]{2,1,0:T(8,128)S(1)}, f32[4,72,512]{2,1,0:T(8,128)S(1)}, u32[]{:S(2)}, u32[]{:S(2)}) collective-permute-start(f32[4,72,512]{2,1,0:T(8,128)S(1)} %pad_maximum_fusion.same), channel_id=1, source_target_pairs={{0,1},{1,0},{2,3},{3,2},{4,5},{5,4},{6,7},{7,6},{8,9},{9,8},{10,11... | collective-permute-start | bytes 1769480 | tf_op jit(solution)/shard_map/ppermute | solution.py:65
  28.3 21.2 %collective-permute-start.3 = (f32[2,136,512]{2,1,0:T(8,128)S(1)}, f32[2,136,512]{2,1,0:T(8,128)}, u32[]{:S(2)}, u32[]{:S(2)}) collective-permute-start(f32[2,136,512]{2,1,0:T(8,128)S(1)} %pad_maximum_fusion.1.p0), channel_id=1, source_target_pairs={{0,24},{1,97},{2,26},{3,99},{4,28},{5,101},{6,30},{7,103},{8,0},{9... | collective-permute-start | bytes 1671176 | tf_op jit(solution)/shard_map/ppermute | solution.py:39
  30.7 18.8 %collective-permute-start.8 = (f32[2,136,512]{2,1,0:T(8,128)S(1)}, f32[2,136,512]{2,1,0:T(8,128)}, u32[]{:S(2)}, u32[]{:S(2)}) collective-permute-start(f32[2,136,512]{2,1,0:T(8,128)S(1)} %pad_maximum_fusion.2.p1), channel_id=1, source_target_pairs={{0,8},{1,33},{2,10},{3,35},{4,12},{5,37},{6,14},{7,39},{8,16},{9,4... | collective-permute-start | bytes 1671176 | tf_op jit(solution)/shard_map/ppermute | solution.py:39
  32.3 17.2 %collective-permute-start.6 = (f32[2,136,512]{2,1,0:T(8,128)S(1)}, f32[2,136,512]{2,1,0:T(8,128)}, u32[]{:S(2)}, u32[]{:S(2)}) collective-permute-start(f32[2,136,512]{2,1,0:T(8,128)S(1)} %collective-permute-done.5.p6), channel_id=1, source_target_pairs={{0,8},{1,33},{2,10},{3,35},{4,12},{5,37},{6,14},{7,39},{8,16},{9,4... | collective-permute-start | bytes 1671176 | tf_op jit(solution)/shard_map/ppermute | solution.py:39
  32.5 17.0 %collective-permute-start.7 = (f32[2,136,512]{2,1,0:T(8,128)}, f32[2,136,512]{2,1,0:T(8,128)}, u32[]{:S(2)}, u32[]{:S(2)}) collective-permute-start(f32[2,136,512]{2,1,0:T(8,128)} %collective-permute-done.4.p3), channel_id=1, source_target_pairs={{0,24},{1,97},{2,26},{3,99},{4,28},{5,101},{6,30},{7,103},{8,0},{9... | collective-permute-start | bytes 1671176 | tf_op jit(solution)/shard_map/ppermute | solution.py:39
  35.8 13.7 %all-to-all-start = ((f32[16,8,128]{2,1,0:T(8,128)}), f32[16,8,128]{2,1,0:T(8,128)S(1)}, u32[]{:S(2)}, u32[]{:S(2)}) async-start(f32[16,8,128]{2,1,0:T(8,128)} %broadcast_in_dim.47), calls=%async_computation | async-start | bytes 131072 | tf_op jit(solution)/shard_map/all_to_all | solution.py:581
  40.0 39.4 %copy-start.1 = (f32[64,512]{1,0:T(8,128)S(1)}, f32[64,512]{1,0:T(8,128)}, u32[]{:S(2)}) copy-start(f32[64,512]{1,0:T(8,128)} %r_ref.5) | copy-start | bytes 393220
  40.0 39.4 %copy-start.4 = (f32[512]{0:T(512)S(1)}, f32[512]{0:T(512)}, u32[]{:S(2)}) copy-start(f32[512]{0:T(512)} %param.9) | copy-start | bytes 6148
  64.5 4.9 %collective-permute-start.13 = (f32[4,264,128]{2,1,0:T(8,128)S(1)}, f32[4,264,128]{2,1,0:T(8,128)S(1)}, u32[]{:S(2)}, u32[]{:S(2)}) collective-permute-start(f32[4,264,128]{2,1,0:T(8,128)S(1)} %get-tuple-element.30), channel_id=1, source_target_pairs={{0,1},{1,0},{2,3},{3,2},{4,5},{5,4},{6,7},{7,6},{8,9},{9,8},{10,11... | collective-permute-start | bytes 1622024 | tf_op jit(solution)/shard_map/ppermute | solution.py:65
  69.4 6.4 %collective-permute-start.16 = (f32[264,128]{1,0:T(8,128)S(1)}, f32[264,128]{1,0:T(8,128)S(1)}, u32[]{:S(2)}, u32[]{:S(2)}) collective-permute-start(f32[264,128]{1,0:T(8,128)S(1)} %get-tuple-element.56), channel_id=1, source_target_pairs={{0,4},{2,6},{4,0},{6,2},{1,5},{3,7},{5,1},{7,3},{8,12},{10,14},{12... | collective-permute-start | bytes 405512 | tf_op jit(solution)/shard_map/ppermute | solution.py:69
  69.5 6.3 %collective-permute-start.15 = (f32[264,128]{1,0:T(8,128)S(1)}, f32[264,128]{1,0:T(8,128)S(1)}, u32[]{:S(2)}, u32[]{:S(2)}) collective-permute-start(f32[264,128]{1,0:T(8,128)S(1)} %get-tuple-element.57), channel_id=1, source_target_pairs={{0,6},{2,0},{4,2},{6,4},{1,7},{3,1},{5,3},{7,5},{8,14},{10,8},{12,... | collective-permute-start | bytes 405512 | tf_op jit(solution)/shard_map/ppermute | solution.py:69
  69.6 9.8 %collective-permute-start.14 = (f32[264,128]{1,0:T(8,128)S(1)}, f32[264,128]{1,0:T(8,128)S(1)}, u32[]{:S(2)}, u32[]{:S(2)}) collective-permute-start(f32[264,128]{1,0:T(8,128)S(1)} %get-tuple-element.58), channel_id=1, source_target_pairs={{0,2},{2,4},{4,6},{6,0},{1,3},{3,5},{5,7},{7,1},{8,10},{10,12},{12... | collective-permute-start | bytes 405512 | tf_op jit(solution)/shard_map/ppermute | solution.py:69
  79.6 4.2 %collective-permute-start.17 = (f32[264,128]{1,0:T(8,128)S(1)}, f32[264,128]{1,0:T(8,128)S(1)}, u32[]{:S(2)}, u32[]{:S(2)}) collective-permute-start(f32[264,128]{1,0:T(8,128)S(1)} %get-tuple-element.31.w_ref.w0_ref), channel_id=1, source_target_pairs={{0,96},{1,25},{2,98},{3,27},{4,100},{5,29},{6,102},{7,31},{8,104},... | collective-permute-start | bytes 405512 | tf_op jit(solution)/shard_map/ppermute | solution.py:39
  81.0 6.8 %collective-permute-start.21 = (f32[264,128]{1,0:T(8,128)S(1)}, f32[264,128]{1,0:T(8,128)S(1)}, u32[]{:S(2)}, u32[]{:S(2)}) collective-permute-start(f32[264,128]{1,0:T(8,128)S(1)} %get-tuple-element.31.w_ref.w0_ref), channel_id=1, source_target_pairs={{0,32},{1,9},{2,34},{3,11},{4,36},{5,13},{6,38},{7,15},{8,40},{9,1... | collective-permute-start | bytes 405512 | tf_op jit(solution)/shard_map/ppermute | solution.py:39
  81.1 6.8 %collective-permute-start.20 = (f32[264,128]{1,0:T(8,128)S(1)}, f32[264,128]{1,0:T(8,128)S(1)}, u32[]{:S(2)}, u32[]{:S(2)}) collective-permute-start(f32[264,128]{1,0:T(8,128)S(1)} %get-tuple-element.31.w_ref.w0_ref), channel_id=1, source_target_pairs={{0,64},{1,17},{2,66},{3,19},{4,68},{5,21},{6,70},{7,23},{8,72},{9,... | collective-permute-start | bytes 405512 | tf_op jit(solution)/shard_map/ppermute | solution.py:39
  83.8 7.9 %collective-permute-start.18 = (f32[2,264,128]{2,1,0:T(8,128)S(1)}, f32[2,264,128]{2,1,0:T(8,128)S(1)}, u32[]{:S(2)}, u32[]{:S(2)}) collective-permute-start(f32[2,264,128]{2,1,0:T(8,128)S(1)} %pad_maximum_fusion.3.p0), channel_id=1, source_target_pairs={{0,8},{1,33},{2,10},{3,35},{4,12},{5,37},{6,14},{7,39},{8,16},{9,4... | collective-permute-start | bytes 811016 | tf_op jit(solution)/shard_map/ppermute | solution.py:39
  87.9 5.7 %collective-permute-start.22 = (f32[2,264,128]{2,1,0:T(8,128)S(1)}, f32[2,264,128]{2,1,0:T(8,128)S(1)}, u32[]{:S(2)}, u32[]{:S(2)}) collective-permute-start(f32[2,264,128]{2,1,0:T(8,128)S(1)} %pad_maximum_fusion.4.p1), channel_id=1, source_target_pairs={{0,24},{1,97},{2,26},{3,99},{4,28},{5,101},{6,30},{7,103},{8,0},{9... | collective-permute-start | bytes 811016 | tf_op jit(solution)/shard_map/ppermute | solution.py:39
  87.9 8.2 %collective-permute-start.24 = (f32[2,264,128]{2,1,0:T(8,128)S(1)}, f32[2,264,128]{2,1,0:T(8,128)S(1)}, u32[]{:S(2)}, u32[]{:S(2)}) collective-permute-start(f32[2,264,128]{2,1,0:T(8,128)S(1)} %pad_maximum_fusion.3.p0), channel_id=1, source_target_pairs={{0,24},{1,97},{2,26},{3,99},{4,28},{5,101},{6,30},{7,103},{8,0},{9... | collective-permute-start | bytes 811016 | tf_op jit(solution)/shard_map/ppermute | solution.py:39
  88.4 7.7 %collective-permute-start.25 = (f32[2,264,128]{2,1,0:T(8,128)S(1)}, f32[2,264,128]{2,1,0:T(8,128)S(1)}, u32[]{:S(2)}, u32[]{:S(2)}) collective-permute-start(f32[2,264,128]{2,1,0:T(8,128)S(1)} %pad_maximum_fusion.4.p1), channel_id=1, source_target_pairs={{0,8},{1,33},{2,10},{3,35},{4,12},{5,37},{6,14},{7,39},{8,16},{9,4... | collective-permute-start | bytes 811016 | tf_op jit(solution)/shard_map/ppermute | solution.py:39
  91.7 8.8 %collective-permute-start.19 = (f32[2,264,128]{2,1,0:T(8,128)S(1)}, f32[2,264,128]{2,1,0:T(8,128)S(1)}, u32[]{:S(2)}, u32[]{:S(2)}) collective-permute-start(f32[2,264,128]{2,1,0:T(8,128)S(1)} %collective-permute-done.18.p6), channel_id=1, source_target_pairs={{0,8},{1,33},{2,10},{3,35},{4,12},{5,37},{6,14},{7,39},{8,16},{9,4... | collective-permute-start | bytes 811016 | tf_op jit(solution)/shard_map/ppermute | solution.py:39
  93.5 6.9 %collective-permute-start.23 = (f32[2,264,128]{2,1,0:T(8,128)S(1)}, f32[2,264,128]{2,1,0:T(8,128)S(1)}, u32[]{:S(2)}, u32[]{:S(2)}) collective-permute-start(f32[2,264,128]{2,1,0:T(8,128)S(1)} %collective-permute-done.22.p3), channel_id=1, source_target_pairs={{0,24},{1,97},{2,26},{3,99},{4,28},{5,101},{6,30},{7,103},{8,0},{9... | collective-permute-start | bytes 811016 | tf_op jit(solution)/shard_map/ppermute | solution.py:39
  104.3 7.2 %collective-permute-start.26 = (f32[4,264,128]{2,1,0:T(8,128)S(1)}, f32[4,264,128]{2,1,0:T(8,128)S(1)}, u32[]{:S(2)}, u32[]{:S(2)}) collective-permute-start(f32[4,264,128]{2,1,0:T(8,128)S(1)} %get-tuple-element.35), channel_id=1, source_target_pairs={{0,1},{1,0},{2,3},{3,2},{4,5},{5,4},{6,7},{7,6},{8,9},{9,8},{10,11... | collective-permute-start | bytes 1622024 | tf_op jit(solution)/shard_map/ppermute | solution.py:65
  111.5 6.4 %collective-permute-start.29 = (f32[264,128]{1,0:T(8,128)S(1)}, f32[264,128]{1,0:T(8,128)S(1)}, u32[]{:S(2)}, u32[]{:S(2)}) collective-permute-start(f32[264,128]{1,0:T(8,128)S(1)} %get-tuple-element.53), channel_id=1, source_target_pairs={{0,4},{2,6},{4,0},{6,2},{1,5},{3,7},{5,1},{7,3},{8,12},{10,14},{12... | collective-permute-start | bytes 405512 | tf_op jit(solution)/shard_map/ppermute | solution.py:69
  111.6 6.3 %collective-permute-start.28 = (f32[264,128]{1,0:T(8,128)S(1)}, f32[264,128]{1,0:T(8,128)S(1)}, u32[]{:S(2)}, u32[]{:S(2)}) collective-permute-start(f32[264,128]{1,0:T(8,128)S(1)} %get-tuple-element.54), channel_id=1, source_target_pairs={{0,6},{2,0},{4,2},{6,4},{1,7},{3,1},{5,3},{7,5},{8,14},{10,8},{12,... | collective-permute-start | bytes 405512 | tf_op jit(solution)/shard_map/ppermute | solution.py:69
  111.6 9.8 %collective-permute-start.27 = (f32[264,128]{1,0:T(8,128)S(1)}, f32[264,128]{1,0:T(8,128)S(1)}, u32[]{:S(2)}, u32[]{:S(2)}) collective-permute-start(f32[264,128]{1,0:T(8,128)S(1)} %get-tuple-element.55), channel_id=1, source_target_pairs={{0,2},{2,4},{4,6},{6,0},{1,3},{3,5},{5,7},{7,1},{8,10},{10,12},{12... | collective-permute-start | bytes 405512 | tf_op jit(solution)/shard_map/ppermute | solution.py:69
  121.7 4.2 %collective-permute-start.30 = (f32[264,128]{1,0:T(8,128)S(1)}, f32[264,128]{1,0:T(8,128)S(1)}, u32[]{:S(2)}, u32[]{:S(2)}) collective-permute-start(f32[264,128]{1,0:T(8,128)S(1)} %get-tuple-element.37.w1_ref), channel_id=1, source_target_pairs={{0,96},{1,25},{2,98},{3,27},{4,100},{5,29},{6,102},{7,31},{8,104},... | collective-permute-start | bytes 405512 | tf_op jit(solution)/shard_map/ppermute | solution.py:39
  122.4 6.8 %collective-permute-start.34 = (f32[264,128]{1,0:T(8,128)S(1)}, f32[264,128]{1,0:T(8,128)S(1)}, u32[]{:S(2)}, u32[]{:S(2)}) collective-permute-start(f32[264,128]{1,0:T(8,128)S(1)} %get-tuple-element.37.w1_ref), channel_id=1, source_target_pairs={{0,32},{1,9},{2,34},{3,11},{4,36},{5,13},{6,38},{7,15},{8,40},{9,1... | collective-permute-start | bytes 405512 | tf_op jit(solution)/shard_map/ppermute | solution.py:39
  123.2 6.0 %collective-permute-start.33 = (f32[264,128]{1,0:T(8,128)S(1)}, f32[264,128]{1,0:T(8,128)S(1)}, u32[]{:S(2)}, u32[]{:S(2)}) collective-permute-start(f32[264,128]{1,0:T(8,128)S(1)} %get-tuple-element.37.w1_ref), channel_id=1, source_target_pairs={{0,64},{1,17},{2,66},{3,19},{4,68},{5,21},{6,70},{7,23},{8,72},{9,... | collective-permute-start | bytes 405512 | tf_op jit(solution)/shard_map/ppermute | solution.py:39
  125.9 7.8 %collective-permute-start.31 = (f32[2,264,128]{2,1,0:T(8,128)S(1)}, f32[2,264,128]{2,1,0:T(8,128)S(1)}, u32[]{:S(2)}, u32[]{:S(2)}) collective-permute-start(f32[2,264,128]{2,1,0:T(8,128)S(1)} %pad_maximum_fusion.5.p0), channel_id=1, source_target_pairs={{0,8},{1,33},{2,10},{3,35},{4,12},{5,37},{6,14},{7,39},{8,16},{9,4... | collective-permute-start | bytes 811016 | tf_op jit(solution)/shard_map/ppermute | solution.py:39
  129.3 5.4 %collective-permute-start.35 = (f32[2,264,128]{2,1,0:T(8,128)S(1)}, f32[2,264,128]{2,1,0:T(8,128)S(1)}, u32[]{:S(2)}, u32[]{:S(2)}) collective-permute-start(f32[2,264,128]{2,1,0:T(8,128)S(1)} %pad_maximum_fusion.6.p1), channel_id=1, source_target_pairs={{0,24},{1,97},{2,26},{3,99},{4,28},{5,101},{6,30},{7,103},{8,0},{9... | collective-permute-start | bytes 811016 | tf_op jit(solution)/shard_map/ppermute | solution.py:39
  129.6 8.3 %collective-permute-start.37 = (f32[2,264,128]{2,1,0:T(8,128)S(1)}, f32[2,264,128]{2,1,0:T(8,128)S(1)}, u32[]{:S(2)}, u32[]{:S(2)}) collective-permute-start(f32[2,264,128]{2,1,0:T(8,128)S(1)} %pad_maximum_fusion.5.p0), channel_id=1, source_target_pairs={{0,24},{1,97},{2,26},{3,99},{4,28},{5,101},{6,30},{7,103},{8,0},{9... | collective-permute-start | bytes 811016 | tf_op jit(solution)/shard_map/ppermute | solution.py:39
  131.9 6.5 %collective-permute-start.38 = (f32[2,264,128]{2,1,0:T(8,128)S(1)}, f32[2,264,128]{2,1,0:T(8,128)S(1)}, u32[]{:S(2)}, u32[]{:S(2)}) collective-permute-start(f32[2,264,128]{2,1,0:T(8,128)S(1)} %pad_maximum_fusion.6.p1), channel_id=1, source_target_pairs={{0,8},{1,33},{2,10},{3,35},{4,12},{5,37},{6,14},{7,39},{8,16},{9,4... | collective-permute-start | bytes 811016 | tf_op jit(solution)/shard_map/ppermute | solution.py:39
  133.8 8.9 %collective-permute-start.32 = (f32[2,264,128]{2,1,0:T(8,128)S(1)}, f32[2,264,128]{2,1,0:T(8,128)S(1)}, u32[]{:S(2)}, u32[]{:S(2)}) collective-permute-start(f32[2,264,128]{2,1,0:T(8,128)S(1)} %collective-permute-done.31.p6), channel_id=1, source_target_pairs={{0,8},{1,33},{2,10},{3,35},{4,12},{5,37},{6,14},{7,39},{8,16},{9,4... | collective-permute-start | bytes 811016 | tf_op jit(solution)/shard_map/ppermute | solution.py:39
  134.7 8.1 %collective-permute-start.36 = (f32[2,264,128]{2,1,0:T(8,128)S(1)}, f32[2,264,128]{2,1,0:T(8,128)S(1)}, u32[]{:S(2)}, u32[]{:S(2)}) collective-permute-start(f32[2,264,128]{2,1,0:T(8,128)S(1)} %collective-permute-done.35.p3), channel_id=1, source_target_pairs={{0,24},{1,97},{2,26},{3,99},{4,28},{5,101},{6,30},{7,103},{8,0},{9... | collective-permute-start | bytes 811016 | tf_op jit(solution)/shard_map/ppermute | solution.py:39
  146.5 6.2 %collective-permute-start.39 = (f32[4,264,128]{2,1,0:T(8,128)S(1)}, f32[4,264,128]{2,1,0:T(8,128)S(1)}, u32[]{:S(2)}, u32[]{:S(2)}) collective-permute-start(f32[4,264,128]{2,1,0:T(8,128)S(1)} %get-tuple-element.39), channel_id=1, source_target_pairs={{0,1},{1,0},{2,3},{3,2},{4,5},{5,4},{6,7},{7,6},{8,9},{9,8},{10,11... | collective-permute-start | bytes 1622024 | tf_op jit(solution)/shard_map/ppermute | solution.py:65
  152.8 6.4 %collective-permute-start.42 = (f32[264,128]{1,0:T(8,128)S(1)}, f32[264,128]{1,0:T(8,128)S(1)}, u32[]{:S(2)}, u32[]{:S(2)}) collective-permute-start(f32[264,128]{1,0:T(8,128)S(1)} %get-tuple-element.50), channel_id=1, source_target_pairs={{0,4},{2,6},{4,0},{6,2},{1,5},{3,7},{5,1},{7,3},{8,12},{10,14},{12... | collective-permute-start | bytes 405512 | tf_op jit(solution)/shard_map/ppermute | solution.py:69
  152.9 6.3 %collective-permute-start.41 = (f32[264,128]{1,0:T(8,128)S(1)}, f32[264,128]{1,0:T(8,128)S(1)}, u32[]{:S(2)}, u32[]{:S(2)}) collective-permute-start(f32[264,128]{1,0:T(8,128)S(1)} %get-tuple-element.51), channel_id=1, source_target_pairs={{0,6},{2,0},{4,2},{6,4},{1,7},{3,1},{5,3},{7,5},{8,14},{10,8},{12,... | collective-permute-start | bytes 405512 | tf_op jit(solution)/shard_map/ppermute | solution.py:69
  153.0 9.8 %collective-permute-start.40 = (f32[264,128]{1,0:T(8,128)S(1)}, f32[264,128]{1,0:T(8,128)S(1)}, u32[]{:S(2)}, u32[]{:S(2)}) collective-permute-start(f32[264,128]{1,0:T(8,128)S(1)} %get-tuple-element.52), channel_id=1, source_target_pairs={{0,2},{2,4},{4,6},{6,0},{1,3},{3,5},{5,7},{7,1},{8,10},{10,12},{12... | collective-permute-start | bytes 405512 | tf_op jit(solution)/shard_map/ppermute | solution.py:69
  (1 other events, 0.7 us)

commit v4 on v3

--- a/solution.py
+++ b/solution.py
@@ -481,7 +481,7 @@
         out_specs=[VMEM, VMEM],
         scratch_shapes=[pltpu.VMEM((1, TILE), jnp.int32), pltpu.SemaphoreType.DMA((3,))],
         compiler_params=pltpu.CompilerParams(vmem_limit_bytes=4 << 20),
-    )(slots, factors, component, values)
+    )(slots, *[pltpu.with_memory_space_constraint(v, pltpu.HBM) for v in (factors, component, values)])
 
 
 def laid(parts):

time: 180 us -> 173 us (0.961)
  starting transfers between devices: 56.8 us -> 68.9 us
  Pallas kernels: 33.6 us -> 22.9 us
  waiting for transfers between devices: 67.6 us -> 62.2 us
  local copies, waits for them, and re-layouts: 3.97 us -> 1.48 us
    ppermute x27, starting transfers between devices: 25.3 us -> 38 us  [hop(): return lax.ppermute(a, ALL, along_row(stage, step))]
    pallas_call x1, Pallas kernels: 14.9 us -> 9.15 us  [first_operate(): pl.pallas_call(first_kernel, out_shape=[PART, PART, jax.ShapeDtypeStruct(...]
    ppermute x27, waiting for transfers between devices: 28.3 us -> 24.8 us  [hop(): return lax.ppermute(a, ALL, along_row(stage, step))]
    pallas_call x2, Pallas kernels: 8.59 us -> 5.53 us  [later_operate(): pl.pallas_call(near_kernel, out_shape=ACC, in_specs=[SMEM, SMEM] + [VMEM]...]
    pallas_call x2, Pallas kernels: 7.55 us -> 5.04 us  [later_operate(): pl.pallas_call(far_kernel, out_shape=[PART, PART], in_specs=[SMEM, SMEM]...]
    unnamed x11 -> x5, local copies, waits for them, and re-layouts: 3.25 us -> 0.76 us
    ppermute x12, waiting for transfers between devices: 25.1 us -> 23.2 us  [shift_y(): return lax.ppermute(a, Y, [(i, (i + step) % 4) for i in range(4)])]
  transfers between devices with their start and end apart: 44 -> 44, of which waited for: 24 -> 29; matrix products, arithmetic and copies ran while one was open for 1% -> 1% of each run, Pallas kernels for 5% -> 3%
where the time goes in v4:
time: 173 us; the launch traced here: 174 us
  starting transfers between devices  68.9 us (40%)
  waiting for transfers between devices  62.2 us (36%)
  Pallas kernels  22.9 us (13%)
  blocking collectives  16.5 us (10%)
    ppermute x27, starting transfers between devices, hop(): return lax.ppermute(a, ALL, along_row(stage, step))  38 us
    ppermute x27, waiting for transfers between devices, hop(): return lax.ppermute(a, ALL, along_row(stage, step))  24.8 us
    ppermute x12, waiting for transfers between devices, shift_y(): return lax.ppermute(a, Y, [(i, (i + step) % 4) for i in range(4)])  23.2 us
    all_to_all x1, blocking collectives, to_everyone(): return lax.all_to_all(copies, axes, split_axis=0, concat_axis=0, tiled=True)  16.5 us
    ppermute x4, starting transfers between devices, swap_core(): return lax.ppermute(a, C, [(0, 1), (1, 0)])  15.3 us
    ppermute x12, starting transfers between devices, shift_y(): return lax.ppermute(a, Y, [(i, (i + step) % 4) for i in range(4)])  11.5 us
    all_to_all x1, waiting for transfers between devices, shards(): cells = lax.all_to_all(cells, ROW, split_axis=0, concat_axis=0, tiled=True)  9.53 us
    pallas_call x1, Pallas kernels, first_operate(): pl.pallas_call(first_kernel, out_shape=[PART, PART, jax.ShapeDtypeStruct(...  9.15 us
  transfers between devices with their start and end apart: 44, of which 29 were waited for; matrix products, arithmetic and copies ran while one was open for 1% of the time, Pallas kernels for 3%

profile of v4, /device:TPU:1, one launch (start us, length us, event | category | flops | bytes accessed | tf_op | source)
XLA Modules:
  0.0 173.9 jit_solution(12568079456476790569)
XLA Ops:
  1.4 1.6 shard_map.77
  3.0 2.2 %collective-permute-start.11 = (f32[72,512]{1,0:T(8,128)S(1)}, f32[72,512]{1,0:T(8,128)S(1)}, u32[]{:S(2)}, u32[]{:S(2)}) collective-permute-start(f32[72,512]{1,0:T(8,128)S(1)} %get-tuple-element.27), channel_id=1, source_target_pairs={{0,2},{2,4},{4,6},{6,0},{1,3},{3,5},{5,7},{7,1},{8,10},{10,12},{12... | collective-permute-start | bytes 442376 | tf_op jit(solution)/shard_map/ppermute | solution.py:69
  5.2 2.6 %collective-permute-start.10 = (f32[72,512]{1,0:T(8,128)S(1)}, f32[72,512]{1,0:T(8,128)S(1)}, u32[]{:S(2)}, u32[]{:S(2)}) collective-permute-start(f32[72,512]{1,0:T(8,128)S(1)} %get-tuple-element.27), channel_id=1, source_target_pairs={{0,4},{2,6},{4,0},{6,2},{1,5},{3,7},{5,1},{7,3},{8,12},{10,14},{12... | collective-permute-start | bytes 442376 | tf_op jit(solution)/shard_map/ppermute | solution.py:69
  7.8 1.6 collective-permute-start.2
  9.5 3.3 %collective-permute-start.1 = (f32[136,512]{1,0:T(8,128)S(1)}, f32[136,512]{1,0:T(8,128)S(1)}, u32[]{:S(2)}, u32[]{:S(2)}) collective-permute-start(f32[136,512]{1,0:T(8,128)S(1)} %get-tuple-element.26), channel_id=1, source_target_pairs={{0,64},{1,17},{2,66},{3,19},{4,68},{5,21},{6,70},{7,23},{8,72},{9,... | collective-permute-start | bytes 835592 | tf_op jit(solution)/shard_map/ppermute | solution.py:39
  14.2 5.2 %collective-permute-done = f32[136,512]{1,0:T(8,128)S(1)} collective-permute-done((f32[136,512]{1,0:T(8,128)S(1)}, f32[136,512]{1,0:T(8,128)S(1)}, u32[]{:S(2)}, u32[]{:S(2)}) %collective-permute-start) | collective-permute-done | bytes 278560 | tf_op jit(solution)/shard_map/ppermute | solution.py:39
  20.5 1.3 collective-permute-start.5
  21.8 1.5 collective-permute-start.4
  23.4 3.0 %collective-permute-start.12 = (f32[4,72,512]{2,1,0:T(8,128)S(1)}, f32[4,72,512]{2,1,0:T(8,128)S(1)}, u32[]{:S(2)}, u32[]{:S(2)}) collective-permute-start(f32[4,72,512]{2,1,0:T(8,128)S(1)} %pad_maximum_fusion.same), channel_id=1, source_target_pairs={{0,1},{1,0},{2,3},{3,2},{4,5},{5,4},{6,7},{7,6},{8,9},{9,8},{10,11... | collective-permute-start | bytes 1769480 | tf_op jit(solution)/shard_map/ppermute | solution.py:65
  26.5 2.4 %collective-permute-start.3 = (f32[2,136,512]{2,1,0:T(8,128)S(1)}, f32[2,136,512]{2,1,0:T(8,128)}, u32[]{:S(2)}, u32[]{:S(2)}) collective-permute-start(f32[2,136,512]{2,1,0:T(8,128)S(1)} %pad_maximum_fusion.1.p0), channel_id=1, source_target_pairs={{0,24},{1,97},{2,26},{3,99},{4,28},{5,101},{6,30},{7,103},{8,0},{9... | collective-permute-start | bytes 1671176 | tf_op jit(solution)/shard_map/ppermute | solution.py:39
  28.9 1.6 collective-permute-done.5.p6
  30.7 2.6 %collective-permute-start.7 = (f32[2,136,512]{2,1,0:T(8,128)}, f32[2,136,512]{2,1,0:T(8,128)}, u32[]{:S(2)}, u32[]{:S(2)}) collective-permute-start(f32[2,136,512]{2,1,0:T(8,128)} %collective-permute-done.4.p3), channel_id=1, source_target_pairs={{0,24},{1,97},{2,26},{3,99},{4,28},{5,101},{6,30},{7,103},{8,0},{9... | collective-permute-start | bytes 1671176 | tf_op jit(solution)/shard_map/ppermute | solution.py:39
  33.9 4.1 %all-to-all-start = ((f32[16,8,128]{2,1,0:T(8,128)}), f32[16,8,128]{2,1,0:T(8,128)S(1)}, u32[]{:S(2)}, u32[]{:S(2)}) async-start(f32[16,8,128]{2,1,0:T(8,128)} %broadcast_in_dim.47), calls=%async_computation | async-start | bytes 131072 | tf_op jit(solution)/shard_map/all_to_all | solution.py:581
  38.1 9.5 %all-to-all-done.cells = f32[16,8,128]{2,1,0:T(8,128)S(1)} async-done(((f32[16,8,128]{2,1,0:T(8,128)}), f32[16,8,128]{2,1,0:T(8,128)S(1)}, u32[]{:S(2)}, u32[]{:S(2)}) %all-to-all-start) | async-done | bytes 65568 | tf_op jit(solution)/shard_map/all_to_all | solution.py:581
  47.7 9.1 %shard_map.78 = (f32[4,264,128]{2,1,0:T(8,128)S(1)}, f32[4,264,128]{2,1,0:T(8,128)S(1)}, s32[144]{0:T(256)S(1)}, bf16[48,2,512,512]{3,2,1,0:T(8,128)(2,1)}, f32[24,72,512]{2,1,0:T(8,128)S(1)}) custom-call(s32[4]{0:T(128)S(1)} %pad_add_fusion.1.place_ref, s32[1,1,8,3]{3,2,1,0:T(8,128)S(1)} %copy.13.slots_ref, f32[2,2]{1,0:T(2,128)S(1)} %log_multiply_fusion.lc_ref, ...), custom_call_target="tpu_custom_call" | custom-call | flops 8000000000 | bytes 20000000 | tf_op jit(solution)/shard_map/pallas_call | solution.py:504
  56.8 4.2 %collective-permute-start.13 = (f32[4,264,128]{2,1,0:T(8,128)S(1)}, f32[4,264,128]{2,1,0:T(8,128)S(1)}, u32[]{:S(2)}, u32[]{:S(2)}) collective-permute-start(f32[4,264,128]{2,1,0:T(8,128)S(1)} %get-tuple-element.30), channel_id=1, source_target_pairs={{0,1},{1,0},{2,3},{3,2},{4,5},{5,4},{6,7},{7,6},{8,9},{9,8},{10,11... | collective-permute-start | bytes 1622024 | tf_op jit(solution)/shard_map/ppermute | solution.py:65
  61.0 1.6 collective-permute-done.13.b
  62.7 2.0 %collective-permute-start.15 = (f32[264,128]{1,0:T(8,128)S(1)}, f32[264,128]{1,0:T(8,128)S(1)}, u32[]{:S(2)}, u32[]{:S(2)}) collective-permute-start(f32[264,128]{1,0:T(8,128)S(1)} %get-tuple-element.57), channel_id=1, source_target_pairs={{0,6},{2,0},{4,2},{6,4},{1,7},{3,1},{5,3},{7,5},{8,14},{10,8},{12,... | collective-permute-start | bytes 405512 | tf_op jit(solution)/shard_map/ppermute | solution.py:69
  64.7 4.3 %collective-permute-done.16 = f32[264,128]{1,0:T(8,128)S(1)} collective-permute-done((f32[264,128]{1,0:T(8,128)S(1)}, f32[264,128]{1,0:T(8,128)S(1)}, u32[]{:S(2)}, u32[]{:S(2)}) %collective-permute-start.16) | collective-permute-done | bytes 135200 | tf_op jit(solution)/shard_map/ppermute | solution.py:69
  69.0 3.2 %collective-permute-done.14 = f32[264,128]{1,0:T(8,128)S(1)} collective-permute-done((f32[264,128]{1,0:T(8,128)S(1)}, f32[264,128]{1,0:T(8,128)S(1)}, u32[]{:S(2)}, u32[]{:S(2)}) %collective-permute-start.14) | collective-permute-done | bytes 135200 | tf_op jit(solution)/shard_map/ppermute | solution.py:69
  73.8 7.3 %collective-permute-start.20 = (f32[264,128]{1,0:T(8,128)S(1)}, f32[264,128]{1,0:T(8,128)S(1)}, u32[]{:S(2)}, u32[]{:S(2)}) collective-permute-start(f32[264,128]{1,0:T(8,128)S(1)} %get-tuple-element.31.w_ref.w0_ref), channel_id=1, source_target_pairs={{0,64},{1,17},{2,66},{3,19},{4,68},{5,21},{6,70},{7,23},{8,72},{9,... | collective-permute-start | bytes 405512 | tf_op jit(solution)/shard_map/ppermute | solution.py:39
  82.4 2.6 %collective-permute-done.20 = f32[264,128]{1,0:T(8,128)S(1)} collective-permute-done((f32[264,128]{1,0:T(8,128)S(1)}, f32[264,128]{1,0:T(8,128)S(1)}, u32[]{:S(2)}, u32[]{:S(2)}) %collective-permute-start.20) | collective-permute-done | bytes 135200 | tf_op jit(solution)/shard_map/ppermute | solution.py:39
  85.1 2.9 %collective-permute-start.24 = (f32[2,264,128]{2,1,0:T(8,128)S(1)}, f32[2,264,128]{2,1,0:T(8,128)S(1)}, u32[]{:S(2)}, u32[]{:S(2)}) collective-permute-start(f32[2,264,128]{2,1,0:T(8,128)S(1)} %pad_maximum_fusion.3.p0), channel_id=1, source_target_pairs={{0,24},{1,97},{2,26},{3,99},{4,28},{5,101},{6,30},{7,103},{8,0},{9... | collective-permute-start | bytes 811016 | tf_op jit(solution)/shard_map/ppermute | solution.py:39
  88.0 1.5 collective-permute-done.18.p6
  90.5 1.7 collective-permute-start.23
  92.2 1.4 collective-permute-done.24.p2
  94.5 2.8 %shard_map.80.near_ref = f32[8,264,128]{2,1,0:T(8,128)S(1)} custom-call(s32[144]{0:T(256)S(1)} %get-tuple-element.28.list_ref, f32[2,2]{1,0:T(2,128)S(1)} %log_multiply_fusion.lc_ref, f32[2,264,128]{2,1,0:T(8,128)S(1)} %pad_maximum_fusion.3.p0, f32[2,264,128]{2,1,0:T(8,128)S(1)} %pad_maximum_fusion.4.p1, f32[2,264,128]{2,1,0:T(8,128)S(1)} %collective-permute-done.24.p2, ...), custom_call_target="tpu_custom_call" | custom-call | flops 3000000000 | bytes 12000000 | tf_op jit(solution)/shard_map/pallas_call | solution.py:548
  97.7 2.5 %shard_map.81 = (f32[4,264,128]{2,1,0:T(8,128)S(1)}, f32[4,264,128]{2,1,0:T(8,128)S(1)}) custom-call(s32[144]{0:T(256)S(1)} %get-tuple-element.28.list_ref, f32[2,2]{1,0:T(2,128)S(1)} %log_multiply_fusion.lc_ref, f32[2,264,128]{2,1,0:T(8,128)S(1)} %collective-permute-done.19.p4, f32[2,264,128]{2,1,0:T(8,128)S(1)} %collective-permute-done.23.p5, ...), custom_call_target="tpu_custom_call" | custom-call | flops 1000000000 | bytes 6000000 | tf_op jit(solution)/shard_map/pallas_call | solution.py:557
  100.2 3.7 %collective-permute-start.26 = (f32[4,264,128]{2,1,0:T(8,128)S(1)}, f32[4,264,128]{2,1,0:T(8,128)S(1)}, u32[]{:S(2)}, u32[]{:S(2)}) collective-permute-start(f32[4,264,128]{2,1,0:T(8,128)S(1)} %get-tuple-element.35), channel_id=1, source_target_pairs={{0,1},{1,0},{2,3},{3,2},{4,5},{5,4},{6,7},{7,6},{8,9},{9,8},{10,11... | collective-permute-start | bytes 1622024 | tf_op jit(solution)/shard_map/ppermute | solution.py:65
  104.0 1.6 collective-permute-done.26.b
  105.8 1.6 collective-permute-start.28
  107.4 4.6 %collective-permute-done.29 = f32[264,128]{1,0:T(8,128)S(1)} collective-permute-done((f32[264,128]{1,0:T(8,128)S(1)}, f32[264,128]{1,0:T(8,128)S(1)}, u32[]{:S(2)}, u32[]{:S(2)}) %collective-permute-start.29) | collective-permute-done | bytes 135200 | tf_op jit(solution)/shard_map/ppermute | solution.py:69
  112.7 2.5 %collective-permute-done.27 = f32[264,128]{1,0:T(8,128)S(1)} collective-permute-done((f32[264,128]{1,0:T(8,128)S(1)}, f32[264,128]{1,0:T(8,128)S(1)}, u32[]{:S(2)}, u32[]{:S(2)}) %collective-permute-start.27) | collective-permute-done | bytes 135200 | tf_op jit(solution)/shard_map/ppermute | solution.py:69
  115.5 2.0 %collective-permute-start.30 = (f32[264,128]{1,0:T(8,128)S(1)}, f32[264,128]{1,0:T(8,128)S(1)}, u32[]{:S(2)}, u32[]{:S(2)}) collective-permute-start(f32[264,128]{1,0:T(8,128)S(1)} %get-tuple-element.37.w1_ref), channel_id=1, source_target_pairs={{0,96},{1,25},{2,98},{3,27},{4,100},{5,29},{6,102},{7,31},{8,104},... | collective-permute-start | bytes 405512 | tf_op jit(solution)/shard_map/ppermute | solution.py:39
  117.5 4.5 %collective-permute-start.33 = (f32[264,128]{1,0:T(8,128)S(1)}, f32[264,128]{1,0:T(8,128)S(1)}, u32[]{:S(2)}, u32[]{:S(2)}) collective-permute-start(f32[264,128]{1,0:T(8,128)S(1)} %get-tuple-element.37.w1_ref), channel_id=1, source_target_pairs={{0,64},{1,17},{2,66},{3,19},{4,68},{5,21},{6,70},{7,23},{8,72},{9,... | collective-permute-start | bytes 405512 | tf_op jit(solution)/shard_map/ppermute | solution.py:39
  123.3 2.6 %collective-permute-done.33 = f32[264,128]{1,0:T(8,128)S(1)} collective-permute-done((f32[264,128]{1,0:T(8,128)S(1)}, f32[264,128]{1,0:T(8,128)S(1)}, u32[]{:S(2)}, u32[]{:S(2)}) %collective-permute-start.33) | collective-permute-done | bytes 135200 | tf_op jit(solution)/shard_map/ppermute | solution.py:39
  126.0 2.4 %collective-permute-start.37 = (f32[2,264,128]{2,1,0:T(8,128)S(1)}, f32[2,264,128]{2,1,0:T(8,128)S(1)}, u32[]{:S(2)}, u32[]{:S(2)}) collective-permute-start(f32[2,264,128]{2,1,0:T(8,128)S(1)} %pad_maximum_fusion.5.p0), channel_id=1, source_target_pairs={{0,24},{1,97},{2,26},{3,99},{4,28},{5,101},{6,30},{7,103},{8,0},{9... | collective-permute-start | bytes 811016 | tf_op jit(solution)/shard_map/ppermute | solution.py:39
  128.4 2.1 %collective-permute-done.31.p6 = f32[2,264,128]{2,1,0:T(8,128)S(1)} collective-permute-done((f32[2,264,128]{2,1,0:T(8,128)S(1)}, f32[2,264,128]{2,1,0:T(8,128)S(1)}, u32[]{:S(2)}, u32[]{:S(2)}) %collective-permute-start.31) | collective-permute-done | bytes 270368 | tf_op jit(solution)/shard_map/ppermute | solution.py:39
  131.3 1.8 %collective-permute-start.36 = (f32[2,264,128]{2,1,0:T(8,128)S(1)}, f32[2,264,128]{2,1,0:T(8,128)S(1)}, u32[]{:S(2)}, u32[]{:S(2)}) collective-permute-start(f32[2,264,128]{2,1,0:T(8,128)S(1)} %collective-permute-done.35.p3), channel_id=1, source_target_pairs={{0,24},{1,97},{2,26},{3,99},{4,28},{5,101},{6,30},{7,103},{8,0},{9... | collective-permute-start | bytes 811016 | tf_op jit(solution)/shard_map/ppermute | solution.py:39
  133.1 1.4 collective-permute-done.37.p2
  134.9 2.8 %shard_map.83.near_ref = f32[8,264,128]{2,1,0:T(8,128)S(1)} custom-call(s32[144]{0:T(256)S(1)} %get-tuple-element.28.list_ref, f32[2,2]{1,0:T(2,128)S(1)} %log_multiply_fusion.lc_ref, f32[2,264,128]{2,1,0:T(8,128)S(1)} %pad_maximum_fusion.5.p0, f32[2,264,128]{2,1,0:T(8,128)S(1)} %pad_maximum_fusion.6.p1, f32[2,264,128]{2,1,0:T(8,128)S(1)} %collective-permute-done.37.p2, ...), custom_call_target="tpu_custom_call" | custom-call | flops 3000000000 | bytes 12000000 | tf_op jit(solution)/shard_map/pallas_call | solution.py:548
  138.1 2.5 %shard_map.84 = (f32[4,264,128]{2,1,0:T(8,128)S(1)}, f32[4,264,128]{2,1,0:T(8,128)S(1)}) custom-call(s32[144]{0:T(256)S(1)} %get-tuple-element.28.list_ref, f32[2,2]{1,0:T(2,128)S(1)} %log_multiply_fusion.lc_ref, f32[2,264,128]{2,1,0:T(8,128)S(1)} %collective-permute-done.32.p4, f32[2,264,128]{2,1,0:T(8,128)S(1)} %collective-permute-done.36.p5, ...), custom_call_target="tpu_custom_call" | custom-call | flops 1000000000 | bytes 6000000 | tf_op jit(solution)/shard_map/pallas_call | solution.py:557
  140.6 4.3 %collective-permute-start.39 = (f32[4,264,128]{2,1,0:T(8,128)S(1)}, f32[4,264,128]{2,1,0:T(8,128)S(1)}, u32[]{:S(2)}, u32[]{:S(2)}) collective-permute-start(f32[4,264,128]{2,1,0:T(8,128)S(1)} %get-tuple-element.39), channel_id=1, source_target_pairs={{0,1},{1,0},{2,3},{3,2},{4,5},{5,4},{6,7},{7,6},{8,9},{9,8},{10,11... | collective-permute-start | bytes 1622024 | tf_op jit(solution)/shard_map/ppermute | solution.py:65
  144.9 1.6 collective-permute-done.39.b
  146.8 1.6 collective-permute-start.41
  148.3 4.6 %collective-permute-done.42 = f32[264,128]{1,0:T(8,128)S(1)} collective-permute-done((f32[264,128]{1,0:T(8,128)S(1)}, f32[264,128]{1,0:T(8,128)S(1)}, u32[]{:S(2)}, u32[]{:S(2)}) %collective-permute-start.42) | collective-permute-done | bytes 135200 | tf_op jit(solution)/shard_map/ppermute | solution.py:69
  153.5 2.7 %collective-permute-done.40 = f32[264,128]{1,0:T(8,128)S(1)} collective-permute-done((f32[264,128]{1,0:T(8,128)S(1)}, f32[264,128]{1,0:T(8,128)S(1)}, u32[]{:S(2)}, u32[]{:S(2)}) %collective-permute-start.40) | collective-permute-done | bytes 135200 | tf_op jit(solution)/shard_map/ppermute | solution.py:69
  156.6 16.5 %all_to_all.10 = f32[128,1,128]{2,1,0:T(1,128)S(1)} all-to-all(f32[128,1,128]{2,1,0:T(1,128)S(1)} %broadcast_in_dim.59), channel_id=1, replica_groups=mesh['row_0'=4,'row_1'=4,'col_0'=4,'col_1'=2] {'row_0','row_1','col_0','..., dimensions={0} | all-to-all | bytes 131072 | tf_op jit(solution)/shard_map/all_to_all | solution.py:570
  (78 shorter events, 16.1 us)
Async XLA Ops:
  3.0 20.4 %collective-permute-start.11 = (f32[72,512]{1,0:T(8,128)S(1)}, f32[72,512]{1,0:T(8,128)S(1)}, u32[]{:S(2)}, u32[]{:S(2)}) collective-permute-start(f32[72,512]{1,0:T(8,128)S(1)} %get-tuple-element.27), channel_id=1, source_target_pairs={{0,2},{2,4},{4,6},{6,0},{1,3},{3,5},{5,7},{7,1},{8,10},{10,12},{12... | collective-permute-start | bytes 442376 | tf_op jit(solution)/shard_map/ppermute | solution.py:69
  5.2 18.2 %collective-permute-start.10 = (f32[72,512]{1,0:T(8,128)S(1)}, f32[72,512]{1,0:T(8,128)S(1)}, u32[]{:S(2)}, u32[]{:S(2)}) collective-permute-start(f32[72,512]{1,0:T(8,128)S(1)} %get-tuple-element.27), channel_id=1, source_target_pairs={{0,4},{2,6},{4,0},{6,2},{1,5},{3,7},{5,1},{7,3},{8,12},{10,14},{12... | collective-permute-start | bytes 442376 | tf_op jit(solution)/shard_map/ppermute | solution.py:69
  7.8 12.7 %collective-permute-start.2 = (f32[136,512]{1,0:T(8,128)S(1)}, f32[136,512]{1,0:T(8,128)S(1)}, u32[]{:S(2)}, u32[]{:S(2)}) collective-permute-start(f32[136,512]{1,0:T(8,128)S(1)} %get-tuple-element.26), channel_id=1, source_target_pairs={{0,32},{1,9},{2,34},{3,11},{4,36},{5,13},{6,38},{7,15},{8,40},{9,1... | collective-permute-start | bytes 835592 | tf_op jit(solution)/shard_map/ppermute | solution.py:39
  9.5 12.3 %collective-permute-start.1 = (f32[136,512]{1,0:T(8,128)S(1)}, f32[136,512]{1,0:T(8,128)S(1)}, u32[]{:S(2)}, u32[]{:S(2)}) collective-permute-start(f32[136,512]{1,0:T(8,128)S(1)} %get-tuple-element.26), channel_id=1, source_target_pairs={{0,64},{1,17},{2,66},{3,19},{4,68},{5,21},{6,70},{7,23},{8,72},{9,... | collective-permute-start | bytes 835592 | tf_op jit(solution)/shard_map/ppermute | solution.py:39
  12.8 6.6 %collective-permute-start = (f32[136,512]{1,0:T(8,128)S(1)}, f32[136,512]{1,0:T(8,128)S(1)}, u32[]{:S(2)}, u32[]{:S(2)}) collective-permute-start(f32[136,512]{1,0:T(8,128)S(1)} %get-tuple-element.26), channel_id=1, source_target_pairs={{0,96},{1,25},{2,98},{3,27},{4,100},{5,29},{6,102},{7,31},{8,104},... | collective-permute-start | bytes 835592 | tf_op jit(solution)/shard_map/ppermute | solution.py:39
  19.4 4.0 %collective-permute-start.9 = (f32[72,512]{1,0:T(8,128)S(1)}, f32[72,512]{1,0:T(8,128)S(1)}, u32[]{:S(2)}, u32[]{:S(2)}) collective-permute-start(f32[72,512]{1,0:T(8,128)S(1)} %get-tuple-element.27), channel_id=1, source_target_pairs={{0,6},{2,0},{4,2},{6,4},{1,7},{3,1},{5,3},{7,5},{8,14},{10,8},{12,... | collective-permute-start | bytes 442376 | tf_op jit(solution)/shard_map/ppermute | solution.py:69
  20.5 10.0 %collective-permute-start.5 = (f32[2,136,512]{2,1,0:T(8,128)S(1)}, f32[2,136,512]{2,1,0:T(8,128)S(1)}, u32[]{:S(2)}, u32[]{:S(2)}) collective-permute-start(f32[2,136,512]{2,1,0:T(8,128)S(1)} %pad_maximum_fusion.1.p0), channel_id=1, source_target_pairs={{0,8},{1,33},{2,10},{3,35},{4,12},{5,37},{6,14},{7,39},{8,16},{9,4... | collective-permute-start | bytes 1671176 | tf_op jit(solution)/shard_map/ppermute | solution.py:39
  21.8 8.9 %collective-permute-start.4 = (f32[2,136,512]{2,1,0:T(8,128)S(1)}, f32[2,136,512]{2,1,0:T(8,128)}, u32[]{:S(2)}, u32[]{:S(2)}) collective-permute-start(f32[2,136,512]{2,1,0:T(8,128)S(1)} %pad_maximum_fusion.2.p1), channel_id=1, source_target_pairs={{0,24},{1,97},{2,26},{3,99},{4,28},{5,101},{6,30},{7,103},{8,0},{9... | collective-permute-start | bytes 1671176 | tf_op jit(solution)/shard_map/ppermute | solution.py:39
  23.4 9.8 %collective-permute-start.12 = (f32[4,72,512]{2,1,0:T(8,128)S(1)}, f32[4,72,512]{2,1,0:T(8,128)S(1)}, u32[]{:S(2)}, u32[]{:S(2)}) collective-permute-start(f32[4,72,512]{2,1,0:T(8,128)S(1)} %pad_maximum_fusion.same), channel_id=1, source_target_pairs={{0,1},{1,0},{2,3},{3,2},{4,5},{5,4},{6,7},{7,6},{8,9},{9,8},{10,11... | collective-permute-start | bytes 1769480 | tf_op jit(solution)/shard_map/ppermute | solution.py:65
  26.5 21.2 %collective-permute-start.3 = (f32[2,136,512]{2,1,0:T(8,128)S(1)}, f32[2,136,512]{2,1,0:T(8,128)}, u32[]{:S(2)}, u32[]{:S(2)}) collective-permute-start(f32[2,136,512]{2,1,0:T(8,128)S(1)} %pad_maximum_fusion.1.p0), channel_id=1, source_target_pairs={{0,24},{1,97},{2,26},{3,99},{4,28},{5,101},{6,30},{7,103},{8,0},{9... | collective-permute-start | bytes 1671176 | tf_op jit(solution)/shard_map/ppermute | solution.py:39
  28.9 18.8 %collective-permute-start.8 = (f32[2,136,512]{2,1,0:T(8,128)S(1)}, f32[2,136,512]{2,1,0:T(8,128)}, u32[]{:S(2)}, u32[]{:S(2)}) collective-permute-start(f32[2,136,512]{2,1,0:T(8,128)S(1)} %pad_maximum_fusion.2.p1), channel_id=1, source_target_pairs={{0,8},{1,33},{2,10},{3,35},{4,12},{5,37},{6,14},{7,39},{8,16},{9,4... | collective-permute-start | bytes 1671176 | tf_op jit(solution)/shard_map/ppermute | solution.py:39
  30.5 17.2 %collective-permute-start.6 = (f32[2,136,512]{2,1,0:T(8,128)S(1)}, f32[2,136,512]{2,1,0:T(8,128)}, u32[]{:S(2)}, u32[]{:S(2)}) collective-permute-start(f32[2,136,512]{2,1,0:T(8,128)S(1)} %collective-permute-done.5.p6), channel_id=1, source_target_pairs={{0,8},{1,33},{2,10},{3,35},{4,12},{5,37},{6,14},{7,39},{8,16},{9,4... | collective-permute-start | bytes 1671176 | tf_op jit(solution)/shard_map/ppermute | solution.py:39
  30.7 17.0 %collective-permute-start.7 = (f32[2,136,512]{2,1,0:T(8,128)}, f32[2,136,512]{2,1,0:T(8,128)}, u32[]{:S(2)}, u32[]{:S(2)}) collective-permute-start(f32[2,136,512]{2,1,0:T(8,128)} %collective-permute-done.4.p3), channel_id=1, source_target_pairs={{0,24},{1,97},{2,26},{3,99},{4,28},{5,101},{6,30},{7,103},{8,0},{9... | collective-permute-start | bytes 1671176 | tf_op jit(solution)/shard_map/ppermute | solution.py:39
  33.9 13.7 %all-to-all-start = ((f32[16,8,128]{2,1,0:T(8,128)}), f32[16,8,128]{2,1,0:T(8,128)S(1)}, u32[]{:S(2)}, u32[]{:S(2)}) async-start(f32[16,8,128]{2,1,0:T(8,128)} %broadcast_in_dim.47), calls=%async_computation | async-start | bytes 131072 | tf_op jit(solution)/shard_map/all_to_all | solution.py:581
  38.1 34.1 %copy-start = (f32[64,512]{1,0:T(8,128)S(1)}, f32[64,512]{1,0:T(8,128)}, u32[]{:S(2)}) copy-start(f32[64,512]{1,0:T(8,128)} %r_ref.5) | copy-start | bytes 393220
  38.1 34.1 %copy-start.1 = (f32[512]{0:T(512)S(1)}, f32[512]{0:T(512)}, u32[]{:S(2)}) copy-start(f32[512]{0:T(512)} %param.9) | copy-start | bytes 6148
  56.8 5.8 %collective-permute-start.13 = (f32[4,264,128]{2,1,0:T(8,128)S(1)}, f32[4,264,128]{2,1,0:T(8,128)S(1)}, u32[]{:S(2)}, u32[]{:S(2)}) collective-permute-start(f32[4,264,128]{2,1,0:T(8,128)S(1)} %get-tuple-element.30), channel_id=1, source_target_pairs={{0,1},{1,0},{2,3},{3,2},{4,5},{5,4},{6,7},{7,6},{8,9},{9,8},{10,11... | collective-permute-start | bytes 1622024 | tf_op jit(solution)/shard_map/ppermute | solution.py:65
  62.6 6.4 %collective-permute-start.16 = (f32[264,128]{1,0:T(8,128)S(1)}, f32[264,128]{1,0:T(8,128)S(1)}, u32[]{:S(2)}, u32[]{:S(2)}) collective-permute-start(f32[264,128]{1,0:T(8,128)S(1)} %get-tuple-element.56), channel_id=1, source_target_pairs={{0,4},{2,6},{4,0},{6,2},{1,5},{3,7},{5,1},{7,3},{8,12},{10,14},{12... | collective-permute-start | bytes 405512 | tf_op jit(solution)/shard_map/ppermute | solution.py:69
  62.7 6.3 %collective-permute-start.15 = (f32[264,128]{1,0:T(8,128)S(1)}, f32[264,128]{1,0:T(8,128)S(1)}, u32[]{:S(2)}, u32[]{:S(2)}) collective-permute-start(f32[264,128]{1,0:T(8,128)S(1)} %get-tuple-element.57), channel_id=1, source_target_pairs={{0,6},{2,0},{4,2},{6,4},{1,7},{3,1},{5,3},{7,5},{8,14},{10,8},{12,... | collective-permute-start | bytes 405512 | tf_op jit(solution)/shard_map/ppermute | solution.py:69
  64.7 7.5 %collective-permute-start.14 = (f32[264,128]{1,0:T(8,128)S(1)}, f32[264,128]{1,0:T(8,128)S(1)}, u32[]{:S(2)}, u32[]{:S(2)}) collective-permute-start(f32[264,128]{1,0:T(8,128)S(1)} %get-tuple-element.58), channel_id=1, source_target_pairs={{0,2},{2,4},{4,6},{6,0},{1,3},{3,5},{5,7},{7,1},{8,10},{10,12},{12... | collective-permute-start | bytes 405512 | tf_op jit(solution)/shard_map/ppermute | solution.py:69
  72.4 8.8 %collective-permute-start.17 = (f32[264,128]{1,0:T(8,128)S(1)}, f32[264,128]{1,0:T(8,128)S(1)}, u32[]{:S(2)}, u32[]{:S(2)}) collective-permute-start(f32[264,128]{1,0:T(8,128)S(1)} %get-tuple-element.31.w_ref.w0_ref), channel_id=1, source_target_pairs={{0,96},{1,25},{2,98},{3,27},{4,100},{5,29},{6,102},{7,31},{8,104},... | collective-permute-start | bytes 405512 | tf_op jit(solution)/shard_map/ppermute | solution.py:39
  72.6 9.7 %collective-permute-start.21 = (f32[264,128]{1,0:T(8,128)S(1)}, f32[264,128]{1,0:T(8,128)S(1)}, u32[]{:S(2)}, u32[]{:S(2)}) collective-permute-start(f32[264,128]{1,0:T(8,128)S(1)} %get-tuple-element.31.w_ref.w0_ref), channel_id=1, source_target_pairs={{0,32},{1,9},{2,34},{3,11},{4,36},{5,13},{6,38},{7,15},{8,40},{9,1... | collective-permute-start | bytes 405512 | tf_op jit(solution)/shard_map/ppermute | solution.py:39
  73.8 11.1 %collective-permute-start.20 = (f32[264,128]{1,0:T(8,128)S(1)}, f32[264,128]{1,0:T(8,128)S(1)}, u32[]{:S(2)}, u32[]{:S(2)}) collective-permute-start(f32[264,128]{1,0:T(8,128)S(1)} %get-tuple-element.31.w_ref.w0_ref), channel_id=1, source_target_pairs={{0,64},{1,17},{2,66},{3,19},{4,68},{5,21},{6,70},{7,23},{8,72},{9,... | collective-permute-start | bytes 405512 | tf_op jit(solution)/shard_map/ppermute | solution.py:39
  81.2 8.3 %collective-permute-start.18 = (f32[2,264,128]{2,1,0:T(8,128)S(1)}, f32[2,264,128]{2,1,0:T(8,128)S(1)}, u32[]{:S(2)}, u32[]{:S(2)}) collective-permute-start(f32[2,264,128]{2,1,0:T(8,128)S(1)} %pad_maximum_fusion.3.p0), channel_id=1, source_target_pairs={{0,8},{1,33},{2,10},{3,35},{4,12},{5,37},{6,14},{7,39},{8,16},{9,4... | collective-permute-start | bytes 811016 | tf_op jit(solution)/shard_map/ppermute | solution.py:39
  85.0 5.5 %collective-permute-start.22 = (f32[2,264,128]{2,1,0:T(8,128)S(1)}, f32[2,264,128]{2,1,0:T(8,128)S(1)}, u32[]{:S(2)}, u32[]{:S(2)}) collective-permute-start(f32[2,264,128]{2,1,0:T(8,128)S(1)} %pad_maximum_fusion.4.p1), channel_id=1, source_target_pairs={{0,24},{1,97},{2,26},{3,99},{4,28},{5,101},{6,30},{7,103},{8,0},{9... | collective-permute-start | bytes 811016 | tf_op jit(solution)/shard_map/ppermute | solution.py:39
  85.1 8.5 %collective-permute-start.24 = (f32[2,264,128]{2,1,0:T(8,128)S(1)}, f32[2,264,128]{2,1,0:T(8,128)S(1)}, u32[]{:S(2)}, u32[]{:S(2)}) collective-permute-start(f32[2,264,128]{2,1,0:T(8,128)S(1)} %pad_maximum_fusion.3.p0), channel_id=1, source_target_pairs={{0,24},{1,97},{2,26},{3,99},{4,28},{5,101},{6,30},{7,103},{8,0},{9... | collective-permute-start | bytes 811016 | tf_op jit(solution)/shard_map/ppermute | solution.py:39
  88.0 6.5 %collective-permute-start.25 = (f32[2,264,128]{2,1,0:T(8,128)S(1)}, f32[2,264,128]{2,1,0:T(8,128)S(1)}, u32[]{:S(2)}, u32[]{:S(2)}) collective-permute-start(f32[2,264,128]{2,1,0:T(8,128)S(1)} %pad_maximum_fusion.4.p1), channel_id=1, source_target_pairs={{0,8},{1,33},{2,10},{3,35},{4,12},{5,37},{6,14},{7,39},{8,16},{9,4... | collective-permute-start | bytes 811016 | tf_op jit(solution)/shard_map/ppermute | solution.py:39
  89.5 8.2 %collective-permute-start.19 = (f32[2,264,128]{2,1,0:T(8,128)S(1)}, f32[2,264,128]{2,1,0:T(8,128)S(1)}, u32[]{:S(2)}, u32[]{:S(2)}) collective-permute-start(f32[2,264,128]{2,1,0:T(8,128)S(1)} %collective-permute-done.18.p6), channel_id=1, source_target_pairs={{0,8},{1,33},{2,10},{3,35},{4,12},{5,37},{6,14},{7,39},{8,16},{9,4... | collective-permute-start | bytes 811016 | tf_op jit(solution)/shard_map/ppermute | solution.py:39
  90.5 7.2 %collective-permute-start.23 = (f32[2,264,128]{2,1,0:T(8,128)S(1)}, f32[2,264,128]{2,1,0:T(8,128)S(1)}, u32[]{:S(2)}, u32[]{:S(2)}) collective-permute-start(f32[2,264,128]{2,1,0:T(8,128)S(1)} %collective-permute-done.22.p3), channel_id=1, source_target_pairs={{0,24},{1,97},{2,26},{3,99},{4,28},{5,101},{6,30},{7,103},{8,0},{9... | collective-permute-start | bytes 811016 | tf_op jit(solution)/shard_map/ppermute | solution.py:39
  100.2 5.3 %collective-permute-start.26 = (f32[4,264,128]{2,1,0:T(8,128)S(1)}, f32[4,264,128]{2,1,0:T(8,128)S(1)}, u32[]{:S(2)}, u32[]{:S(2)}) collective-permute-start(f32[4,264,128]{2,1,0:T(8,128)S(1)} %get-tuple-element.35), channel_id=1, source_target_pairs={{0,1},{1,0},{2,3},{3,2},{4,5},{5,4},{6,7},{7,6},{8,9},{9,8},{10,11... | collective-permute-start | bytes 1622024 | tf_op jit(solution)/shard_map/ppermute | solution.py:65
  105.6 6.4 %collective-permute-start.29 = (f32[264,128]{1,0:T(8,128)S(1)}, f32[264,128]{1,0:T(8,128)S(1)}, u32[]{:S(2)}, u32[]{:S(2)}) collective-permute-start(f32[264,128]{1,0:T(8,128)S(1)} %get-tuple-element.53), channel_id=1, source_target_pairs={{0,4},{2,6},{4,0},{6,2},{1,5},{3,7},{5,1},{7,3},{8,12},{10,14},{12... | collective-permute-start | bytes 405512 | tf_op jit(solution)/shard_map/ppermute | solution.py:69
  105.8 6.9 %collective-permute-start.28 = (f32[264,128]{1,0:T(8,128)S(1)}, f32[264,128]{1,0:T(8,128)S(1)}, u32[]{:S(2)}, u32[]{:S(2)}) collective-permute-start(f32[264,128]{1,0:T(8,128)S(1)} %get-tuple-element.54), channel_id=1, source_target_pairs={{0,6},{2,0},{4,2},{6,4},{1,7},{3,1},{5,3},{7,5},{8,14},{10,8},{12,... | collective-permute-start | bytes 405512 | tf_op jit(solution)/shard_map/ppermute | solution.py:69
  107.4 7.9 %collective-permute-start.27 = (f32[264,128]{1,0:T(8,128)S(1)}, f32[264,128]{1,0:T(8,128)S(1)}, u32[]{:S(2)}, u32[]{:S(2)}) collective-permute-start(f32[264,128]{1,0:T(8,128)S(1)} %get-tuple-element.55), channel_id=1, source_target_pairs={{0,2},{2,4},{4,6},{6,0},{1,3},{3,5},{5,7},{7,1},{8,10},{10,12},{12... | collective-permute-start | bytes 405512 | tf_op jit(solution)/shard_map/ppermute | solution.py:69
  115.5 6.6 %collective-permute-start.30 = (f32[264,128]{1,0:T(8,128)S(1)}, f32[264,128]{1,0:T(8,128)S(1)}, u32[]{:S(2)}, u32[]{:S(2)}) collective-permute-start(f32[264,128]{1,0:T(8,128)S(1)} %get-tuple-element.37.w1_ref), channel_id=1, source_target_pairs={{0,96},{1,25},{2,98},{3,27},{4,100},{5,29},{6,102},{7,31},{8,104},... | collective-permute-start | bytes 405512 | tf_op jit(solution)/shard_map/ppermute | solution.py:39
  117.5 5.8 %collective-permute-start.34 = (f32[264,128]{1,0:T(8,128)S(1)}, f32[264,128]{1,0:T(8,128)S(1)}, u32[]{:S(2)}, u32[]{:S(2)}) collective-permute-start(f32[264,128]{1,0:T(8,128)S(1)} %get-tuple-element.37.w1_ref), channel_id=1, source_target_pairs={{0,32},{1,9},{2,34},{3,11},{4,36},{5,13},{6,38},{7,15},{8,40},{9,1... | collective-permute-start | bytes 405512 | tf_op jit(solution)/shard_map/ppermute | solution.py:39
  117.5 8.4 %collective-permute-start.33 = (f32[264,128]{1,0:T(8,128)S(1)}, f32[264,128]{1,0:T(8,128)S(1)}, u32[]{:S(2)}, u32[]{:S(2)}) collective-permute-start(f32[264,128]{1,0:T(8,128)S(1)} %get-tuple-element.37.w1_ref), channel_id=1, source_target_pairs={{0,64},{1,17},{2,66},{3,19},{4,68},{5,21},{6,70},{7,23},{8,72},{9,... | collective-permute-start | bytes 405512 | tf_op jit(solution)/shard_map/ppermute | solution.py:39
  122.1 8.3 %collective-permute-start.31 = (f32[2,264,128]{2,1,0:T(8,128)S(1)}, f32[2,264,128]{2,1,0:T(8,128)S(1)}, u32[]{:S(2)}, u32[]{:S(2)}) collective-permute-start(f32[2,264,128]{2,1,0:T(8,128)S(1)} %pad_maximum_fusion.5.p0), channel_id=1, source_target_pairs={{0,8},{1,33},{2,10},{3,35},{4,12},{5,37},{6,14},{7,39},{8,16},{9,4... | collective-permute-start | bytes 811016 | tf_op jit(solution)/shard_map/ppermute | solution.py:39
  125.9 5.4 %collective-permute-start.35 = (f32[2,264,128]{2,1,0:T(8,128)S(1)}, f32[2,264,128]{2,1,0:T(8,128)S(1)}, u32[]{:S(2)}, u32[]{:S(2)}) collective-permute-start(f32[2,264,128]{2,1,0:T(8,128)S(1)} %pad_maximum_fusion.6.p1), channel_id=1, source_target_pairs={{0,24},{1,97},{2,26},{3,99},{4,28},{5,101},{6,30},{7,103},{8,0},{9... | collective-permute-start | bytes 811016 | tf_op jit(solution)/shard_map/ppermute | solution.py:39
  126.0 8.5 %collective-permute-start.37 = (f32[2,264,128]{2,1,0:T(8,128)S(1)}, f32[2,264,128]{2,1,0:T(8,128)S(1)}, u32[]{:S(2)}, u32[]{:S(2)}) collective-permute-start(f32[2,264,128]{2,1,0:T(8,128)S(1)} %pad_maximum_fusion.5.p0), channel_id=1, source_target_pairs={{0,24},{1,97},{2,26},{3,99},{4,28},{5,101},{6,30},{7,103},{8,0},{9... | collective-permute-start | bytes 811016 | tf_op jit(solution)/shard_map/ppermute | solution.py:39
  128.4 6.5 %collective-permute-start.38 = (f32[2,264,128]{2,1,0:T(8,128)S(1)}, f32[2,264,128]{2,1,0:T(8,128)S(1)}, u32[]{:S(2)}, u32[]{:S(2)}) collective-permute-start(f32[2,264,128]{2,1,0:T(8,128)S(1)} %pad_maximum_fusion.6.p1), channel_id=1, source_target_pairs={{0,8},{1,33},{2,10},{3,35},{4,12},{5,37},{6,14},{7,39},{8,16},{9,4... | collective-permute-start | bytes 811016 | tf_op jit(solution)/shard_map/ppermute | solution.py:39
  130.4 7.7 %collective-permute-start.32 = (f32[2,264,128]{2,1,0:T(8,128)S(1)}, f32[2,264,128]{2,1,0:T(8,128)S(1)}, u32[]{:S(2)}, u32[]{:S(2)}) collective-permute-start(f32[2,264,128]{2,1,0:T(8,128)S(1)} %collective-permute-done.31.p6), channel_id=1, source_target_pairs={{0,8},{1,33},{2,10},{3,35},{4,12},{5,37},{6,14},{7,39},{8,16},{9,4... | collective-permute-start | bytes 811016 | tf_op jit(solution)/shard_map/ppermute | solution.py:39
  131.3 6.8 %collective-permute-start.36 = (f32[2,264,128]{2,1,0:T(8,128)S(1)}, f32[2,264,128]{2,1,0:T(8,128)S(1)}, u32[]{:S(2)}, u32[]{:S(2)}) collective-permute-start(f32[2,264,128]{2,1,0:T(8,128)S(1)} %collective-permute-done.35.p3), channel_id=1, source_target_pairs={{0,24},{1,97},{2,26},{3,99},{4,28},{5,101},{6,30},{7,103},{8,0},{9... | collective-permute-start | bytes 811016 | tf_op jit(solution)/shard_map/ppermute | solution.py:39
  140.6 5.9 %collective-permute-start.39 = (f32[4,264,128]{2,1,0:T(8,128)S(1)}, f32[4,264,128]{2,1,0:T(8,128)S(1)}, u32[]{:S(2)}, u32[]{:S(2)}) collective-permute-start(f32[4,264,128]{2,1,0:T(8,128)S(1)} %get-tuple-element.39), channel_id=1, source_target_pairs={{0,1},{1,0},{2,3},{3,2},{4,5},{5,4},{6,7},{7,6},{8,9},{9,8},{10,11... | collective-permute-start | bytes 1622024 | tf_op jit(solution)/shard_map/ppermute | solution.py:65
  146.6 6.4 %collective-permute-start.42 = (f32[264,128]{1,0:T(8,128)S(1)}, f32[264,128]{1,0:T(8,128)S(1)}, u32[]{:S(2)}, u32[]{:S(2)}) collective-permute-start(f32[264,128]{1,0:T(8,128)S(1)} %get-tuple-element.50), channel_id=1, source_target_pairs={{0,4},{2,6},{4,0},{6,2},{1,5},{3,7},{5,1},{7,3},{8,12},{10,14},{12... | collective-permute-start | bytes 405512 | tf_op jit(solution)/shard_map/ppermute | solution.py:69
  146.8 6.7 %collective-permute-start.41 = (f32[264,128]{1,0:T(8,128)S(1)}, f32[264,128]{1,0:T(8,128)S(1)}, u32[]{:S(2)}, u32[]{:S(2)}) collective-permute-start(f32[264,128]{1,0:T(8,128)S(1)} %get-tuple-element.51), channel_id=1, source_target_pairs={{0,6},{2,0},{4,2},{6,4},{1,7},{3,1},{5,3},{7,5},{8,14},{10,8},{12,... | collective-permute-start | bytes 405512 | tf_op jit(solution)/shard_map/ppermute | solution.py:69
  148.3 7.9 %collective-permute-start.40 = (f32[264,128]{1,0:T(8,128)S(1)}, f32[264,128]{1,0:T(8,128)S(1)}, u32[]{:S(2)}, u32[]{:S(2)}) collective-permute-start(f32[264,128]{1,0:T(8,128)S(1)} %get-tuple-element.52), channel_id=1, source_target_pairs={{0,2},{2,4},{4,6},{6,0},{1,3},{3,5},{5,7},{7,1},{8,10},{10,12},{12... | collective-permute-start | bytes 405512 | tf_op jit(solution)/shard_map/ppermute | solution.py:69

commit v5 on v4

--- a/solution.py
+++ b/solution.py
@@ -190,8 +190,13 @@
     list_ref[SLOTS_OUT - 1] = n
     for load in loads[0:18]:
         load.wait()
-    facts = pltpu.make_async_copy(fin_ref, facts_ref, fact_sem)
-    facts.start()
+
+    @pl.when(n > KEPT)
+    def _():
+        facts = pltpu.make_async_copy(fin_ref, facts_ref, fact_sem)
+        facts.start()
+        facts.wait()
+
     for place in range(16):
         split_into(xs_ref, place, slice(None), x_ref[place])
 
@@ -231,7 +236,6 @@
 
     keep_ref[...] = acc_ref[0:4]
     other_ref[...] = acc_ref[4:8]
-    facts.wait()
 
 
 DEPTH = 4

time: 173 us -> 174 us (level); the launches traced: 174 us -> 172 us
  starting transfers between devices: 68.9 us -> 61.8 us
  waiting for transfers between devices: 62.2 us -> 66.7 us
  Pallas kernels: 22.9 us -> 25.2 us
  blocking collectives: 16.5 us -> 14.7 us
    ppermute x27, starting transfers between devices: 38 us -> 24.5 us  [hop(): return lax.ppermute(a, ALL, along_row(stage, step))]
    ppermute x4, starting transfers between devices: 15.3 us -> 22.5 us  [swap_core(): return lax.ppermute(a, C, [(0, 1), (1, 0)])]
    pallas_call x2, Pallas kernels: 5.53 us -> 9.28 us  [later_operate(): pl.pallas_call(near_kernel, out_shape=ACC, in_specs=[SMEM, SMEM] + [VMEM]...]
    pallas_call x2, Pallas kernels: 5.04 us -> 1.7 us  [later_operate(): pl.pallas_call(far_kernel, out_shape=[PART, PART], in_specs=[SMEM, SMEM]...]
    ppermute x27, waiting for transfers between devices: 24.8 us -> 27.4 us  [hop(): return lax.ppermute(a, ALL, along_row(stage, step))]
    pallas_call x1, Pallas kernels: 9.15 us -> 11.1 us  [first_operate(): pl.pallas_call(first_kernel, out_shape=[PART, PART, jax.ShapeDtypeStruct(...]
    ppermute x12, waiting for transfers between devices: 23.2 us -> 25.1 us  [shift_y(): return lax.ppermute(a, Y, [(i, (i + step) % 4) for i in range(4)])]
    all_to_all x1, blocking collectives: 16.5 us -> 14.7 us  [to_everyone(): return lax.all_to_all(copies, axes, split_axis=0, concat_axis=0, tiled=True)]
  transfers between devices with their start and end apart: 44 -> 44, of which waited for: 29 -> 25; matrix products, arithmetic and copies ran while one was open for 1% -> 1% of each run, Pallas kernels for 3% -> 5%
where the time goes in v5:
time: 174 us; the launch traced here: 172 us
  waiting for transfers between devices  66.7 us (38%)
  starting transfers between devices  61.8 us (36%)
  Pallas kernels  25.2 us (14%)
  blocking collectives  14.7 us (8%)
    ppermute x27, waiting for transfers between devices, hop(): return lax.ppermute(a, ALL, along_row(stage, step))  27.4 us
    ppermute x12, waiting for transfers between devices, shift_y(): return lax.ppermute(a, Y, [(i, (i + step) % 4) for i in range(4)])  25.1 us
    ppermute x27, starting transfers between devices, hop(): return lax.ppermute(a, ALL, along_row(stage, step))  24.5 us
    ppermute x4, starting transfers between devices, swap_core(): return lax.ppermute(a, C, [(0, 1), (1, 0)])  22.5 us
    all_to_all x1, blocking collectives, to_everyone(): return lax.all_to_all(copies, axes, split_axis=0, concat_axis=0, tiled=True)  14.7 us
    pallas_call x1, Pallas kernels, first_operate(): pl.pallas_call(first_kernel, out_shape=[PART, PART, jax.ShapeDtypeStruct(...  11.1 us
    ppermute x12, starting transfers between devices, shift_y(): return lax.ppermute(a, Y, [(i, (i + step) % 4) for i in range(4)])  10.7 us
    all_to_all x1, waiting for transfers between devices, shards(): cells = lax.all_to_all(cells, ROW, split_axis=0, concat_axis=0, tiled=True)  9.53 us
  transfers between devices with their start and end apart: 44, of which 25 were waited for; matrix products, arithmetic and copies ran while one was open for 1% of the time, Pallas kernels for 5%

profile of v5, /device:TPU:1, one launch (start us, length us, event | category | flops | bytes accessed | tf_op | source)
XLA Modules:
  0.0 172.0 jit_solution(11796727492353811120)
XLA Ops:
  1.4 1.6 shard_map.77
  3.0 2.2 %collective-permute-start.11 = (f32[72,512]{1,0:T(8,128)S(1)}, f32[72,512]{1,0:T(8,128)S(1)}, u32[]{:S(2)}, u32[]{:S(2)}) collective-permute-start(f32[72,512]{1,0:T(8,128)S(1)} %get-tuple-element.27), channel_id=1, source_target_pairs={{0,2},{2,4},{4,6},{6,0},{1,3},{3,5},{5,7},{7,1},{8,10},{10,12},{12... | collective-permute-start | bytes 442376 | tf_op jit(solution)/shard_map/ppermute | solution.py:69
  5.2 2.6 %collective-permute-start.10 = (f32[72,512]{1,0:T(8,128)S(1)}, f32[72,512]{1,0:T(8,128)S(1)}, u32[]{:S(2)}, u32[]{:S(2)}) collective-permute-start(f32[72,512]{1,0:T(8,128)S(1)} %get-tuple-element.27), channel_id=1, source_target_pairs={{0,4},{2,6},{4,0},{6,2},{1,5},{3,7},{5,1},{7,3},{8,12},{10,14},{12... | collective-permute-start | bytes 442376 | tf_op jit(solution)/shard_map/ppermute | solution.py:69
  7.8 1.6 collective-permute-start.2
  9.5 3.3 %collective-permute-start.1 = (f32[136,512]{1,0:T(8,128)S(1)}, f32[136,512]{1,0:T(8,128)S(1)}, u32[]{:S(2)}, u32[]{:S(2)}) collective-permute-start(f32[136,512]{1,0:T(8,128)S(1)} %get-tuple-element.26), channel_id=1, source_target_pairs={{0,64},{1,17},{2,66},{3,19},{4,68},{5,21},{6,70},{7,23},{8,72},{9,... | collective-permute-start | bytes 835592 | tf_op jit(solution)/shard_map/ppermute | solution.py:39
  14.2 5.2 %collective-permute-done = f32[136,512]{1,0:T(8,128)S(1)} collective-permute-done((f32[136,512]{1,0:T(8,128)S(1)}, f32[136,512]{1,0:T(8,128)S(1)}, u32[]{:S(2)}, u32[]{:S(2)}) %collective-permute-start) | collective-permute-done | bytes 278560 | tf_op jit(solution)/shard_map/ppermute | solution.py:39
  20.5 1.3 collective-permute-start.5
  21.8 1.5 collective-permute-start.4
  23.4 3.0 %collective-permute-start.12 = (f32[4,72,512]{2,1,0:T(8,128)S(1)}, f32[4,72,512]{2,1,0:T(8,128)S(1)}, u32[]{:S(2)}, u32[]{:S(2)}) collective-permute-start(f32[4,72,512]{2,1,0:T(8,128)S(1)} %pad_maximum_fusion.same), channel_id=1, source_target_pairs={{0,1},{1,0},{2,3},{3,2},{4,5},{5,4},{6,7},{7,6},{8,9},{9,8},{10,11... | collective-permute-start | bytes 1769480 | tf_op jit(solution)/shard_map/ppermute | solution.py:65
  26.5 2.4 %collective-permute-start.3 = (f32[2,136,512]{2,1,0:T(8,128)S(1)}, f32[2,136,512]{2,1,0:T(8,128)}, u32[]{:S(2)}, u32[]{:S(2)}) collective-permute-start(f32[2,136,512]{2,1,0:T(8,128)S(1)} %pad_maximum_fusion.1.p0), channel_id=1, source_target_pairs={{0,24},{1,97},{2,26},{3,99},{4,28},{5,101},{6,30},{7,103},{8,0},{9... | collective-permute-start | bytes 1671176 | tf_op jit(solution)/shard_map/ppermute | solution.py:39
  28.9 1.6 collective-permute-done.5.p6
  30.7 2.6 %collective-permute-start.7 = (f32[2,136,512]{2,1,0:T(8,128)}, f32[2,136,512]{2,1,0:T(8,128)}, u32[]{:S(2)}, u32[]{:S(2)}) collective-permute-start(f32[2,136,512]{2,1,0:T(8,128)} %collective-permute-done.4.p3), channel_id=1, source_target_pairs={{0,24},{1,97},{2,26},{3,99},{4,28},{5,101},{6,30},{7,103},{8,0},{9... | collective-permute-start | bytes 1671176 | tf_op jit(solution)/shard_map/ppermute | solution.py:39
  33.9 4.1 %all-to-all-start = ((f32[16,8,128]{2,1,0:T(8,128)}), f32[16,8,128]{2,1,0:T(8,128)S(1)}, u32[]{:S(2)}, u32[]{:S(2)}) async-start(f32[16,8,128]{2,1,0:T(8,128)} %broadcast_in_dim.47), calls=%async_computation | async-start | bytes 131072 | tf_op jit(solution)/shard_map/all_to_all | solution.py:585
  38.1 9.5 %all-to-all-done.cells = f32[16,8,128]{2,1,0:T(8,128)S(1)} async-done(((f32[16,8,128]{2,1,0:T(8,128)}), f32[16,8,128]{2,1,0:T(8,128)S(1)}, u32[]{:S(2)}, u32[]{:S(2)}) %all-to-all-start) | async-done | bytes 65568 | tf_op jit(solution)/shard_map/all_to_all | solution.py:585
  47.7 11.1 %shard_map.78 = (f32[4,264,128]{2,1,0:T(8,128)S(1)}, f32[4,264,128]{2,1,0:T(8,128)S(1)}, s32[144]{0:T(256)S(1)}, bf16[48,2,512,512]{3,2,1,0:T(8,128)(2,1)}, f32[24,72,512]{2,1,0:T(8,128)S(1)}) custom-call(s32[4]{0:T(128)S(1)} %pad_add_fusion.1.place_ref, s32[1,1,8,3]{3,2,1,0:T(8,128)S(1)} %copy.13.slots_ref, f32[2,2]{1,0:T(2,128)S(1)} %log_multiply_fusion.lc_ref, ...), custom_call_target="tpu_custom_call" | custom-call | flops 8000000000 | bytes 20000000 | tf_op jit(solution)/shard_map/pallas_call | solution.py:508
  58.8 6.6 %collective-permute-start.13 = (f32[4,264,128]{2,1,0:T(8,128)S(1)}, f32[4,264,128]{2,1,0:T(8,128)S(1)}, u32[]{:S(2)}, u32[]{:S(2)}) collective-permute-start(f32[4,264,128]{2,1,0:T(8,128)S(1)} %get-tuple-element.30), channel_id=1, source_target_pairs={{0,1},{1,0},{2,3},{3,2},{4,5},{5,4},{6,7},{7,6},{8,9},{9,8},{10,11... | collective-permute-start | bytes 1622024 | tf_op jit(solution)/shard_map/ppermute | solution.py:65
  65.4 1.6 collective-permute-done.13.b
  68.6 4.8 %collective-permute-done.16 = f32[264,128]{1,0:T(8,128)S(1)} collective-permute-done((f32[264,128]{1,0:T(8,128)S(1)}, f32[264,128]{1,0:T(8,128)S(1)}, u32[]{:S(2)}, u32[]{:S(2)}) %collective-permute-start.16) | collective-permute-done | bytes 135200 | tf_op jit(solution)/shard_map/ppermute | solution.py:69
  73.4 3.6 %collective-permute-done.14 = f32[264,128]{1,0:T(8,128)S(1)} collective-permute-done((f32[264,128]{1,0:T(8,128)S(1)}, f32[264,128]{1,0:T(8,128)S(1)}, u32[]{:S(2)}, u32[]{:S(2)}) %collective-permute-start.14) | collective-permute-done | bytes 135200 | tf_op jit(solution)/shard_map/ppermute | solution.py:69
  77.2 1.5 collective-permute-start.21
  79.3 2.1 %collective-permute-done.17 = f32[264,128]{1,0:T(8,128)S(1)} collective-permute-done((f32[264,128]{1,0:T(8,128)S(1)}, f32[264,128]{1,0:T(8,128)S(1)}, u32[]{:S(2)}, u32[]{:S(2)}) %collective-permute-start.17) | collective-permute-done | bytes 135200 | tf_op jit(solution)/shard_map/ppermute | solution.py:39
  81.4 1.2 collective-permute-done.21
  82.6 2.0 %collective-permute-done.20 = f32[264,128]{1,0:T(8,128)S(1)} collective-permute-done((f32[264,128]{1,0:T(8,128)S(1)}, f32[264,128]{1,0:T(8,128)S(1)}, u32[]{:S(2)}, u32[]{:S(2)}) %collective-permute-start.20) | collective-permute-done | bytes 135200 | tf_op jit(solution)/shard_map/ppermute | solution.py:39
  84.8 1.5 collective-permute-start.25
  86.2 2.7 %collective-permute-done.18.p6 = f32[2,264,128]{2,1,0:T(8,128)S(1)} collective-permute-done((f32[2,264,128]{2,1,0:T(8,128)S(1)}, f32[2,264,128]{2,1,0:T(8,128)S(1)}, u32[]{:S(2)}, u32[]{:S(2)}) %collective-permute-start.18) | collective-permute-done | bytes 270368 | tf_op jit(solution)/shard_map/ppermute | solution.py:39
  88.9 1.4 collective-permute-done.22.p3
  90.3 1.3 collective-permute-start.23
  91.6 1.6 collective-permute-done.24.p2
  93.2 4.6 %shard_map.80.near_ref = f32[8,264,128]{2,1,0:T(8,128)S(1)} custom-call(s32[144]{0:T(256)S(1)} %get-tuple-element.28.list_ref, f32[2,2]{1,0:T(2,128)S(1)} %log_multiply_fusion.lc_ref, f32[2,264,128]{2,1,0:T(8,128)S(1)} %pad_maximum_fusion.3.p0, f32[2,264,128]{2,1,0:T(8,128)S(1)} %pad_maximum_fusion.4.p1, f32[2,264,128]{2,1,0:T(8,128)S(1)} %collective-permute-done.24.p2, ...), custom_call_target="tpu_custom_call" | custom-call | flops 3000000000 | bytes 12000000 | tf_op jit(solution)/shard_map/pallas_call | solution.py:552
  98.7 5.7 %collective-permute-start.26 = (f32[4,264,128]{2,1,0:T(8,128)S(1)}, f32[4,264,128]{2,1,0:T(8,128)S(1)}, u32[]{:S(2)}, u32[]{:S(2)}) collective-permute-start(f32[4,264,128]{2,1,0:T(8,128)S(1)} %get-tuple-element.35), channel_id=1, source_target_pairs={{0,1},{1,0},{2,3},{3,2},{4,5},{5,4},{6,7},{7,6},{8,9},{9,8},{10,11... | collective-permute-start | bytes 1622024 | tf_op jit(solution)/shard_map/ppermute | solution.py:65
  104.5 1.6 collective-permute-done.26.b
  106.2 1.5 collective-permute-start.27
  107.7 4.8 %collective-permute-done.29 = f32[264,128]{1,0:T(8,128)S(1)} collective-permute-done((f32[264,128]{1,0:T(8,128)S(1)}, f32[264,128]{1,0:T(8,128)S(1)}, u32[]{:S(2)}, u32[]{:S(2)}) %collective-permute-start.29) | collective-permute-done | bytes 135200 | tf_op jit(solution)/shard_map/ppermute | solution.py:69
  112.5 3.6 %collective-permute-done.27 = f32[264,128]{1,0:T(8,128)S(1)} collective-permute-done((f32[264,128]{1,0:T(8,128)S(1)}, f32[264,128]{1,0:T(8,128)S(1)}, u32[]{:S(2)}, u32[]{:S(2)}) %collective-permute-start.27) | collective-permute-done | bytes 135200 | tf_op jit(solution)/shard_map/ppermute | solution.py:69
  116.4 1.5 collective-permute-start.34
  118.2 2.3 %collective-permute-done.30 = f32[264,128]{1,0:T(8,128)S(1)} collective-permute-done((f32[264,128]{1,0:T(8,128)S(1)}, f32[264,128]{1,0:T(8,128)S(1)}, u32[]{:S(2)}, u32[]{:S(2)}) %collective-permute-start.30) | collective-permute-done | bytes 135200 | tf_op jit(solution)/shard_map/ppermute | solution.py:39
  120.6 1.2 collective-permute-done.34
  121.8 1.4 collective-permute-done.33
  123.4 1.3 collective-permute-start.37
  124.8 3.6 %collective-permute-done.31.p6 = f32[2,264,128]{2,1,0:T(8,128)S(1)} collective-permute-done((f32[2,264,128]{2,1,0:T(8,128)S(1)}, f32[2,264,128]{2,1,0:T(8,128)S(1)}, u32[]{:S(2)}, u32[]{:S(2)}) %collective-permute-start.31) | collective-permute-done | bytes 270368 | tf_op jit(solution)/shard_map/ppermute | solution.py:39
  128.9 2.2 %collective-permute-start.36 = (f32[2,264,128]{2,1,0:T(8,128)S(1)}, f32[2,264,128]{2,1,0:T(8,128)S(1)}, u32[]{:S(2)}, u32[]{:S(2)}) collective-permute-start(f32[2,264,128]{2,1,0:T(8,128)S(1)} %collective-permute-done.35.p3), channel_id=1, source_target_pairs={{0,24},{1,97},{2,26},{3,99},{4,28},{5,101},{6,30},{7,103},{8,0},{9... | collective-permute-start | bytes 811016 | tf_op jit(solution)/shard_map/ppermute | solution.py:39
  131.8 4.6 %shard_map.83.near_ref = f32[8,264,128]{2,1,0:T(8,128)S(1)} custom-call(s32[144]{0:T(256)S(1)} %get-tuple-element.28.list_ref, f32[2,2]{1,0:T(2,128)S(1)} %log_multiply_fusion.lc_ref, f32[2,264,128]{2,1,0:T(8,128)S(1)} %pad_maximum_fusion.5.p0, f32[2,264,128]{2,1,0:T(8,128)S(1)} %pad_maximum_fusion.6.p1, f32[2,264,128]{2,1,0:T(8,128)S(1)} %collective-permute-done.37.p2, ...), custom_call_target="tpu_custom_call" | custom-call | flops 3000000000 | bytes 12000000 | tf_op jit(solution)/shard_map/pallas_call | solution.py:552
  137.3 7.1 %collective-permute-start.39 = (f32[4,264,128]{2,1,0:T(8,128)S(1)}, f32[4,264,128]{2,1,0:T(8,128)S(1)}, u32[]{:S(2)}, u32[]{:S(2)}) collective-permute-start(f32[4,264,128]{2,1,0:T(8,128)S(1)} %get-tuple-element.39), channel_id=1, source_target_pairs={{0,1},{1,0},{2,3},{3,2},{4,5},{5,4},{6,7},{7,6},{8,9},{9,8},{10,11... | collective-permute-start | bytes 1622024 | tf_op jit(solution)/shard_map/ppermute | solution.py:65
  144.4 1.6 collective-permute-done.39.b
  146.2 1.5 collective-permute-start.40
  147.7 4.8 %collective-permute-done.42 = f32[264,128]{1,0:T(8,128)S(1)} collective-permute-done((f32[264,128]{1,0:T(8,128)S(1)}, f32[264,128]{1,0:T(8,128)S(1)}, u32[]{:S(2)}, u32[]{:S(2)}) %collective-permute-start.42) | collective-permute-done | bytes 135200 | tf_op jit(solution)/shard_map/ppermute | solution.py:69
  152.5 3.6 %collective-permute-done.40 = f32[264,128]{1,0:T(8,128)S(1)} collective-permute-done((f32[264,128]{1,0:T(8,128)S(1)}, f32[264,128]{1,0:T(8,128)S(1)}, u32[]{:S(2)}, u32[]{:S(2)}) %collective-permute-start.40) | collective-permute-done | bytes 135200 | tf_op jit(solution)/shard_map/ppermute | solution.py:69
  156.4 14.7 %all_to_all.10 = f32[128,1,128]{2,1,0:T(1,128)S(1)} all-to-all(f32[128,1,128]{2,1,0:T(1,128)S(1)} %broadcast_in_dim.59), channel_id=1, replica_groups=mesh['row_0'=4,'row_1'=4,'col_0'=4,'col_1'=2] {'row_0','row_1','col_0','..., dimensions={0} | all-to-all | bytes 131072 | tf_op jit(solution)/shard_map/all_to_all | solution.py:574
  (78 shorter events, 12.8 us)
Async XLA Ops:
  3.0 20.4 %collective-permute-start.11 = (f32[72,512]{1,0:T(8,128)S(1)}, f32[72,512]{1,0:T(8,128)S(1)}, u32[]{:S(2)}, u32[]{:S(2)}) collective-permute-start(f32[72,512]{1,0:T(8,128)S(1)} %get-tuple-element.27), channel_id=1, source_target_pairs={{0,2},{2,4},{4,6},{6,0},{1,3},{3,5},{5,7},{7,1},{8,10},{10,12},{12... | collective-permute-start | bytes 442376 | tf_op jit(solution)/shard_map/ppermute | solution.py:69
  5.2 18.2 %collective-permute-start.10 = (f32[72,512]{1,0:T(8,128)S(1)}, f32[72,512]{1,0:T(8,128)S(1)}, u32[]{:S(2)}, u32[]{:S(2)}) collective-permute-start(f32[72,512]{1,0:T(8,128)S(1)} %get-tuple-element.27), channel_id=1, source_target_pairs={{0,4},{2,6},{4,0},{6,2},{1,5},{3,7},{5,1},{7,3},{8,12},{10,14},{12... | collective-permute-start | bytes 442376 | tf_op jit(solution)/shard_map/ppermute | solution.py:69
  7.8 12.7 %collective-permute-start.2 = (f32[136,512]{1,0:T(8,128)S(1)}, f32[136,512]{1,0:T(8,128)S(1)}, u32[]{:S(2)}, u32[]{:S(2)}) collective-permute-start(f32[136,512]{1,0:T(8,128)S(1)} %get-tuple-element.26), channel_id=1, source_target_pairs={{0,32},{1,9},{2,34},{3,11},{4,36},{5,13},{6,38},{7,15},{8,40},{9,1... | collective-permute-start | bytes 835592 | tf_op jit(solution)/shard_map/ppermute | solution.py:39
  9.5 12.3 %collective-permute-start.1 = (f32[136,512]{1,0:T(8,128)S(1)}, f32[136,512]{1,0:T(8,128)S(1)}, u32[]{:S(2)}, u32[]{:S(2)}) collective-permute-start(f32[136,512]{1,0:T(8,128)S(1)} %get-tuple-element.26), channel_id=1, source_target_pairs={{0,64},{1,17},{2,66},{3,19},{4,68},{5,21},{6,70},{7,23},{8,72},{9,... | collective-permute-start | bytes 835592 | tf_op jit(solution)/shard_map/ppermute | solution.py:39
  12.8 6.6 %collective-permute-start = (f32[136,512]{1,0:T(8,128)S(1)}, f32[136,512]{1,0:T(8,128)S(1)}, u32[]{:S(2)}, u32[]{:S(2)}) collective-permute-start(f32[136,512]{1,0:T(8,128)S(1)} %get-tuple-element.26), channel_id=1, source_target_pairs={{0,96},{1,25},{2,98},{3,27},{4,100},{5,29},{6,102},{7,31},{8,104},... | collective-permute-start | bytes 835592 | tf_op jit(solution)/shard_map/ppermute | solution.py:39
  19.4 4.0 %collective-permute-start.9 = (f32[72,512]{1,0:T(8,128)S(1)}, f32[72,512]{1,0:T(8,128)S(1)}, u32[]{:S(2)}, u32[]{:S(2)}) collective-permute-start(f32[72,512]{1,0:T(8,128)S(1)} %get-tuple-element.27), channel_id=1, source_target_pairs={{0,6},{2,0},{4,2},{6,4},{1,7},{3,1},{5,3},{7,5},{8,14},{10,8},{12,... | collective-permute-start | bytes 442376 | tf_op jit(solution)/shard_map/ppermute | solution.py:69
  20.5 10.0 %collective-permute-start.5 = (f32[2,136,512]{2,1,0:T(8,128)S(1)}, f32[2,136,512]{2,1,0:T(8,128)S(1)}, u32[]{:S(2)}, u32[]{:S(2)}) collective-permute-start(f32[2,136,512]{2,1,0:T(8,128)S(1)} %pad_maximum_fusion.1.p0), channel_id=1, source_target_pairs={{0,8},{1,33},{2,10},{3,35},{4,12},{5,37},{6,14},{7,39},{8,16},{9,4... | collective-permute-start | bytes 1671176 | tf_op jit(solution)/shard_map/ppermute | solution.py:39
  21.8 8.9 %collective-permute-start.4 = (f32[2,136,512]{2,1,0:T(8,128)S(1)}, f32[2,136,512]{2,1,0:T(8,128)}, u32[]{:S(2)}, u32[]{:S(2)}) collective-permute-start(f32[2,136,512]{2,1,0:T(8,128)S(1)} %pad_maximum_fusion.2.p1), channel_id=1, source_target_pairs={{0,24},{1,97},{2,26},{3,99},{4,28},{5,101},{6,30},{7,103},{8,0},{9... | collective-permute-start | bytes 1671176 | tf_op jit(solution)/shard_map/ppermute | solution.py:39
  23.4 9.8 %collective-permute-start.12 = (f32[4,72,512]{2,1,0:T(8,128)S(1)}, f32[4,72,512]{2,1,0:T(8,128)S(1)}, u32[]{:S(2)}, u32[]{:S(2)}) collective-permute-start(f32[4,72,512]{2,1,0:T(8,128)S(1)} %pad_maximum_fusion.same), channel_id=1, source_target_pairs={{0,1},{1,0},{2,3},{3,2},{4,5},{5,4},{6,7},{7,6},{8,9},{9,8},{10,11... | collective-permute-start | bytes 1769480 | tf_op jit(solution)/shard_map/ppermute | solution.py:65
  26.5 21.2 %collective-permute-start.3 = (f32[2,136,512]{2,1,0:T(8,128)S(1)}, f32[2,136,512]{2,1,0:T(8,128)}, u32[]{:S(2)}, u32[]{:S(2)}) collective-permute-start(f32[2,136,512]{2,1,0:T(8,128)S(1)} %pad_maximum_fusion.1.p0), channel_id=1, source_target_pairs={{0,24},{1,97},{2,26},{3,99},{4,28},{5,101},{6,30},{7,103},{8,0},{9... | collective-permute-start | bytes 1671176 | tf_op jit(solution)/shard_map/ppermute | solution.py:39
  28.9 18.8 %collective-permute-start.8 = (f32[2,136,512]{2,1,0:T(8,128)S(1)}, f32[2,136,512]{2,1,0:T(8,128)}, u32[]{:S(2)}, u32[]{:S(2)}) collective-permute-start(f32[2,136,512]{2,1,0:T(8,128)S(1)} %pad_maximum_fusion.2.p1), channel_id=1, source_target_pairs={{0,8},{1,33},{2,10},{3,35},{4,12},{5,37},{6,14},{7,39},{8,16},{9,4... | collective-permute-start | bytes 1671176 | tf_op jit(solution)/shard_map/ppermute | solution.py:39
  30.5 17.2 %collective-permute-start.6 = (f32[2,136,512]{2,1,0:T(8,128)S(1)}, f32[2,136,512]{2,1,0:T(8,128)}, u32[]{:S(2)}, u32[]{:S(2)}) collective-permute-start(f32[2,136,512]{2,1,0:T(8,128)S(1)} %collective-permute-done.5.p6), channel_id=1, source_target_pairs={{0,8},{1,33},{2,10},{3,35},{4,12},{5,37},{6,14},{7,39},{8,16},{9,4... | collective-permute-start | bytes 1671176 | tf_op jit(solution)/shard_map/ppermute | solution.py:39
  30.7 17.0 %collective-permute-start.7 = (f32[2,136,512]{2,1,0:T(8,128)}, f32[2,136,512]{2,1,0:T(8,128)}, u32[]{:S(2)}, u32[]{:S(2)}) collective-permute-start(f32[2,136,512]{2,1,0:T(8,128)} %collective-permute-done.4.p3), channel_id=1, source_target_pairs={{0,24},{1,97},{2,26},{3,99},{4,28},{5,101},{6,30},{7,103},{8,0},{9... | collective-permute-start | bytes 1671176 | tf_op jit(solution)/shard_map/ppermute | solution.py:39
  33.9 13.7 %all-to-all-start = ((f32[16,8,128]{2,1,0:T(8,128)}), f32[16,8,128]{2,1,0:T(8,128)S(1)}, u32[]{:S(2)}, u32[]{:S(2)}) async-start(f32[16,8,128]{2,1,0:T(8,128)} %broadcast_in_dim.47), calls=%async_computation | async-start | bytes 131072 | tf_op jit(solution)/shard_map/all_to_all | solution.py:585
  38.1 38.9 %copy-start = (f32[64,512]{1,0:T(8,128)S(1)}, f32[64,512]{1,0:T(8,128)}, u32[]{:S(2)}) copy-start(f32[64,512]{1,0:T(8,128)} %r_ref.5) | copy-start | bytes 393220
  38.1 38.9 %copy-start.1 = (f32[512]{0:T(512)S(1)}, f32[512]{0:T(512)}, u32[]{:S(2)}) copy-start(f32[512]{0:T(512)} %param.9) | copy-start | bytes 6148
  58.8 8.2 %collective-permute-start.13 = (f32[4,264,128]{2,1,0:T(8,128)S(1)}, f32[4,264,128]{2,1,0:T(8,128)S(1)}, u32[]{:S(2)}, u32[]{:S(2)}) collective-permute-start(f32[4,264,128]{2,1,0:T(8,128)S(1)} %get-tuple-element.30), channel_id=1, source_target_pairs={{0,1},{1,0},{2,3},{3,2},{4,5},{5,4},{6,7},{7,6},{8,9},{9,8},{10,11... | collective-permute-start | bytes 1622024 | tf_op jit(solution)/shard_map/ppermute | solution.py:65
  67.0 6.4 %collective-permute-start.16 = (f32[264,128]{1,0:T(8,128)S(1)}, f32[264,128]{1,0:T(8,128)S(1)}, u32[]{:S(2)}, u32[]{:S(2)}) collective-permute-start(f32[264,128]{1,0:T(8,128)S(1)} %get-tuple-element.56), channel_id=1, source_target_pairs={{0,4},{2,6},{4,0},{6,2},{1,5},{3,7},{5,1},{7,3},{8,12},{10,14},{12... | collective-permute-start | bytes 405512 | tf_op jit(solution)/shard_map/ppermute | solution.py:69
  67.1 6.3 %collective-permute-start.15 = (f32[264,128]{1,0:T(8,128)S(1)}, f32[264,128]{1,0:T(8,128)S(1)}, u32[]{:S(2)}, u32[]{:S(2)}) collective-permute-start(f32[264,128]{1,0:T(8,128)S(1)} %get-tuple-element.57), channel_id=1, source_target_pairs={{0,6},{2,0},{4,2},{6,4},{1,7},{3,1},{5,3},{7,5},{8,14},{10,8},{12,... | collective-permute-start | bytes 405512 | tf_op jit(solution)/shard_map/ppermute | solution.py:69
  67.6 9.4 %collective-permute-start.14 = (f32[264,128]{1,0:T(8,128)S(1)}, f32[264,128]{1,0:T(8,128)S(1)}, u32[]{:S(2)}, u32[]{:S(2)}) collective-permute-start(f32[264,128]{1,0:T(8,128)S(1)} %get-tuple-element.58), channel_id=1, source_target_pairs={{0,2},{2,4},{4,6},{6,0},{1,3},{3,5},{5,7},{7,1},{8,10},{10,12},{12... | collective-permute-start | bytes 405512 | tf_op jit(solution)/shard_map/ppermute | solution.py:69
  77.2 4.2 %collective-permute-start.17 = (f32[264,128]{1,0:T(8,128)S(1)}, f32[264,128]{1,0:T(8,128)S(1)}, u32[]{:S(2)}, u32[]{:S(2)}) collective-permute-start(f32[264,128]{1,0:T(8,128)S(1)} %get-tuple-element.31.w_ref.w0_ref), channel_id=1, source_target_pairs={{0,96},{1,25},{2,98},{3,27},{4,100},{5,29},{6,102},{7,31},{8,104},... | collective-permute-start | bytes 405512 | tf_op jit(solution)/shard_map/ppermute | solution.py:39
  77.2 5.4 %collective-permute-start.21 = (f32[264,128]{1,0:T(8,128)S(1)}, f32[264,128]{1,0:T(8,128)S(1)}, u32[]{:S(2)}, u32[]{:S(2)}) collective-permute-start(f32[264,128]{1,0:T(8,128)S(1)} %get-tuple-element.31.w_ref.w0_ref), channel_id=1, source_target_pairs={{0,32},{1,9},{2,34},{3,11},{4,36},{5,13},{6,38},{7,15},{8,40},{9,1... | collective-permute-start | bytes 405512 | tf_op jit(solution)/shard_map/ppermute | solution.py:39
  78.6 6.0 %collective-permute-start.20 = (f32[264,128]{1,0:T(8,128)S(1)}, f32[264,128]{1,0:T(8,128)S(1)}, u32[]{:S(2)}, u32[]{:S(2)}) collective-permute-start(f32[264,128]{1,0:T(8,128)S(1)} %get-tuple-element.31.w_ref.w0_ref), channel_id=1, source_target_pairs={{0,64},{1,17},{2,66},{3,19},{4,68},{5,21},{6,70},{7,23},{8,72},{9,... | collective-permute-start | bytes 405512 | tf_op jit(solution)/shard_map/ppermute | solution.py:39
  81.4 7.6 %collective-permute-start.18 = (f32[2,264,128]{2,1,0:T(8,128)S(1)}, f32[2,264,128]{2,1,0:T(8,128)S(1)}, u32[]{:S(2)}, u32[]{:S(2)}) collective-permute-start(f32[2,264,128]{2,1,0:T(8,128)S(1)} %pad_maximum_fusion.3.p0), channel_id=1, source_target_pairs={{0,8},{1,33},{2,10},{3,35},{4,12},{5,37},{6,14},{7,39},{8,16},{9,4... | collective-permute-start | bytes 811016 | tf_op jit(solution)/shard_map/ppermute | solution.py:39
  84.6 5.7 %collective-permute-start.22 = (f32[2,264,128]{2,1,0:T(8,128)S(1)}, f32[2,264,128]{2,1,0:T(8,128)S(1)}, u32[]{:S(2)}, u32[]{:S(2)}) collective-permute-start(f32[2,264,128]{2,1,0:T(8,128)S(1)} %pad_maximum_fusion.4.p1), channel_id=1, source_target_pairs={{0,24},{1,97},{2,26},{3,99},{4,28},{5,101},{6,30},{7,103},{8,0},{9... | collective-permute-start | bytes 811016 | tf_op jit(solution)/shard_map/ppermute | solution.py:39
  84.7 8.5 %collective-permute-start.24 = (f32[2,264,128]{2,1,0:T(8,128)S(1)}, f32[2,264,128]{2,1,0:T(8,128)S(1)}, u32[]{:S(2)}, u32[]{:S(2)}) collective-permute-start(f32[2,264,128]{2,1,0:T(8,128)S(1)} %pad_maximum_fusion.3.p0), channel_id=1, source_target_pairs={{0,24},{1,97},{2,26},{3,99},{4,28},{5,101},{6,30},{7,103},{8,0},{9... | collective-permute-start | bytes 811016 | tf_op jit(solution)/shard_map/ppermute | solution.py:39
  84.8 8.4 %collective-permute-start.25 = (f32[2,264,128]{2,1,0:T(8,128)S(1)}, f32[2,264,128]{2,1,0:T(8,128)S(1)}, u32[]{:S(2)}, u32[]{:S(2)}) collective-permute-start(f32[2,264,128]{2,1,0:T(8,128)S(1)} %pad_maximum_fusion.4.p1), channel_id=1, source_target_pairs={{0,8},{1,33},{2,10},{3,35},{4,12},{5,37},{6,14},{7,39},{8,16},{9,4... | collective-permute-start | bytes 811016 | tf_op jit(solution)/shard_map/ppermute | solution.py:39
  88.9 8.9 %collective-permute-start.19 = (f32[2,264,128]{2,1,0:T(8,128)S(1)}, f32[2,264,128]{2,1,0:T(8,128)S(1)}, u32[]{:S(2)}, u32[]{:S(2)}) collective-permute-start(f32[2,264,128]{2,1,0:T(8,128)S(1)} %collective-permute-done.18.p6), channel_id=1, source_target_pairs={{0,8},{1,33},{2,10},{3,35},{4,12},{5,37},{6,14},{7,39},{8,16},{9,4... | collective-permute-start | bytes 811016 | tf_op jit(solution)/shard_map/ppermute | solution.py:39
  90.3 7.6 %collective-permute-start.23 = (f32[2,264,128]{2,1,0:T(8,128)S(1)}, f32[2,264,128]{2,1,0:T(8,128)S(1)}, u32[]{:S(2)}, u32[]{:S(2)}) collective-permute-start(f32[2,264,128]{2,1,0:T(8,128)S(1)} %collective-permute-done.22.p3), channel_id=1, source_target_pairs={{0,24},{1,97},{2,26},{3,99},{4,28},{5,101},{6,30},{7,103},{8,0},{9... | collective-permute-start | bytes 811016 | tf_op jit(solution)/shard_map/ppermute | solution.py:39
  98.7 7.3 %collective-permute-start.26 = (f32[4,264,128]{2,1,0:T(8,128)S(1)}, f32[4,264,128]{2,1,0:T(8,128)S(1)}, u32[]{:S(2)}, u32[]{:S(2)}) collective-permute-start(f32[4,264,128]{2,1,0:T(8,128)S(1)} %get-tuple-element.35), channel_id=1, source_target_pairs={{0,1},{1,0},{2,3},{3,2},{4,5},{5,4},{6,7},{7,6},{8,9},{9,8},{10,11... | collective-permute-start | bytes 1622024 | tf_op jit(solution)/shard_map/ppermute | solution.py:65
  106.1 6.4 %collective-permute-start.29 = (f32[264,128]{1,0:T(8,128)S(1)}, f32[264,128]{1,0:T(8,128)S(1)}, u32[]{:S(2)}, u32[]{:S(2)}) collective-permute-start(f32[264,128]{1,0:T(8,128)S(1)} %get-tuple-element.53), channel_id=1, source_target_pairs={{0,4},{2,6},{4,0},{6,2},{1,5},{3,7},{5,1},{7,3},{8,12},{10,14},{12... | collective-permute-start | bytes 405512 | tf_op jit(solution)/shard_map/ppermute | solution.py:69
  106.2 6.3 %collective-permute-start.28 = (f32[264,128]{1,0:T(8,128)S(1)}, f32[264,128]{1,0:T(8,128)S(1)}, u32[]{:S(2)}, u32[]{:S(2)}) collective-permute-start(f32[264,128]{1,0:T(8,128)S(1)} %get-tuple-element.54), channel_id=1, source_target_pairs={{0,6},{2,0},{4,2},{6,4},{1,7},{3,1},{5,3},{7,5},{8,14},{10,8},{12,... | collective-permute-start | bytes 405512 | tf_op jit(solution)/shard_map/ppermute | solution.py:69
  106.2 9.8 %collective-permute-start.27 = (f32[264,128]{1,0:T(8,128)S(1)}, f32[264,128]{1,0:T(8,128)S(1)}, u32[]{:S(2)}, u32[]{:S(2)}) collective-permute-start(f32[264,128]{1,0:T(8,128)S(1)} %get-tuple-element.55), channel_id=1, source_target_pairs={{0,2},{2,4},{4,6},{6,0},{1,3},{3,5},{5,7},{7,1},{8,10},{10,12},{12... | collective-permute-start | bytes 405512 | tf_op jit(solution)/shard_map/ppermute | solution.py:69
  116.3 4.2 %collective-permute-start.30 = (f32[264,128]{1,0:T(8,128)S(1)}, f32[264,128]{1,0:T(8,128)S(1)}, u32[]{:S(2)}, u32[]{:S(2)}) collective-permute-start(f32[264,128]{1,0:T(8,128)S(1)} %get-tuple-element.37.w1_ref), channel_id=1, source_target_pairs={{0,96},{1,25},{2,98},{3,27},{4,100},{5,29},{6,102},{7,31},{8,104},... | collective-permute-start | bytes 405512 | tf_op jit(solution)/shard_map/ppermute | solution.py:39
  116.4 5.4 %collective-permute-start.34 = (f32[264,128]{1,0:T(8,128)S(1)}, f32[264,128]{1,0:T(8,128)S(1)}, u32[]{:S(2)}, u32[]{:S(2)}) collective-permute-start(f32[264,128]{1,0:T(8,128)S(1)} %get-tuple-element.37.w1_ref), channel_id=1, source_target_pairs={{0,32},{1,9},{2,34},{3,11},{4,36},{5,13},{6,38},{7,15},{8,40},{9,1... | collective-permute-start | bytes 405512 | tf_op jit(solution)/shard_map/ppermute | solution.py:39
  117.8 5.4 %collective-permute-start.33 = (f32[264,128]{1,0:T(8,128)S(1)}, f32[264,128]{1,0:T(8,128)S(1)}, u32[]{:S(2)}, u32[]{:S(2)}) collective-permute-start(f32[264,128]{1,0:T(8,128)S(1)} %get-tuple-element.37.w1_ref), channel_id=1, source_target_pairs={{0,64},{1,17},{2,66},{3,19},{4,68},{5,21},{6,70},{7,23},{8,72},{9,... | collective-permute-start | bytes 405512 | tf_op jit(solution)/shard_map/ppermute | solution.py:39
  120.5 7.9 %collective-permute-start.31 = (f32[2,264,128]{2,1,0:T(8,128)S(1)}, f32[2,264,128]{2,1,0:T(8,128)S(1)}, u32[]{:S(2)}, u32[]{:S(2)}) collective-permute-start(f32[2,264,128]{2,1,0:T(8,128)S(1)} %pad_maximum_fusion.5.p0), channel_id=1, source_target_pairs={{0,8},{1,33},{2,10},{3,35},{4,12},{5,37},{6,14},{7,39},{8,16},{9,4... | collective-permute-start | bytes 811016 | tf_op jit(solution)/shard_map/ppermute | solution.py:39
  123.2 5.7 %collective-permute-start.35 = (f32[2,264,128]{2,1,0:T(8,128)S(1)}, f32[2,264,128]{2,1,0:T(8,128)S(1)}, u32[]{:S(2)}, u32[]{:S(2)}) collective-permute-start(f32[2,264,128]{2,1,0:T(8,128)S(1)} %pad_maximum_fusion.6.p1), channel_id=1, source_target_pairs={{0,24},{1,97},{2,26},{3,99},{4,28},{5,101},{6,30},{7,103},{8,0},{9... | collective-permute-start | bytes 811016 | tf_op jit(solution)/shard_map/ppermute | solution.py:39
  123.4 8.4 %collective-permute-start.37 = (f32[2,264,128]{2,1,0:T(8,128)S(1)}, f32[2,264,128]{2,1,0:T(8,128)S(1)}, u32[]{:S(2)}, u32[]{:S(2)}) collective-permute-start(f32[2,264,128]{2,1,0:T(8,128)S(1)} %pad_maximum_fusion.5.p0), channel_id=1, source_target_pairs={{0,24},{1,97},{2,26},{3,99},{4,28},{5,101},{6,30},{7,103},{8,0},{9... | collective-permute-start | bytes 811016 | tf_op jit(solution)/shard_map/ppermute | solution.py:39
  124.6 7.1 %collective-permute-start.38 = (f32[2,264,128]{2,1,0:T(8,128)S(1)}, f32[2,264,128]{2,1,0:T(8,128)S(1)}, u32[]{:S(2)}, u32[]{:S(2)}) collective-permute-start(f32[2,264,128]{2,1,0:T(8,128)S(1)} %pad_maximum_fusion.6.p1), channel_id=1, source_target_pairs={{0,8},{1,33},{2,10},{3,35},{4,12},{5,37},{6,14},{7,39},{8,16},{9,4... | collective-permute-start | bytes 811016 | tf_op jit(solution)/shard_map/ppermute | solution.py:39
  128.4 8.0 %collective-permute-start.32 = (f32[2,264,128]{2,1,0:T(8,128)S(1)}, f32[2,264,128]{2,1,0:T(8,128)S(1)}, u32[]{:S(2)}, u32[]{:S(2)}) collective-permute-start(f32[2,264,128]{2,1,0:T(8,128)S(1)} %collective-permute-done.31.p6), channel_id=1, source_target_pairs={{0,8},{1,33},{2,10},{3,35},{4,12},{5,37},{6,14},{7,39},{8,16},{9,4... | collective-permute-start | bytes 811016 | tf_op jit(solution)/shard_map/ppermute | solution.py:39
  128.9 7.6 %collective-permute-start.36 = (f32[2,264,128]{2,1,0:T(8,128)S(1)}, f32[2,264,128]{2,1,0:T(8,128)S(1)}, u32[]{:S(2)}, u32[]{:S(2)}) collective-permute-start(f32[2,264,128]{2,1,0:T(8,128)S(1)} %collective-permute-done.35.p3), channel_id=1, source_target_pairs={{0,24},{1,97},{2,26},{3,99},{4,28},{5,101},{6,30},{7,103},{8,0},{9... | collective-permute-start | bytes 811016 | tf_op jit(solution)/shard_map/ppermute | solution.py:39
  137.3 8.7 %collective-permute-start.39 = (f32[4,264,128]{2,1,0:T(8,128)S(1)}, f32[4,264,128]{2,1,0:T(8,128)S(1)}, u32[]{:S(2)}, u32[]{:S(2)}) collective-permute-start(f32[4,264,128]{2,1,0:T(8,128)S(1)} %get-tuple-element.39), channel_id=1, source_target_pairs={{0,1},{1,0},{2,3},{3,2},{4,5},{5,4},{6,7},{7,6},{8,9},{9,8},{10,11... | collective-permute-start | bytes 1622024 | tf_op jit(solution)/shard_map/ppermute | solution.py:65
  146.1 6.4 %collective-permute-start.42 = (f32[264,128]{1,0:T(8,128)S(1)}, f32[264,128]{1,0:T(8,128)S(1)}, u32[]{:S(2)}, u32[]{:S(2)}) collective-permute-start(f32[264,128]{1,0:T(8,128)S(1)} %get-tuple-element.50), channel_id=1, source_target_pairs={{0,4},{2,6},{4,0},{6,2},{1,5},{3,7},{5,1},{7,3},{8,12},{10,14},{12... | collective-permute-start | bytes 405512 | tf_op jit(solution)/shard_map/ppermute | solution.py:69
  146.2 6.3 %collective-permute-start.41 = (f32[264,128]{1,0:T(8,128)S(1)}, f32[264,128]{1,0:T(8,128)S(1)}, u32[]{:S(2)}, u32[]{:S(2)}) collective-permute-start(f32[264,128]{1,0:T(8,128)S(1)} %get-tuple-element.51), channel_id=1, source_target_pairs={{0,6},{2,0},{4,2},{6,4},{1,7},{3,1},{5,3},{7,5},{8,14},{10,8},{12,... | collective-permute-start | bytes 405512 | tf_op jit(solution)/shard_map/ppermute | solution.py:69
  146.2 9.8 %collective-permute-start.40 = (f32[264,128]{1,0:T(8,128)S(1)}, f32[264,128]{1,0:T(8,128)S(1)}, u32[]{:S(2)}, u32[]{:S(2)}) collective-permute-start(f32[264,128]{1,0:T(8,128)S(1)} %get-tuple-element.52), channel_id=1, source_target_pairs={{0,2},{2,4},{4,6},{6,0},{1,3},{3,5},{5,7},{7,1},{8,10},{10,12},{12... | collective-permute-start | bytes 405512 | tf_op jit(solution)/shard_map/ppermute | solution.py:69
